TPU v7x, 32 devices: a whole 2x2x4 slice. The times are simulated.
32 devices in a mesh: wide: 16 (over z, y, core), narrow: 2 (over x).
Axes of the slice: x: 2, y: 2, z: 4, core: 2. Of those that a mesh axis runs over, the one named last changes fastest.
Arguments:
- tokens: bfloat16 [32768, 768], P(('wide', 'narrow')), may hold values from -6 to 6
- kept_patches: int32 [256, 128], P(('wide', 'narrow')), may hold values from 0 to 511, as said below
- resolution: int32 [256], P(('wide', 'narrow')), may hold values from 0 to 1, as said below
- position_table: bfloat16 [640, 768], replicated, may hold values from -4 to 4
- norm_one_gain: bfloat16 [768], replicated, may hold values from 0.25 to 1.75
- norm_one_shift: bfloat16 [768], replicated, may hold values from -3 to 3
- project_weight: bfloat16 [768, 2304], replicated, may hold values from -0.21875 to 0.21875
- query_bias: bfloat16 [768], replicated, may hold values from -3 to 3
- value_bias: bfloat16 [768], replicated, may hold values from -3 to 3
- output_weight: bfloat16 [768, 768], replicated, may hold values from -0.875 to 0.875
- output_bias: bfloat16 [768], replicated, may hold values from -3 to 3
- norm_two_gain: bfloat16 [768], replicated, may hold values from 0.25 to 1.75
- norm_two_shift: bfloat16 [768], replicated, may hold values from -3 to 3
- expand_weight: bfloat16 [768, 3072], replicated, may hold values from -0.21875 to 0.21875
- expand_bias: bfloat16 [3072], replicated, may hold values from -3 to 3
- reduce_weight: bfloat16 [3072, 768], replicated, may hold values from -0.109375 to 0.109375
- reduce_bias: bfloat16 [768], replicated, may hold values from -3 to 3
- cotangent: bfloat16 [32768, 768], P(('wide', 'narrow')), may hold values from -6 to 6
Outputs:
- layer_output: bfloat16 [32768, 768], P(('wide', 'narrow'))
- token_gradient: bfloat16 [32768, 768], P(('wide', 'narrow'))
- position_gradient: float32 [640, 768], replicated
- norm_one_gain_gradient: float32 [768], replicated
- norm_one_shift_gradient: float32 [768], replicated
- project_weight_gradient: float32 [768, 2304], replicated
- query_bias_gradient: float32 [768], replicated
- value_bias_gradient: float32 [768], replicated
- output_weight_gradient: float32 [768, 768], replicated
- output_bias_gradient: float32 [768], replicated
- norm_two_gain_gradient: float32 [768], replicated
- norm_two_shift_gradient: float32 [768], replicated
- expand_weight_gradient: float32 [768, 3072], replicated
- expand_bias_gradient: float32 [3072], replicated
- reduce_weight_gradient: float32 [3072, 768], replicated
- reduce_bias_gradient: float32 [768], replicated
Inputs may be any that keep to these rules, and one draw needn't show every extreme that they name: `kept_patches`: in a group with resolution 1 the entries are 128 distinct patches of one fine sample. In a group with resolution 0 the group holds 4 coarse samples: for each s the rows with entry // 128 = s are 32 distinct patches of that sample. `resolution`: the same on all 8 groups of one device.
All inputs are finite; a program needn't handle non-finite values.
Results may differ from a plain program's by a relative error of at most 0.012.
Values sent between devices are 32-bit elements; how exact they have to be, the bound alone decides.
No kernel may reach another device: no remote copies, remote signals or barrier semaphores. Data moves between devices by JAX's collectives and lax.ppermute only.
A program may use at most 192 MiB of HBM per device.

v0:
```python
from functools import partial

import jax
import jax.numpy as jnp
from jax import lax
from jax.sharding import PartitionSpec as P

HEADS = 12
PATCH_LO = 128


epsilon = 1e-06
big_negative = -1e30


def norm_forward(stream, norm_gain, norm_shift):
    centre = stream - jnp.mean(stream, axis=-1, keepdims=True)
    inverse = lax.rsqrt(jnp.mean(centre * centre, axis=-1, keepdims=True) + epsilon)
    normed = centre * inverse
    return (normed, inverse, normed * norm_gain + norm_shift)


def norm_backward(upstream, normed, inverse, norm_gain):
    scaled = upstream * norm_gain
    inner = jnp.mean(scaled * normed, axis=-1, keepdims=True)
    stream_gradient = inverse * (scaled - jnp.mean(scaled, axis=-1, keepdims=True) - normed * inner)
    return (stream_gradient, jnp.sum(upstream * normed, axis=0), jnp.sum(upstream, axis=0))


def body(
    tokens,
    kept_patches,
    resolution,
    position_table,
    norm_one_gain,
    norm_one_shift,
    project_weight,
    query_bias,
    value_bias,
    output_weight,
    output_bias,
    norm_two_gain,
    norm_two_shift,
    expand_weight,
    expand_bias,
    reduce_weight,
    reduce_bias,
    cotangent,
):
    f32 = jnp.float32
    bf16 = jnp.bfloat16
    group_count, group_rows = kept_patches.shape
    model_width = tokens.shape[1]
    head_width = model_width // HEADS
    score_scale = head_width ** (-0.5)
    fine_grid = resolution[:, None] == 1
    place_index = jnp.where(fine_grid, PATCH_LO + kept_patches, kept_patches % PATCH_LO).reshape(-1)
    sample_index = jnp.where(fine_grid, 0, kept_patches // PATCH_LO)
    same_sample = (sample_index[:, :, None] == sample_index[:, None, :])[:, None]

    def split_heads(columns):
        return columns.reshape(group_count, group_rows, HEADS, head_width)

    stream_in = tokens.astype(f32) + jnp.take(position_table, place_index, axis=0).astype(f32)
    one_gain = norm_one_gain.astype(f32)
    normed_one, inverse_one, affine_one = norm_forward(
        stream_in, one_gain, norm_one_shift.astype(f32)
    )
    first_low = affine_one.astype(bf16)
    joined_bias = jnp.concatenate([query_bias, jnp.zeros_like(query_bias), value_bias]).astype(f32)
    projected = (
        jnp.dot(first_low, project_weight, preferred_element_type=f32) + joined_bias
    ).astype(bf16)
    queries = split_heads(projected[:, :model_width])
    keys_all = split_heads(projected[:, model_width : 2 * model_width])
    values = split_heads(projected[:, 2 * model_width :])

    def masked_scores():
        raw_scores = (
            jnp.einsum("gqhd,gkhd->ghqk", queries, keys_all, preferred_element_type=f32)
            * score_scale
        )
        return jnp.where(same_sample, raw_scores, big_negative)

    scores = masked_scores()
    top_score = jnp.max(scores, axis=-1, keepdims=True)
    exponent = jnp.exp(scores - top_score)
    total = jnp.sum(exponent, axis=-1, keepdims=True)
    softmax_weights = exponent / total
    log_total = top_score + jnp.log(total)
    heads_out = (
        jnp.einsum(
            "ghqk,gkhd->gqhd", softmax_weights.astype(bf16), values, preferred_element_type=f32
        )
        .reshape(-1, model_width)
        .astype(bf16)
    )
    stream_mid = stream_in + (
        jnp.dot(heads_out, output_weight, preferred_element_type=f32) + output_bias.astype(f32)
    )
    two_gain = norm_two_gain.astype(f32)
    normed_two, inverse_two, affine_two = norm_forward(
        stream_mid, two_gain, norm_two_shift.astype(f32)
    )
    second_low = affine_two.astype(bf16)
    hidden_pre = jnp.dot(
        second_low, expand_weight, preferred_element_type=f32
    ) + expand_bias.astype(f32)
    hidden, gelu_back = jax.vjp(partial(jax.nn.gelu, approximate=False), hidden_pre)
    hidden_low = hidden.astype(bf16)
    layer_output = (
        stream_mid
        + (jnp.dot(hidden_low, reduce_weight, preferred_element_type=f32) + reduce_bias.astype(f32))
    ).astype(bf16)
    out_gradient = cotangent.astype(f32)
    reduce_weight_gradient = jnp.einsum(
        "rf,rd->fd", hidden_low, cotangent, preferred_element_type=f32
    )
    reduce_bias_gradient = jnp.sum(out_gradient, axis=0)
    hidden_gradient = jnp.einsum("rd,fd->rf", cotangent, reduce_weight, preferred_element_type=f32)
    pre_gradient = gelu_back(hidden_gradient)[0].astype(bf16)
    expand_bias_gradient = jnp.sum(pre_gradient.astype(f32), axis=0)
    expand_weight_gradient = jnp.einsum(
        "rd,rf->df", second_low, pre_gradient, preferred_element_type=f32
    )
    second_gradient = jnp.einsum(
        "rf,df->rd", pre_gradient, expand_weight, preferred_element_type=f32
    )
    mid_from_norm, norm_two_gain_gradient, norm_two_shift_gradient = norm_backward(
        second_gradient, normed_two, inverse_two, two_gain
    )
    mid_gradient = out_gradient + mid_from_norm
    branch_gradient = mid_gradient.astype(bf16)
    output_bias_gradient = jnp.sum(branch_gradient.astype(f32), axis=0)
    output_weight_gradient = jnp.einsum(
        "re,rd->ed", heads_out, branch_gradient, preferred_element_type=f32
    )
    heads_gradient = split_heads(
        jnp.einsum("rd,ed->re", branch_gradient, output_weight, preferred_element_type=f32).astype(
            bf16
        )
    )
    again_weights = jnp.exp(masked_scores() - log_total)
    weight_gradient = jnp.einsum(
        "gqhd,gkhd->ghqk", heads_gradient, values, preferred_element_type=f32
    )
    value_gradient = jnp.einsum(
        "ghqk,gqhd->gkhd", again_weights.astype(bf16), heads_gradient, preferred_element_type=f32
    )
    row_inner = jnp.sum(weight_gradient * again_weights, axis=-1, keepdims=True)
    score_gradient = (again_weights * (weight_gradient - row_inner)).astype(bf16)
    query_gradient = (
        jnp.einsum("ghqk,gkhd->gqhd", score_gradient, keys_all, preferred_element_type=f32)
        * score_scale
    )
    key_gradient = (
        jnp.einsum("ghqk,gqhd->gkhd", score_gradient, queries, preferred_element_type=f32)
        * score_scale
    )
    projected_gradient = jnp.concatenate(
        [
            query_gradient.reshape(-1, model_width),
            key_gradient.reshape(-1, model_width),
            value_gradient.reshape(-1, model_width),
        ],
        axis=1,
    ).astype(bf16)
    query_bias_gradient = jnp.sum(projected_gradient[:, :model_width].astype(f32), axis=0)
    value_bias_gradient = jnp.sum(projected_gradient[:, 2 * model_width :].astype(f32), axis=0)
    project_weight_gradient = jnp.einsum(
        "rd,re->de", first_low, projected_gradient, preferred_element_type=f32
    )
    first_gradient = jnp.einsum(
        "re,de->rd", projected_gradient, project_weight, preferred_element_type=f32
    )
    in_from_norm, norm_one_gain_gradient, norm_one_shift_gradient = norm_backward(
        first_gradient, normed_one, inverse_one, one_gain
    )
    in_gradient = mid_gradient + in_from_norm
    token_gradient = in_gradient.astype(bf16)
    position_gradient = jax.ops.segment_sum(
        in_gradient, place_index, num_segments=position_table.shape[0]
    )
    (
        position_gradient,
        norm_one_gain_gradient,
        norm_one_shift_gradient,
        project_weight_gradient,
        query_bias_gradient,
        value_bias_gradient,
        output_weight_gradient,
        output_bias_gradient,
        norm_two_gain_gradient,
        norm_two_shift_gradient,
        expand_weight_gradient,
        expand_bias_gradient,
        reduce_weight_gradient,
        reduce_bias_gradient,
    ) = (
        lax.psum_scatter(position_gradient, "narrow", scatter_dimension=0, tiled=True),
        lax.psum_scatter(norm_one_gain_gradient, "narrow", scatter_dimension=0, tiled=True),
        lax.psum_scatter(norm_one_shift_gradient, "narrow", scatter_dimension=0, tiled=True),
        lax.psum_scatter(project_weight_gradient, "narrow", scatter_dimension=0, tiled=True),
        lax.psum_scatter(query_bias_gradient, "narrow", scatter_dimension=0, tiled=True),
        lax.psum_scatter(value_bias_gradient, "narrow", scatter_dimension=0, tiled=True),
        lax.psum_scatter(output_weight_gradient, "narrow", scatter_dimension=0, tiled=True),
        lax.psum_scatter(output_bias_gradient, "narrow", scatter_dimension=0, tiled=True),
        lax.psum_scatter(norm_two_gain_gradient, "narrow", scatter_dimension=0, tiled=True),
        lax.psum_scatter(norm_two_shift_gradient, "narrow", scatter_dimension=0, tiled=True),
        lax.psum_scatter(expand_weight_gradient, "narrow", scatter_dimension=0, tiled=True),
        lax.psum_scatter(expand_bias_gradient, "narrow", scatter_dimension=0, tiled=True),
        lax.psum_scatter(reduce_weight_gradient, "narrow", scatter_dimension=0, tiled=True),
        lax.psum_scatter(reduce_bias_gradient, "narrow", scatter_dimension=0, tiled=True),
    )
    (
        position_gradient,
        norm_one_gain_gradient,
        norm_one_shift_gradient,
        project_weight_gradient,
        query_bias_gradient,
        value_bias_gradient,
        output_weight_gradient,
        output_bias_gradient,
        norm_two_gain_gradient,
        norm_two_shift_gradient,
        expand_weight_gradient,
        expand_bias_gradient,
        reduce_weight_gradient,
        reduce_bias_gradient,
    ) = lax.psum(
        (
            position_gradient,
            norm_one_gain_gradient,
            norm_one_shift_gradient,
            project_weight_gradient,
            query_bias_gradient,
            value_bias_gradient,
            output_weight_gradient,
            output_bias_gradient,
            norm_two_gain_gradient,
            norm_two_shift_gradient,
            expand_weight_gradient,
            expand_bias_gradient,
            reduce_weight_gradient,
            reduce_bias_gradient,
        ),
        "wide",
    )
    (
        position_gradient,
        norm_one_gain_gradient,
        norm_one_shift_gradient,
        project_weight_gradient,
        query_bias_gradient,
        value_bias_gradient,
        output_weight_gradient,
        output_bias_gradient,
        norm_two_gain_gradient,
        norm_two_shift_gradient,
        expand_weight_gradient,
        expand_bias_gradient,
        reduce_weight_gradient,
        reduce_bias_gradient,
    ) = (
        lax.all_gather(position_gradient, "narrow", axis=0, tiled=True),
        lax.all_gather(norm_one_gain_gradient, "narrow", axis=0, tiled=True),
        lax.all_gather(norm_one_shift_gradient, "narrow", axis=0, tiled=True),
        lax.all_gather(project_weight_gradient, "narrow", axis=0, tiled=True),
        lax.all_gather(query_bias_gradient, "narrow", axis=0, tiled=True),
        lax.all_gather(value_bias_gradient, "narrow", axis=0, tiled=True),
        lax.all_gather(output_weight_gradient, "narrow", axis=0, tiled=True),
        lax.all_gather(output_bias_gradient, "narrow", axis=0, tiled=True),
        lax.all_gather(norm_two_gain_gradient, "narrow", axis=0, tiled=True),
        lax.all_gather(norm_two_shift_gradient, "narrow", axis=0, tiled=True),
        lax.all_gather(expand_weight_gradient, "narrow", axis=0, tiled=True),
        lax.all_gather(expand_bias_gradient, "narrow", axis=0, tiled=True),
        lax.all_gather(reduce_weight_gradient, "narrow", axis=0, tiled=True),
        lax.all_gather(reduce_bias_gradient, "narrow", axis=0, tiled=True),
    )
    return (
        layer_output,
        token_gradient,
        position_gradient,
        norm_one_gain_gradient,
        norm_one_shift_gradient,
        project_weight_gradient,
        query_bias_gradient,
        value_bias_gradient,
        output_weight_gradient,
        output_bias_gradient,
        norm_two_gain_gradient,
        norm_two_shift_gradient,
        expand_weight_gradient,
        expand_bias_gradient,
        reduce_weight_gradient,
        reduce_bias_gradient,
    )


def solution(mesh):
    placed = (
        P(("wide", "narrow"), None),
        P(("wide", "narrow"), None),
        P(("wide", "narrow")),
        P(),
        P(),
        P(),
        P(),
        P(),
        P(),
        P(),
        P(),
        P(),
        P(),
        P(),
        P(),
        P(),
        P(),
        P(("wide", "narrow"), None),
    )
    return jax.shard_map(
        body,
        mesh=mesh,
        in_specs=placed,
        out_specs=(
            P(("wide", "narrow"), None),
            P(("wide", "narrow"), None),
            P(),
            P(),
            P(),
            P(),
            P(),
            P(),
            P(),
            P(),
            P(),
            P(),
            P(),
            P(),
            P(),
            P(),
        ),
        check_vma=False,
    )
```

profile of v0, /device:TPU:0, one launch (start us, length us, event | category | flops | bytes accessed | tf_op | source)
XLA Modules:
  0.0 1307.6 jit_solution(10302080798258088202)
XLA Ops:
  9.8 6.9 gather_fusion
  65.6 38.0 %multiply_convert_fusion = (bf16[1024,3072]{1,0:T(8,128)(2,1)}, f32[1024,3072]{1,0:T(8,128)}, f32[1024,3072]{1,0:T(8,128)}) fusion(f32[3072]{0:T(1024)} %convert_element_type.110, bf16[768,3072]{1,0:T(8,128)(2,1)} %param.31, f32[1024,768]{0,1:T(8,128)} %copy-done.9, f32[768]{0:T(1024)S(1)} %convert_element_type.108, f32[768]{0:T(1024)S(1)} %convert_element_type.107, ...), kind=kOutput, calls=%fused_computation.6 | convolution fusion | flops 5043388416 | bytes 39348224 | tf_op jit(solution)/shard_map/dot_general | solution.py:106
  103.6 17.3 %convert_reduce_fusion = (f32[3072]{0:T(1024)}, bf16[1024,3072]{1,0:T(8,128)(2,1)}) fusion(f32[1024,3072]{1,0:T(8,128)} %get-tuple-element.98, bf16[1024,768]{1,0:T(8,128)(2,1)S(1)} %copy-done.22, bf16[3072,768]{1,0:T(8,128)(2,1)} %param.33, f32[1024,3072]{1,0:T(8,128)} %get-tuple-element.109, f32[3072]{0:T(1024)S(1)} %copy-done.38), kind=kOutput, calls=%fused_computation.4 | convolution fusion | flops 4885312512 | bytes 37773312 | tf_op jit(solution)/shard_map/rd,fd->rf/dot_general | solution.py:120
  121.0 10.5 fusion.55
  152.7 5.2 fusion.23
  158.0 7.3 multiply_reduce_fusion
  178.7 6.2 fusion.54
  193.5 5.6 fusion.48
  202.7 9.3 scatter_custom_fusion
  217.6 10.7 fusion.47
  229.0 10.5 fusion.45
  239.6 10.0 fusion.56
  249.7 33.4 %reduce-scatter.10.cloned.1.call-done = f32[384,768]{1,0:T(8,128)} async-done(((f32[768,768]{1,0:T(8,128)}), f32[384,768]{1,0:T(8,128)}) %reduce-scatter.10.cloned.1.call-update) | async-done | bytes 1179664 | tf_op jit(solution)/shard_map/reduce_scatter | solution.py:206
  283.1 88.6 %reduce-scatter.8.cloned.1.call-done = f32[384,2304]{1,0:T(8,128)} async-done(((f32[768,2304]{1,0:T(8,128)}), f32[384,2304]{1,0:T(8,128)}) %reduce-scatter.8.cloned.1.call-update) | async-done | bytes 3538960 | tf_op jit(solution)/shard_map/reduce_scatter | solution.py:203
  371.7 113.4 %reduce-scatter.12.cloned.1.call-done = f32[384,3072]{1,0:T(8,128)} async-done(((f32[768,3072]{1,0:T(8,128)}), f32[384,3072]{1,0:T(8,128)}) %reduce-scatter.12.cloned.1.call-update) | async-done | bytes 4718608 | tf_op jit(solution)/shard_map/reduce_scatter | solution.py:210
  485.1 113.4 %reduce-scatter.14.cloned.1.call-done = f32[1536,768]{1,0:T(8,128)} async-done(((f32[3072,768]{1,0:T(8,128)}), f32[1536,768]{1,0:T(8,128)}) %reduce-scatter.14.cloned.1.call-update) | async-done | bytes 4718608 | tf_op jit(solution)/shard_map/reduce_scatter | solution.py:212
  598.5 276.5 %all-reduce.14.cloned.1.call-done = (f32[320,768]{1,0:T(8,128)}, f32[384,2304]{1,0:T(8,128)}, f32[384,768]{1,0:T(8,128)}, f32[384,3072]{1,0:T(8,128)}, f32[1536,768]{1,0:T(8,128)}) async-done(((f32[320,768]{1,0:T(8,128)}, f32[384,2304]{1,0:T(8,128)}, f32[384,768]{1,0:T(8,128)}, f32[384,3072]{1,0:T(8,128)}, f32[1536,768]{1,0:T(8,128)}), (f32[320,768]{1,0:T(8,128)}, f32[384,2304]{1,0:T(8,128)}, ...) | async-done | bytes 15138832 | tf_op jit(solution)/shard_map/psum | solution.py:230
  883.6 11.1 all-reduce.11
  906.2 58.4 %all-reduce.9 = (f32[384]{0:T(512)}, f32[384]{0:T(512)}, f32[384]{0:T(512)}, f32[384]{0:T(512)}, f32[384]{0:T(512)}, /*index=5*/f32[384]{0:T(512)}, f32[384]{0:T(512)}, f32[1536]{0:T(1024)S(1)}, f32[384]{0:T(512)}) all-reduce(f32[384]{0:T(512)} %dynamic-slice.1, ...), channel_id=1, replica_groups=mesh['wide'=16,'narrow'=2] {'wide'}, use_global_device_ids=true, to_apply=%region_16.17 | all-reduce | flops 4608 | bytes 36864 | tf_op jit(solution)/shard_map/psum | solution.py:230
  1024.8 10.0 add_convert_fusion.2
  1038.2 119.4 %all-gather.21.cloned.1.call-done = f32[768,3072]{1,0:T(8,128)} async-done(((f32[384,3072]{1,0:T(8,128)}), f32[768,3072]{1,0:T(8,128)}) %all-gather.21.cloned.1.call-update) | async-done | bytes 9437200 | tf_op jit(solution)/shard_map/all_gather | solution.py:275
  1157.6 119.6 %all-gather.23.cloned.1.call-done = f32[3072,768]{1,0:T(8,128)} async-done(((f32[1536,768]{1,0:T(8,128)}), f32[3072,768]{1,0:T(8,128)}) %all-gather.23.cloned.1.call-update) | async-done | bytes 9437200 | tf_op jit(solution)/shard_map/all_gather | solution.py:277
  1280.3 6.8 copy.184
  1292.8 8.0 copy.188
  (259 shorter events, 195.4 us)
Async XLA Ops:
  7.2 18.4 %copy-start = (bf16[768,2304]{1,0:T(8,128)(2,1)S(1)}, bf16[768,2304]{1,0:T(8,128)(2,1)}, u32[]{:S(2)}) copy-start(bf16[768,2304]{1,0:T(8,128)(2,1)} %param.24) | copy-start | bytes 10616836
  7.2 242.5 %reduce-scatter.6.cloned.1.call-start = ((), (), s32[]{:S(2)}) async-start(), calls=%async_computation.5 | async-start | bytes 2949120 | tf_op jit(solution)/shard_map/reduce_scatter | solution.py:200
  9.0 48.8 %copy-start.32 = (pred[1024]{0:T(1024)(128)(4,1)}, pred[1024]{0:T(1024)(128)(4,1)S(1)}, u32[]{:S(2)}) copy-start(pred[1024]{0:T(1024)(128)(4,1)S(1)} %get-tuple-element.99) | copy-start | bytes 3076
  63.0 40.6 %copy-start.41 = (f32[768]{0:T(1024)}, f32[768]{0:T(1024)S(1)}, u32[]{:S(2)}) copy-start(f32[768]{0:T(1024)S(1)} %convert_element_type.108) | copy-start | bytes 9220
  65.6 38.0 %copy-start.22 = (bf16[1024,768]{1,0:T(8,128)(2,1)S(1)}, bf16[1024,768]{1,0:T(8,128)(2,1)}, u32[]{:S(2)}) copy-start(bf16[1024,768]{1,0:T(8,128)(2,1)} %param.35) | copy-start | bytes 4718596
  65.6 38.0 %copy-start.38 = (f32[3072]{0:T(1024)S(1)}, f32[3072]{0:T(1024)}, u32[]{:S(2)}) copy-start(f32[3072]{0:T(1024)} %convert_element_type.110) | copy-start | bytes 36868
  152.7 12.6 slice-start
  157.9 7.4 slice-start.1
  212.1 71.0 %reduce-scatter.10.cloned.1.call-start = ((), (), s32[]{:S(2)}) async-start(), calls=%async_computation.9 | async-start | bytes 3538944 | tf_op jit(solution)/shard_map/reduce_scatter | solution.py:206
  217.6 154.1 %reduce-scatter.8.cloned.1.call-start = ((), (), s32[]{:S(2)}) async-start(), calls=%async_computation.7 | async-start | bytes 10616832 | tf_op jit(solution)/shard_map/reduce_scatter | solution.py:203
  228.4 256.7 %reduce-scatter.12.cloned.1.call-start = ((), (), s32[]{:S(2)}) async-start(), calls=%async_computation.11 | async-start | bytes 14155776 | tf_op jit(solution)/shard_map/reduce_scatter | solution.py:210
  239.6 358.9 %reduce-scatter.14.cloned.1.call-start = ((), (), s32[]{:S(2)}) async-start(), calls=%async_computation.13 | async-start | bytes 14155776 | tf_op jit(solution)/shard_map/reduce_scatter | solution.py:212
  249.7 625.4 %all-reduce.14.cloned.1.call-start = ((), (), s32[]{:S(2)}) async-start(), calls=%async_computation.15 | async-start | bytes 30277632 | tf_op jit(solution)/shard_map/psum | solution.py:230
  598.5 438.8 %all-gather.15.cloned.1.call-start = ((), (), s32[]{:S(2)}) async-start(), calls=%async_computation.6 | async-start | bytes 2949120 | tf_op jit(solution)/shard_map/all_gather | solution.py:265
  875.0 162.3 %all-gather.19.cloned.1.call-start = ((), (), s32[]{:S(2)}) async-start(), calls=%async_computation.10 | async-start | bytes 3538944 | tf_op jit(solution)/shard_map/all_gather | solution.py:271
  875.8 162.4 %all-gather.17.cloned.1.call-start = ((), (), s32[]{:S(2)}) async-start(), calls=%async_computation.8 | async-start | bytes 10616832 | tf_op jit(solution)/shard_map/all_gather | solution.py:268
  876.5 281.1 %all-gather.21.cloned.1.call-start = ((), (), s32[]{:S(2)}) async-start(), calls=%async_computation.12 | async-start | bytes 14155776 | tf_op jit(solution)/shard_map/all_gather | solution.py:275
  877.1 400.1 %all-gather.23.cloned.1.call-start = ((), (), s32[]{:S(2)}) async-start(), calls=%async_computation.14 | async-start | bytes 14155776 | tf_op jit(solution)/shard_map/all_gather | solution.py:277
  877.2 6.5 copy-start.34
  877.2 6.5 copy-start.35
  1277.2 11.3 slice-start.2
  1280.3 6.8 copy-start.21
  1280.3 8.2 slice-start.3
  1280.3 8.2 slice-start.4
  (46 other events, 158.4 us)
Sparse Core Ops, SparseCore 0:
  212.2 33.1 reduce-scatter.5
  248.2 34.7 reduce-scatter.9
  286.0 85.6 reduce-scatter.7
  374.4 110.6 reduce-scatter.11
  487.8 110.6 reduce-scatter.13
  603.4 271.6 all-reduce.13
  876.6 32.7 all-gather.14
  910.9 36.0 all-gather.18
  948.5 89.5 all-gather.16
  1039.6 117.9 all-gather.20
  1159.2 117.9 all-gather.22
where the time goes:
time: 1310 us
  waiting for transfers between devices  868 us (66%)
  matrix products  147 us (11%)
  local copies, waits for them, and re-layouts  112 us (9%)
  blocking collectives  111 us (8%)
  other arithmetic  53.2 us (4%)
  between operations  16.2 us (1%)
    psum x1, waiting for transfers between devices, body(): lax.psum((position_gradient, norm_one_gain_gradient, norm_one_shift_gradi...  276 us
    all_gather x1, waiting for transfers between devices, body(): lax.all_gather(reduce_weight_gradient, 'narrow', axis=0, tiled=True)  120 us
    all_gather x1, waiting for transfers between devices, body(): lax.all_gather(expand_weight_gradient, 'narrow', axis=0, tiled=True)  119 us
    reduce_scatter x1, waiting for transfers between devices, body(): lax.psum_scatter(expand_weight_gradient, 'narrow', scatter_dimension=0, t...  113 us
    reduce_scatter x1, waiting for transfers between devices, body(): lax.psum_scatter(reduce_weight_gradient, 'narrow', scatter_dimension=0, t...  113 us
    reduce_scatter x1, waiting for transfers between devices, body(): lax.psum_scatter(project_weight_gradient, 'narrow', scatter_dimension=0,...  88.6 us
    unnamed x161, local copies, waits for them, and re-layouts  72.5 us
    psum x1, blocking collectives, body(): lax.psum((position_gradient, norm_one_gain_gradient, norm_one_shift_gradi...  58.4 us
  transfers between devices with their start and end apart: 11, of which 8 were waited for; matrix products, arithmetic and copies ran while one was open for 6% of the time, Pallas kernels for 0%

commit v1 on v0

--- a/solution.py
+++ b/solution.py
@@ -181,102 +181,51 @@
     position_gradient = jax.ops.segment_sum(
         in_gradient, place_index, num_segments=position_table.shape[0]
     )
+    every = ("wide", "narrow")
+    small = jnp.concatenate(
+        [
+            norm_one_gain_gradient,
+            norm_one_shift_gradient,
+            query_bias_gradient,
+            value_bias_gradient,
+            output_bias_gradient,
+            norm_two_gain_gradient,
+            norm_two_shift_gradient,
+            reduce_bias_gradient,
+            expand_bias_gradient,
+            jnp.zeros((4 * model_width,), f32),
+        ]
+    ).reshape(-1, model_width)
+    places = position_table.shape[0]
+    reduce_weight_gradient = lax.psum(reduce_weight_gradient, every)
+    expand_weight_gradient, reduce_weight_gradient = lax.optimization_barrier(
+        (expand_weight_gradient, reduce_weight_gradient)
+    )
+    expand_weight_gradient = lax.psum(expand_weight_gradient, every)
+    project_weight_gradient, expand_weight_gradient = lax.optimization_barrier(
+        (project_weight_gradient, expand_weight_gradient)
+    )
+    project_weight_gradient = lax.psum(project_weight_gradient, every)
+    mixed, project_weight_gradient = lax.optimization_barrier(
+        (
+            jnp.concatenate([position_gradient, small, output_weight_gradient]),
+            project_weight_gradient,
+        )
+    )
+    mixed = lax.psum(mixed, every)
+    position_gradient = mixed[:places]
     (
-        position_gradient,
         norm_one_gain_gradient,
         norm_one_shift_gradient,
-        project_weight_gradient,
         query_bias_gradient,
         value_bias_gradient,
-        output_weight_gradient,
         output_bias_gradient,
         norm_two_gain_gradient,
         norm_two_shift_gradient,
-        expand_weight_gradient,
-        expand_bias_gradient,
-        reduce_weight_gradient,
         reduce_bias_gradient,
-    ) = (
-        lax.psum_scatter(position_gradient, "narrow", scatter_dimension=0, tiled=True),
-        lax.psum_scatter(norm_one_gain_gradient, "narrow", scatter_dimension=0, tiled=True),
-        lax.psum_scatter(norm_one_shift_gradient, "narrow", scatter_dimension=0, tiled=True),
-        lax.psum_scatter(project_weight_gradient, "narrow", scatter_dimension=0, tiled=True),
-        lax.psum_scatter(query_bias_gradient, "narrow", scatter_dimension=0, tiled=True),
-        lax.psum_scatter(value_bias_gradient, "narrow", scatter_dimension=0, tiled=True),
-        lax.psum_scatter(output_weight_gradient, "narrow", scatter_dimension=0, tiled=True),
-        lax.psum_scatter(output_bias_gradient, "narrow", scatter_dimension=0, tiled=True),
-        lax.psum_scatter(norm_two_gain_gradient, "narrow", scatter_dimension=0, tiled=True),
-        lax.psum_scatter(norm_two_shift_gradient, "narrow", scatter_dimension=0, tiled=True),
-        lax.psum_scatter(expand_weight_gradient, "narrow", scatter_dimension=0, tiled=True),
-        lax.psum_scatter(expand_bias_gradient, "narrow", scatter_dimension=0, tiled=True),
-        lax.psum_scatter(reduce_weight_gradient, "narrow", scatter_dimension=0, tiled=True),
-        lax.psum_scatter(reduce_bias_gradient, "narrow", scatter_dimension=0, tiled=True),
-    )
-    (
-        position_gradient,
-        norm_one_gain_gradient,
-        norm_one_shift_gradient,
-        project_weight_gradient,
-        query_bias_gradient,
-        value_bias_gradient,
-        output_weight_gradient,
-        output_bias_gradient,
-        norm_two_gain_gradient,
-        norm_two_shift_gradient,
-        expand_weight_gradient,
-        expand_bias_gradient,
-        reduce_weight_gradient,
-        reduce_bias_gradient,
-    ) = lax.psum(
-        (
-            position_gradient,
-            norm_one_gain_gradient,
-            norm_one_shift_gradient,
-            project_weight_gradient,
-            query_bias_gradient,
-            value_bias_gradient,
-            output_weight_gradient,
-            output_bias_gradient,
-            norm_two_gain_gradient,
-            norm_two_shift_gradient,
-            expand_weight_gradient,
-            expand_bias_gradient,
-            reduce_weight_gradient,
-            reduce_bias_gradient,
-        ),
-        "wide",
-    )
-    (
-        position_gradient,
-        norm_one_gain_gradient,
-        norm_one_shift_gradient,
-        project_weight_gradient,
-        query_bias_gradient,
-        value_bias_gradient,
-        output_weight_gradient,
-        output_bias_gradient,
-        norm_two_gain_gradient,
-        norm_two_shift_gradient,
-        expand_weight_gradient,
-        expand_bias_gradient,
-        reduce_weight_gradient,
-        reduce_bias_gradient,
-    ) = (
-        lax.all_gather(position_gradient, "narrow", axis=0, tiled=True),
-        lax.all_gather(norm_one_gain_gradient, "narrow", axis=0, tiled=True),
-        lax.all_gather(norm_one_shift_gradient, "narrow", axis=0, tiled=True),
-        lax.all_gather(project_weight_gradient, "narrow", axis=0, tiled=True),
-        lax.all_gather(query_bias_gradient, "narrow", axis=0, tiled=True),
-        lax.all_gather(value_bias_gradient, "narrow", axis=0, tiled=True),
-        lax.all_gather(output_weight_gradient, "narrow", axis=0, tiled=True),
-        lax.all_gather(output_bias_gradient, "narrow", axis=0, tiled=True),
-        lax.all_gather(norm_two_gain_gradient, "narrow", axis=0, tiled=True),
-        lax.all_gather(norm_two_shift_gradient, "narrow", axis=0, tiled=True),
-        lax.all_gather(expand_weight_gradient, "narrow", axis=0, tiled=True),
-        lax.all_gather(expand_bias_gradient, "narrow", axis=0, tiled=True),
-        lax.all_gather(reduce_weight_gradient, "narrow", axis=0, tiled=True),
-        lax.all_gather(reduce_bias_gradient, "narrow", axis=0, tiled=True),
-    )
+    ) = (mixed[places + k] for k in range(8))
+    expand_bias_gradient = mixed[places + 8 : places + 12].reshape(-1)
+    output_weight_gradient = mixed[places + 16 :]
     return (
         layer_output,
         token_gradient,

time: 1310 us -> 874 us (0.67)
  waiting for transfers between devices: 868 us -> 538 us
  blocking collectives: 111 us -> 0 us
    reduce_scatter x5 -> x0, waiting for transfers between devices: 349 us -> none  [the longest x1 113 us: body(): lax.psum_scatter(expand_weight_gradient, 'narrow', scatter_dimension=0, t...]
    psum x1 -> x4, waiting for transfers between devices: 276 us -> 538 us  [the longest x1 157 us: body(): expand_weight_gradient = lax.psum(expand_weight_gradient, every)]
    all_gather x5 -> x0, waiting for transfers between devices: 240 us -> none  [the longest x1 120 us: body(): lax.all_gather(reduce_weight_gradient, 'narrow', axis=0, tiled=True)]
    psum x1 -> x0, blocking collectives: 58.4 us -> none  [body(): lax.psum((position_gradient, norm_one_gain_gradient, norm_one_shift_gradi...]
    all_gather x9 -> x0, blocking collectives: 41.7 us -> none  [the longest x1 4.86 us: body(): lax.all_gather(norm_two_gain_gradient, 'narrow', axis=0, tiled=True)]
    unnamed x161 -> x146, local copies, waits for them, and re-layouts: 72.5 us -> 60.9 us
  transfers between devices with their start and end apart: 11 -> 4, of which waited for: 8 -> 4; matrix products, arithmetic and copies ran while one was open for 6% -> 19% of each run, Pallas kernels for 0% -> 0%
where the time goes in v1:
time: 874 us; the launch traced here: 873 us
  waiting for transfers between devices  538 us (62%)
  matrix products  150 us (17%)
  local copies, waits for them, and re-layouts  112 us (13%)
  other arithmetic  57.7 us (7%)
  between operations  14.7 us (2%)
    psum x1, waiting for transfers between devices, body(): expand_weight_gradient = lax.psum(expand_weight_gradient, every)  157 us
    psum x1, waiting for transfers between devices, body(): mixed = lax.psum(mixed, every)  135 us
    psum x1, waiting for transfers between devices, body(): reduce_weight_gradient = lax.psum(reduce_weight_gradient, every)  124 us
    psum x1, waiting for transfers between devices, body(): project_weight_gradient = lax.psum(project_weight_gradient, every)  121 us
    unnamed x146, local copies, waits for them, and re-layouts  60.9 us
    dot_general x1, matrix products, body(): jnp.dot(second_low, expand_weight, preferred_element_type=f32)  48.8 us
    dot_general x1, matrix products, body(): jnp.einsum('rd,fd->rf', cotangent, reduce_weight, preferred_element_type=...  18.2 us
  transfers between devices with their start and end apart: 4, of which 4 were waited for; matrix products, arithmetic and copies ran while one was open for 19% of the time, Pallas kernels for 0%

profile of v1, /device:TPU:0, one launch (start us, length us, event | category | flops | bytes accessed | tf_op | source)
XLA Modules:
  0.0 872.6 jit_solution(10508515600622166546)
XLA Ops:
  17.2 6.9 gather_fusion
  32.9 4.6 add_convert_fusion.1
  66.2 48.8 %multiply_convert_fusion = (bf16[1024,3072]{1,0:T(8,128)(2,1)S(1)}, f32[1024,3072]{1,0:T(8,128)}, f32[1024,3072]{1,0:T(8,128)}) fusion(f32[3072]{0:T(1024)S(1)} %copy-done.44, bf16[768,3072]{1,0:T(8,128)(2,1)S(1)} %bitcast.106, f32[1024,768]{0,1:T(8,128)S(1)} %get-tuple-element.89, f32[768]{0:T(1024)S(1)} %copy-done.46, f32[768]{0:T(1024)S(1)} %convert_element_type.107, ...), kind=kOutput, calls=%fused_computation.6 | convolution fusion | flops 5043388416 | bytes 39348224 | tf_op jit(solution)/shard_map/dot_general | solution.py:106
  117.6 7.7 fusion.56
  127.9 18.2 %convert_reduce_fusion = (f32[3072]{0:T(1024)}, bf16[1024,3072]{1,0:T(8,128)(2,1)}) fusion(f32[1024,3072]{1,0:T(8,128)} %get-tuple-element.79, bf16[1024,768]{1,0:T(8,128)(2,1)} %param.35, bf16[3072,768]{1,0:T(8,128)(2,1)} %param.33, f32[1024,3072]{1,0:T(8,128)} %get-tuple-element.90, f32[3072]{0:T(1024)} %convert_element_type.110), kind=kOutput, calls=%fused_computation.4 | convolution fusion | flops 4885312512 | bytes 37773312 | tf_op jit(solution)/shard_map/rd,fd->rf/dot_general | solution.py:120
  146.1 10.4 %fusion.55 = (f32[768]{0:T(1024)}, f32[1024,768]{1,0:T(8,128)}) fusion(bf16[1024,3072]{1,0:T(8,128)(2,1)} %get-tuple-element.98, bf16[768,3072]{1,0:T(8,128)(2,1)} %param.31), kind=kOutput, calls=%fused_computation.138 | convolution fusion | flops 4832623616 | bytes 14158848 | tf_op jit(solution)/shard_map/rf,df->rd/dot_general | solution.py:126
  160.1 4.6 multiply_reduce_fusion.1
  179.2 5.3 fusion.23
  186.9 7.8 fusion.45
  194.8 124.4 %all-reduce.5.cloned.1.call-done = f32[3072,768]{1,0:T(8,128)} async-done(((f32[3072,768]{1,0:T(8,128)}), f32[3072,768]{1,0:T(8,128)}) %all-reduce.5.cloned.1.call-update) | async-done | bytes 9437200 | tf_op jit(solution)/shard_map/psum | solution.py:200
  319.2 5.7 multiply_reduce_fusion
  324.9 4.9 multiply_convert_fusion.1
  338.1 6.6 fusion.54
  348.3 10.9 %fusion.47 = f32[768,2304]{1,0:T(8,128)} fusion(bf16[1024,2304]{0,1:T(8,128)(2,1)} %copy-done.24, f32[768]{0:T(1024)} %convert_element_type.98, f32[768]{0:T(1024)S(1)} %copy-done.34, f32[1024]{0:T(1024)S(1)} %copy-done.36, f32[1024]{0:T(1024)S(1)} %copy-done.32, bf16[1024,768]{0,1:T(8,128)(2,1)} %copy.56, bf16[1024,768]{0,1:T(8,128)(2,1)} %copy.57, ...), kind=kOutput, calls=%fused_computation.132 | convolution fusion | flops 3630956544 | bytes 14957568 | tf_op jit(solution)/shard_map/rd,re->de/dot_general | solution.py:170
  359.2 157.3 %all-reduce.7.cloned.1.call-done = f32[768,3072]{1,0:T(8,128)} async-done(((f32[768,3072]{1,0:T(8,128)}), f32[768,3072]{1,0:T(8,128)}) %all-reduce.7.cloned.1.call-update) | async-done | bytes 9437200 | tf_op jit(solution)/shard_map/psum | solution.py:204
  516.7 4.8 multiply_reduce_fusion.2
  539.1 7.6 fusion.48
  550.3 9.5 %scatter_custom_fusion = f32[640,768]{1,0:T(8,128)} fusion(s32[1024]{0:T(1024)} %bitcast.103, f32[1024,768]{1,0:T(8,128)} %copy.82, f32[]{:T(128)} %constant.33.clone.1), kind=kCustom, calls=%fused_computation.82 | custom fusion | flops 786432 | bytes 1966592 | tf_op jit(solution)/shard_map/scatter-add | solution.py:181
  559.8 4.0 fusion.17
  566.2 121.2 %all-reduce.9.cloned.1.call-done = f32[768,2304]{1,0:T(8,128)} async-done(((f32[768,2304]{1,0:T(8,128)}), f32[768,2304]{1,0:T(8,128)}) %all-reduce.9.cloned.1.call-update) | async-done | bytes 7077904 | tf_op jit(solution)/shard_map/psum | solution.py:208
  687.5 10.0 %add_convert_fusion.2 = bf16[1024,768]{0,1:T(8,128)(2,1)} fusion(f32[1024,768]{0,1:T(8,128)} %copy-done.6, bf16[1024,3072]{1,0:T(8,128)(2,1)} %copy-done.54, bf16[3072,768]{1,0:T(8,128)(2,1)} %param.33, f32[768]{0:T(1024)S(1)} %convert_element_type.112), kind=kOutput, calls=%fused_computation.44 | convolution fusion | flops 4834197504 | bytes 15731712 | tf_op jit(solution)/shard_map/dot_general | solution.py:113
  702.6 134.6 %all-reduce.11.cloned.1.call-done = f32[1424,768]{1,0:T(8,128)} async-done(((f32[1424,768]{1,0:T(8,128)}), f32[1424,768]{1,0:T(8,128)}) %all-reduce.11.cloned.1.call-update) | async-done | bytes 4374544 | tf_op jit(solution)/shard_map/psum | solution.py:215
  846.5 7.0 copy.155
  853.5 8.7 copy.156
  (214 shorter events, 126.4 us)
Async XLA Ops:
  7.2 25.7 %copy-start = (bf16[768,2304]{1,0:T(8,128)(2,1)S(1)}, bf16[768,2304]{1,0:T(8,128)(2,1)}, u32[]{:S(2)}) copy-start(bf16[768,2304]{1,0:T(8,128)(2,1)} %param.24) | copy-start | bytes 10616836
  7.2 312.0 %all-reduce.5.cloned.1.call-start = ((), (), s32[]{:S(2)}) async-start(), calls=%async_computation | async-start | bytes 18874368 | tf_op jit(solution)/shard_map/psum | solution.py:200
  9.8 53.0 %copy-start.37 = (pred[1024]{0:T(1024)(128)(4,1)}, pred[1024]{0:T(1024)(128)(4,1)S(1)}, u32[]{:S(2)}) copy-start(pred[1024]{0:T(1024)(128)(4,1)S(1)} %get-tuple-element.80) | copy-start | bytes 3076
  10.5 22.4 %copy-start.33 = (f32[768]{0:T(1024)}, f32[768]{0:T(1024)S(1)}, u32[]{:S(2)}) copy-start(f32[768]{0:T(1024)S(1)} %convert_element_type.97) | copy-start | bytes 9220
  65.2 49.7 %copy-start.6 = (f32[1024,768]{0,1:T(8,128)}, f32[1024,768]{0,1:T(8,128)S(1)}, u32[]{:S(2)}) copy-start(f32[1024,768]{0,1:T(8,128)S(1)} %get-tuple-element.89) | copy-start | bytes 9437188
  66.2 51.4 %copy-start.20 = (bf16[1024,768]{1,0:T(8,128)(2,1)S(1)}, bf16[1024,768]{1,0:T(8,128)(2,1)}, u32[]{:S(2)}) copy-start(bf16[1024,768]{1,0:T(8,128)(2,1)} %param.35) | copy-start | bytes 4718596
  125.3 391.3 %all-reduce.7.cloned.1.call-start = ((), (), s32[]{:S(2)}) async-start(), calls=%async_computation.1 | async-start | bytes 18874368 | tf_op jit(solution)/shard_map/psum | solution.py:204
  164.9 5.6 copy-start.53
  175.9 11.0 %slice-start.5 = ((s8[6291456]{0:T(1024)(128)(4,1)}), s8[4194304]{0:T(1024)(128)(4,1)S(1)}, s32[]{:S(2)}) async-start(s8[6291456]{0:T(1024)(128)(4,1)} %bitcast.107), calls=%async_computation.9 | async-start | bytes 8388608
  178.1 6.4 copy-start.22
  179.2 7.8 slice-start.6
  319.2 368.2 %all-reduce.9.cloned.1.call-start = ((), (), s32[]{:S(2)}) async-start(), calls=%async_computation.2 | async-start | bytes 14155776 | tf_op jit(solution)/shard_map/psum | solution.py:208
  319.2 5.7 copy-start.23
  338.1 6.6 copy-start.24
  516.6 320.6 %all-reduce.11.cloned.1.call-start = ((), (), s32[]{:S(2)}) async-start(), calls=%async_computation.3 | async-start | bytes 8749056 | tf_op jit(solution)/shard_map/psum | solution.py:215
  521.4 8.5 copy-start.41
  521.4 9.8 %copy-start.39 = (f32[768]{0:T(1024)S(1)}, f32[768]{0:T(1024)}, u32[]{:S(2)}) copy-start(f32[768]{0:T(1024)} %get-tuple-element.62) | copy-start | bytes 9220
  521.4 11.1 %copy-start.48 = (f32[768]{0:T(1024)S(1)}, f32[768]{0:T(1024)}, u32[]{:S(2)}) copy-start(f32[768]{0:T(1024)} %get-tuple-element.95) | copy-start | bytes 9220
  521.4 12.4 %copy-start.40 = (f32[768]{0:T(1024)S(1)}, f32[768]{0:T(1024)}, u32[]{:S(2)}) copy-start(f32[768]{0:T(1024)} %get-tuple-element.85) | copy-start | bytes 9220
  521.4 13.7 %copy-start.43 = (f32[3072]{0:T(1024)S(1)}, f32[3072]{0:T(1024)}, u32[]{:S(2)}) copy-start(f32[3072]{0:T(1024)} %get-tuple-element.97) | copy-start | bytes 36868
  566.2 121.2 %copy-start.51 = (bf16[768]{0:T(1024)(128)(2,1)S(1)}, bf16[768]{0:T(1024)(128)(2,1)}, u32[]{:S(2)}) copy-start(bf16[768]{0:T(1024)(128)(2,1)} %param.34) | copy-start | bytes 4612
  846.5 15.7 %slice-start = ((s8[9437184]{0:T(1024)(128)(4,1)}), s8[4194304]{0:T(1024)(128)(4,1)S(1)}, s32[]{:S(2)}) async-start(s8[9437184]{0:T(1024)(128)(4,1)} %bitcast.87), calls=%async_computation.4 | async-start | bytes 8388608
  846.5 15.7 %slice-start.1 = ((s8[9437184]{0:T(1024)(128)(4,1)}), s8[4194304]{0:T(1024)(128)(4,1)S(1)}, s32[]{:S(2)}) async-start(s8[9437184]{0:T(1024)(128)(4,1)} %bitcast.87), calls=%async_computation.5 | async-start | bytes 8388608
  853.4 8.7 slice-start.2
  (42 other events, 121.7 us)
Sparse Core Ops, SparseCore 0:
  125.4 193.7 all-reduce.4
  325.5 191.0 all-reduce.6
  523.0 164.3 all-reduce.8
  693.5 143.6 all-reduce.10

commit v2 on v1

v2 whole, which is shorter than its diff:
```python
import itertools

import jax
import jax.numpy as jnp
from jax import lax
from jax.experimental import pallas as pl
from jax.experimental.pallas import tpu as pltpu
from jax.sharding import Mesh, PartitionSpec as P

HEADS = 12
PATCH_LO = 128
BLOCK = 256
WIDE = 512
PLAN = "|a|b|a|b|ab||paq+mbpaqbmapqbmpaqb*pmaqpbampqbmpqmpqqmm"

SMALL = pl.CostEstimate(flops=1, transcendentals=0, bytes_accessed=1)

epsilon = 1e-06
big_negative = -1e30
f32 = jnp.float32
bf16 = jnp.bfloat16


AXES = ("z", "y", "c", "x")
CHIPS_FIRST = ("z", "y", "x", "c")


def pairs(sizes, target):
    found = []
    for here in itertools.product(*(range(n) for n in sizes)):
        there = target(*here)
        if there is not None:
            found.append((flat(sizes, here), flat(sizes, there)))
    return found


def flat(sizes, place):
    index = 0
    for n, k in zip(sizes, place):
        index = index * n + k
    return index


def send(value, sizes, target):
    return lax.ppermute(value, AXES, pairs(sizes, target))


def across_core(z, y, c, x):
    return (z, y, 1 - c, x)


def plane_one(z, y, c, x):
    return (z, y, c, 1 - x) if c == 0 else (z, 1 - y, c, x)


def plane_two(z, y, c, x):
    return (z, 1 - y, c, x) if c == 0 else (z, y, c, 1 - x)


def ends_in(z, y, c, x):
    return {0: (1, y, c, x), 3: (2, y, c, x)}.get(z)


def middle(z, y, c, x):
    return {1: (2, y, c, x), 2: (1, y, c, x)}.get(z)


def ends_out(z, y, c, x):
    return {1: (0, y, c, x), 2: (3, y, c, x)}.get(z)


def half(value, index):
    rows = value.shape[0] // 2
    return lax.dynamic_slice_in_dim(value, index * rows, rows, 0)


def join(own, other, index):
    return jnp.concatenate(
        [jnp.where(index == 0, own, other), jnp.where(index == 0, other, own)], axis=0
    )


class Order:
    def __init__(self, token):
        self.token = token

    def tie(self, *values):
        *values, self.token = lax.optimization_barrier((*values, self.token))
        return values[0] if len(values) == 1 else tuple(values)


def plane_first(parts, sizes):
    z, y, c, x = (lax.axis_index(axis) for axis in AXES)
    first = jnp.where(c == 0, x, y)
    second = jnp.where(c == 0, y, x)
    other = sum(half(part, 1 - c) for part in parts)
    came = yield other, across_core
    value = sum(half(part, c) for part in parts) + came
    came = yield half(value, 1 - first), plane_one
    value = half(value, first) + came
    came = yield half(value, 1 - second), plane_two
    value = half(value, second) + came
    value = value + (yield value, ends_in)
    value = value + (yield value, middle)
    came = yield value, ends_out
    value = jnp.where((z == 0) | (z == 3), came, value)
    value = join(value, (yield value, plane_two), second)
    value = join(value, (yield value, plane_one), first)
    came = yield value, across_core
    return value, came


class Sums:
    def __init__(self, sizes, order):
        self.sizes, self.order = sizes, order
        self.steps, self.flying, self.results = {}, {}, {}

    def begin(self, name, steps):
        self.steps[name] = steps
        self.post(name, next(steps))

    def post(self, name, step):
        value, target = step
        self.flying[name] = send(self.order.tie(value), self.sizes, target)

    def wait(self, *names):
        for name in names:
            came = self.order.tie(self.flying.pop(name))
            try:
                step = self.steps[name].send(came)
            except StopIteration as stop:
                self.results[name] = stop.value
            else:
                self.post(name, step)


def assemble(index, pairs, begin, rows, block):
    count = len(pairs)
    steps = rows // block
    lead = begin // block
    width = sum(own.shape[1] for own, _ in pairs)

    def kernel(where, *refs):
        mine = pl.program_id(0) == where[0]
        out = refs[-1]
        at = 0
        for own, other in zip(refs[:count], refs[count : 2 * count]):
            span = slice(at, at + own.shape[1])
            at += own.shape[1]

            @pl.when(mine)
            def _():
                out[:, span] = own[...]

            @pl.when(jnp.logical_not(mine))
            def _():
                out[:, span] = other[...]

    def own_map(h, i, where):
        return (lead + jnp.where(h == where[0], i, jnp.where(h == 0, 0, steps - 1)), 0)

    def other_map(h, i, where):
        return (lead + jnp.where(h == where[0], jnp.where(h == 0, 0, steps - 1), i), 0)

    return pl.pallas_call(
        kernel,
        name="assemble",
        grid_spec=pltpu.PrefetchScalarGridSpec(
            num_scalar_prefetch=1,
            grid=(2, steps),
            in_specs=[pl.BlockSpec((block, own.shape[1]), own_map) for own, _ in pairs]
            + [pl.BlockSpec((block, own.shape[1]), other_map) for own, _ in pairs],
            out_specs=pl.BlockSpec((block, width), lambda h, i, where: (h * steps + i, 0)),
        ),
        out_shape=jax.ShapeDtypeStruct((2 * rows, width), f32),
    )(jnp.reshape(index, (1,)), *(own for own, _ in pairs), *(other for _, other in pairs))


def copy_kernel(source, target):
    target[...] = source[...]


def copied(array, block):
    spec = pl.BlockSpec((block, array.shape[1]), lambda i: (i, 0))
    return pl.pallas_call(
        copy_kernel,
        name="copied",
        grid=(array.shape[0] // block,),
        in_specs=[spec],
        out_specs=spec,
        out_shape=jax.ShapeDtypeStruct(array.shape, array.dtype),
    )(array)


def divide_kernel(where, own, other, weights, places, small):
    heads_half, place_half = weights.shape[0] // 2, places.shape[0] // 2
    top = own.shape[0]

    def fill(low, high):
        weights[:heads_half, :] = low[:heads_half, :]
        weights[heads_half:, :] = high[:heads_half, :]
        places[:place_half, :] = low[heads_half : heads_half + place_half, :]
        places[place_half:, :] = high[heads_half : heads_half + place_half, :]
        small[...] = low[top - 32 :, :]

    @pl.when(where[0] == 0)
    def _():
        fill(own, other)

    @pl.when(where[0] != 0)
    def _():
        fill(other, own)


def mm(first, second):
    return lax.dot_general(first, second, (((1,), (0,)), ((), ())), preferred_element_type=f32)


def mm_nt(first, second):
    return lax.dot_general(first, second, (((1,), (1,)), ((), ())), preferred_element_type=f32)


def mm_tn(first, second):
    return lax.dot_general(first, second, (((0,), (0,)), ((), ())), preferred_element_type=f32)


def normalize(stream):
    centre = stream - jnp.mean(stream, axis=-1, keepdims=True)
    inverse = lax.rsqrt(jnp.mean(centre * centre, axis=-1, keepdims=True) + epsilon)
    return centre * inverse, inverse


def norm_backward(upstream, normed, inverse, gain):
    scaled = upstream * gain
    inner = jnp.mean(scaled * normed, axis=-1, keepdims=True)
    return inverse * (scaled - jnp.mean(scaled, axis=-1, keepdims=True) - normed * inner)


def column_sum(value):
    return jnp.sum(value, axis=0, keepdims=True)


def two_heads(pair, low_lanes):
    zero = jnp.zeros_like(pair)
    return jnp.concatenate(
        [jnp.where(low_lanes, pair, zero), jnp.where(low_lanes, zero, pair)], axis=0
    )


def pair_probs(queries_two, keys_pair, same):
    scores = jnp.where(same, mm_nt(queries_two, keys_pair), big_negative)
    exponent = jnp.exp(scores - jnp.max(scores, axis=-1, keepdims=True))
    return exponent * (1.0 / jnp.sum(exponent, axis=-1, keepdims=True))


def front_kernel(
    tokens,
    place_column,
    sample_column,
    sample_row,
    table,
    one_gain,
    one_shift,
    project_weight,
    joined_bias,
    output_weight,
    output_bias,
    two_gain,
    two_shift,
    stream_out,
    first_out,
    projected_out,
    heads_out,
    mid_out,
    second_out,
):
    rows, width = tokens.shape
    group = sample_row.shape[2]
    scale = (width // HEADS) ** (-0.5)
    places = lax.broadcasted_iota(jnp.int32, (rows, table.shape[0]), 1)
    chosen = (places == place_column[...]).astype(bf16)
    stream = tokens[...].astype(f32) + mm(chosen, table[...])
    stream_out[...] = stream
    normed, _ = normalize(stream)
    first = (normed * one_gain[...] + one_shift[...]).astype(bf16)
    first_out[...] = first
    projected_out[...] = (mm(first, project_weight[...]) + joined_bias[...]).astype(bf16)
    low_lanes = lax.broadcasted_iota(jnp.int32, (group, 128), 1) < 64
    for g in range(rows // group):
        span = slice(g * group, (g + 1) * group)
        same = sample_column[span, :] == sample_row[g]
        same = jnp.concatenate([same, same], axis=0)
        for j in range(width // 128):
            queries = projected_out[span, j * 128 : (j + 1) * 128] * bf16(scale)
            keys = projected_out[span, width + j * 128 : width + (j + 1) * 128]
            values = projected_out[span, 2 * width + j * 128 : 2 * width + (j + 1) * 128]
            probs = pair_probs(two_heads(queries, low_lanes), keys, same)
            both = mm(probs.astype(bf16), values)
            heads_out[span, j * 128 : (j + 1) * 128] = jnp.where(
                low_lanes, both[:group], both[group:]
            ).astype(bf16)
    mid = stream + (mm(heads_out[...], output_weight[...]) + output_bias[...])
    mid_out[...] = mid
    normed, _ = normalize(mid)
    second_out[...] = (normed * two_gain[...] + two_shift[...]).astype(bf16)


def expand_kernel(
    second, cotangent, expand_weight, expand_bias, hidden_out, slope_out, reduce_gradient
):
    before = mm(second[...], expand_weight[...]) + expand_bias[...]
    below = 0.5 * (1.0 + lax.erf(before * (0.5**0.5)))
    density = jnp.exp(-0.5 * before * before) * 0.3989422804014327
    hidden = (before * below).astype(bf16)
    hidden_out[...] = hidden
    slope_out[...] = (below + before * density).astype(bf16)
    reduce_gradient[...] = mm_tn(hidden, cotangent[...])


def reduce_kernel(
    second,
    cotangent,
    before_total,
    before_gradient,
    hidden,
    slope,
    expand_weight,
    reduce_weight,
    reduce_bias,
    total,
    second_gradient,
    expand_gradient,
    bias_gradient,
    *,
    fresh,
):
    step = pl.program_id(0)
    gradient = mm_nt(cotangent[...], reduce_weight[...])
    low = (gradient * slope[...].astype(f32)).astype(bf16)
    bias_gradient[0] = column_sum(low.astype(f32))
    expand_gradient[...] = mm_tn(second[...], low)
    back = mm_nt(low, expand_weight[...])
    ahead = mm(hidden[...], reduce_weight[...])

    @pl.when(step == 0)
    def _():
        if fresh:
            second_gradient[...] = back
            total[...] = before_total[...] + reduce_bias[...] + ahead
        else:
            second_gradient[...] = before_gradient[...] + back
            total[...] = before_total[...] + ahead

    @pl.when(step > 0)
    def _():
        second_gradient[...] += back
        total[...] += ahead


def first_reduce_kernel(
    second, cotangent, mid, hidden, slope, expand_weight, reduce_weight, reduce_bias, *outs
):
    reduce_kernel(
        second, cotangent, mid, None, hidden, slope, expand_weight, reduce_weight, reduce_bias,
        *outs, fresh=True,
    )


def last_reduce_kernel(
    second, cotangent, before_total, before_gradient, hidden, slope, expand_weight,
    reduce_weight, layer_out, second_gradient, expand_gradient, bias_gradient, total,
):
    reduce_kernel(
        second, cotangent, before_total, before_gradient, hidden, slope, expand_weight,
        reduce_weight, None, total, second_gradient, expand_gradient, bias_gradient,
        fresh=False,
    )

    @pl.when(pl.program_id(0) == pl.num_programs(0) - 1)
    def _():
        layer_out[...] = total[...].astype(bf16)


def back_kernel(
    second_gradient,
    mid,
    stream,
    cotangent,
    projected,
    sample_column,
    sample_row,
    one_gain,
    two_gain,
    output_weight,
    project_weight,
    *rest,
):
    token_gradient, in_gradient_out, pieces, branch_out, sums = rest[-5:]
    rows, width = stream.shape
    group = sample_row.shape[2]
    scale = (width // HEADS) ** (-0.5)
    upstream = second_gradient[...]
    out_gradient = cotangent[...].astype(f32)
    normed, inverse = normalize(mid[...])
    two_gain_gradient = column_sum(upstream * normed)
    two_shift_gradient = column_sum(upstream)
    mid_gradient = out_gradient + norm_backward(upstream, normed, inverse, two_gain[...])
    branch = mid_gradient.astype(bf16)
    branch_out[...] = branch
    bias_gradient = column_sum(branch.astype(f32))
    heads_gradient = mm_nt(branch, output_weight[...]).astype(bf16)
    low_lanes = lax.broadcasted_iota(jnp.int32, (group, 128), 1) < 64
    for g in range(rows // group):
        span = slice(g * group, (g + 1) * group)
        same = sample_column[span, :] == sample_row[g]
        same = jnp.concatenate([same, same], axis=0)
        for j in range(width // 128):
            here = [
                slice(k * width + j * 128, k * width + (j + 1) * 128) for k in range(3)
            ]
            queries = two_heads(projected[span, here[0]] * bf16(scale), low_lanes)
            keys = projected[span, here[1]]
            values = projected[span, here[2]]
            upper = two_heads(heads_gradient[span, here[0]], low_lanes)
            probs = pair_probs(queries, keys, same)
            weight_gradient = mm_nt(upper, values)
            inner = jnp.sum(weight_gradient * probs, axis=-1, keepdims=True)
            score_gradient = (probs * (weight_gradient - inner)).astype(bf16)
            both = mm(score_gradient, keys)
            pieces[span, here[0]] = (
                jnp.where(low_lanes, both[:group], both[group:]) * scale
            ).astype(bf16)
            pieces[span, here[1]] = mm_tn(score_gradient, queries).astype(bf16)
            pieces[span, here[2]] = mm_tn(probs.astype(bf16), upper).astype(bf16)
    upstream = mm_nt(pieces[...], project_weight[...])
    normed, inverse = normalize(stream[...])
    in_gradient = mid_gradient + norm_backward(upstream, normed, inverse, one_gain[...])
    in_gradient_out[...] = in_gradient
    token_gradient[...] = in_gradient.astype(bf16)
    sums[0] = jnp.concatenate(
        [
            column_sum(upstream * normed),
            column_sum(upstream),
            column_sum(pieces[:, :width].astype(f32)),
            column_sum(pieces[:, 2 * width :].astype(f32)),
            bias_gradient,
            two_gain_gradient,
            two_shift_gradient,
            column_sum(out_gradient),
        ],
        axis=0,
    )


def project_kernel(first, pieces, project_gradient):
    project_gradient[...] = mm_tn(first[...], pieces[...])


def mixed_kernel(heads, branch, in_gradient, place_row, sums, expand_bias_gradient, mixed):
    rows, width = heads.shape
    top = mixed.shape[0] // 2
    heads_half = width // 2
    place_half = top - heads_half - 32
    both = mm_tn(heads[...], branch[...])
    mixed[:heads_half, :] = both[:heads_half]
    mixed[top : top + heads_half, :] = both[heads_half:]
    high = in_gradient[...].astype(bf16)
    low = (in_gradient[...] - high.astype(f32)).astype(bf16)
    numbers = lax.broadcasted_iota(jnp.int32, (2 * place_half, rows), 0)
    chosen = (numbers == place_row[...]).astype(bf16)
    both = mm(chosen, high) + mm(chosen, low)
    mixed[heads_half : heads_half + place_half, :] = both[:place_half]
    mixed[top + heads_half : top + heads_half + place_half, :] = both[place_half:]
    mixed[top - 32 : top, :] = jnp.zeros((32, width), f32)
    mixed[2 * top - 32 :, :] = jnp.zeros((32, width), f32)
    total = sums[0]
    for k in range(1, sums.shape[0]):
        total = total + sums[k]
    mixed[top - 32 : top - 24, :] = total
    mixed[top - 24 : top - 20, :] = expand_bias_gradient[...]


def whole(array):
    return pl.BlockSpec(array.shape, lambda i: (0,) * array.ndim)


def row_block(array):
    return pl.BlockSpec((BLOCK, array.shape[1]), lambda i: (i, 0))


def lead_block(array, count=1):
    return pl.BlockSpec((count,) + array.shape[1:], lambda i: (i, 0, 0))


def shape(dims, kind):
    return jax.ShapeDtypeStruct(dims, kind)


def body(
    tokens,
    kept_patches,
    resolution,
    position_table,
    norm_one_gain,
    norm_one_shift,
    project_weight,
    query_bias,
    value_bias,
    output_weight,
    output_bias,
    norm_two_gain,
    norm_two_shift,
    expand_weight,
    expand_bias,
    reduce_weight,
    reduce_bias,
    cotangent,
):
    groups, group_rows = kept_patches.shape
    rows, width = tokens.shape
    hidden_width = expand_weight.shape[1]
    places = position_table.shape[0]
    per_step = BLOCK // group_rows
    fine_grid = resolution[:, None] == 1
    place = jnp.where(fine_grid, PATCH_LO + kept_patches, kept_patches % PATCH_LO)
    sample = jnp.where(fine_grid, 0, kept_patches // PATCH_LO)
    place_column = place.reshape(rows, 1)
    place_row = place.reshape(1, rows)
    sample_column = sample.reshape(rows, 1)
    sample_row = sample.reshape(groups, 1, group_rows)

    def line(vector):
        return vector.astype(f32).reshape(1, -1)

    one_gain, two_gain = line(norm_one_gain), line(norm_two_gain)
    joined_bias = line(jnp.concatenate([query_bias, jnp.zeros_like(query_bias), value_bias]))
    front_shapes = (
        shape((rows, width), f32),
        shape((rows, width), bf16),
        shape((rows, 3 * width), bf16),
        shape((rows, width), bf16),
        shape((rows, width), f32),
        shape((rows, width), bf16),
    )
    fixed = (
        position_table,
        one_gain,
        line(norm_one_shift),
        project_weight,
        joined_bias,
        output_weight,
        line(output_bias),
        two_gain,
        line(norm_two_shift),
    )
    stream, first, projected, heads, mid, second = pl.pallas_call(
        front_kernel,
        name="front",
        grid=(rows // BLOCK,),
        in_specs=[
            row_block(tokens),
            row_block(place_column),
            row_block(sample_column),
            lead_block(sample_row, per_step),
        ]
        + [whole(array) for array in fixed],
        out_specs=[row_block(array) for array in front_shapes],
        out_shape=front_shapes,
    )(tokens, place_column, sample_column, sample_row, *fixed)

    columns = pl.BlockSpec((width, WIDE), lambda i: (0, i))
    tall = pl.BlockSpec((rows, WIDE), lambda i: (0, i))
    lines = pl.BlockSpec((WIDE, width), lambda i: (i, 0))
    bias_row = line(expand_bias)
    hidden, slope, reduce_weight_gradient = pl.pallas_call(
        expand_kernel,
        name="expand",
        grid=(hidden_width // WIDE,),
        in_specs=[
            whole(second),
            whole(cotangent),
            columns,
            pl.BlockSpec((1, WIDE), lambda i: (0, i)),
        ],
        out_specs=[tall, tall, lines],
        out_shape=(
            shape((rows, hidden_width), bf16),
            shape((rows, hidden_width), bf16),
            shape((hidden_width, width), f32),
        ),
    )(second, cotangent, expand_weight, bias_row)

    sizes = tuple(lax.axis_size(axis) for axis in AXES)
    paired = sizes == (4, 2, 2, 2)
    order = Order(place_row)
    sums = Sums(sizes, order)
    reduce_weight_gradient, second = order.tie(reduce_weight_gradient, second)
    if paired:
        reduce_weight_gradient = lax.psum_scatter(
            reduce_weight_gradient, CHIPS_FIRST, scatter_dimension=0, tiled=True
        )
    plan = iter(PLAN)

    def advance():
        for name in plan:
            if name == "|":
                break
            if name == "+" and paired:
                sums.results["w"] = lax.all_gather(
                    order.tie(reduce_weight_gradient), CHIPS_FIRST, axis=0, tiled=True
                )
            elif name == "*" and paired:
                sums.results["w"] = order.tie(copied(order.tie(sums.results["w"]), 3 * WIDE // 2))
            elif paired:
                sums.wait(name)
                for both in ("ab", "pq"):
                    if both not in sums.results and all(one in sums.results for one in both):
                        pairs = tuple(order.tie(*sums.results[one]) for one in both)
                        sums.results[both] = order.tie(
                            assemble(lax.axis_index("c"), pairs, 0, width // 2, width // 4)
                        )

    reduce_row = line(reduce_bias)
    half_steps = hidden_width // WIDE // 2
    part = hidden_width // 2
    reduce_shapes = (
        shape((rows, width), f32),
        shape((rows, width), f32),
        shape((width, part), f32),
        shape((half_steps, 1, WIDE), f32),
    )

    def from_step(begin):
        return [
            pl.BlockSpec((rows, WIDE), lambda i: (0, i + begin)),
            pl.BlockSpec((rows, WIDE), lambda i: (0, i + begin)),
            pl.BlockSpec((width, WIDE), lambda i: (0, i + begin)),
            pl.BlockSpec((WIDE, width), lambda i: (i + begin, 0)),
        ]

    reduce_outs = [whole(mid), whole(mid), columns, pl.BlockSpec((1, 1, WIDE), lambda i: (i, 0, 0))]
    so_far, second_gradient, expand_one, bias_one = pl.pallas_call(
        first_reduce_kernel,
        name="reduce_one",
        cost_estimate=SMALL,
        grid=(half_steps,),
        in_specs=[whole(second), whole(cotangent), whole(mid)] + from_step(0) + [whole(reduce_row)],
        out_specs=reduce_outs,
        out_shape=reduce_shapes,
    )(second, cotangent, mid, hidden, slope, expand_weight, reduce_weight, reduce_row)
    if paired:
        sums.begin("a", plane_first([order.tie(expand_one)], sizes))
    advance()
    second_gradient = order.tie(second_gradient)
    layer_output, second_gradient, expand_two, bias_two = pl.pallas_call(
        last_reduce_kernel,
        name="reduce_two",
        cost_estimate=SMALL,
        grid=(half_steps,),
        in_specs=[whole(second), whole(cotangent), whole(mid), whole(mid)] + from_step(half_steps),
        out_specs=[whole(tokens)] + reduce_outs[1:],
        out_shape=(shape((rows, width), bf16),) + reduce_shapes[1:],
        scratch_shapes=[pltpu.VMEM((rows, width), f32)],
    )(second, cotangent, so_far, second_gradient, hidden, slope, expand_weight, reduce_weight)
    expand_two = order.tie(expand_two)
    if paired:
        sums.begin("b", plane_first([expand_two], sizes))
    advance()

    wide_shape = shape((rows, 3 * width), bf16)
    count = rows // BLOCK
    back_shapes = (
        shape((rows, width), bf16),
        shape((rows, width), f32),
        wide_shape,
        shape((rows, width), bf16),
        shape((count, 8, width), f32),
    )
    backs = ()
    for begin in range(count):

        def some(array):
            return pl.BlockSpec((BLOCK, array.shape[1]), lambda i, begin=begin: (begin, 0))

        def lead(size):
            return pl.BlockSpec(size, lambda i, begin=begin: (begin, 0, 0))

        backs = pl.pallas_call(
            back_kernel,
            name="back",
            cost_estimate=SMALL,
            grid=(1,),
            in_specs=[
                some(mid),
                some(mid),
                some(stream),
                some(cotangent),
                some(projected),
                some(sample_column),
                lead((per_step, 1, group_rows)),
                whole(one_gain),
                whole(two_gain),
                whole(output_weight),
                whole(project_weight),
            ]
            + [pl.BlockSpec(memory_space=pl.ANY)] * len(backs),
            out_specs=[some(array) for array in back_shapes[:4]] + [lead((1, 8, width))],
            out_shape=back_shapes,
            input_output_aliases={11 + k: k for k in range(len(backs))},
        )(
            order.tie(second_gradient),
            mid,
            stream,
            cotangent,
            projected,
            sample_column,
            sample_row,
            one_gain,
            two_gain,
            output_weight,
            project_weight,
            *backs,
        )
        backs = order.tie(*backs)
        advance()
    token_gradient, in_gradient, pieces, branch, block_sums = backs

    cut = 3 * width // 2
    narrow_block = width // 2
    project_gradient = pl.pallas_call(
        project_kernel,
        name="project",
        cost_estimate=SMALL,
        grid=(3 * width // narrow_block,),
        in_specs=[whole(first), pl.BlockSpec((rows, narrow_block), lambda i: (0, i))],
        out_specs=pl.BlockSpec((width, narrow_block), lambda i: (0, i)),
        out_shape=shape((width, 3 * width), f32),
    )(first, order.tie(pieces))
    project_gradient = order.tie(project_gradient)
    if paired:
        sums.begin("p", plane_first([project_gradient[:, :cut]], sizes))
        sums.begin("q", plane_first([project_gradient[:, cut:]], sizes))
    advance()
    heads_half, place_half = width // 2, places // 2
    top = heads_half + place_half + 32
    bias_rows = jnp.concatenate([bias_one, bias_two]).reshape(-1, width)
    mixed_inputs = (heads, order.tie(branch), in_gradient, place_row, block_sums, bias_rows)
    mixed_shape = shape((2 * top, width), f32)
    mixed = pl.pallas_call(
        mixed_kernel,
        name="mixed",
        cost_estimate=SMALL,
        grid=(1,),
        in_specs=[whole(array) for array in mixed_inputs],
        out_specs=whole(mixed_shape),
        out_shape=mixed_shape,
    )(*mixed_inputs)
    mixed = order.tie(mixed)
    if paired:
        sums.begin("m", plane_first([mixed], sizes))
        advance()
        core = lax.axis_index("c")
        done = sums.results
        reduce_weight_gradient = done["w"]
        expand_weight_gradient, project_weight_gradient = done["ab"], done["pq"]
        output_weight_gradient, position_gradient, small = pl.pallas_call(
            divide_kernel,
            name="divide",
            in_specs=[pl.BlockSpec(memory_space=pltpu.SMEM)]
            + [pl.BlockSpec(memory_space=pltpu.VMEM)] * 2,
            out_specs=[pl.BlockSpec(memory_space=pltpu.VMEM)] * 3,
            out_shape=(
                shape((width, width), f32),
                shape((places, width), f32),
                shape((32, width), f32),
            ),
        )(jnp.reshape(core, (1,)), *done["m"])
    else:
        (
            reduce_weight_gradient,
            expand_weight_gradient,
            project_weight_gradient,
            mixed,
        ) = lax.psum(
            (
                reduce_weight_gradient,
                jnp.concatenate([expand_one, expand_two], axis=1),
                project_gradient,
                mixed,
            ),
            AXES,
        )
        mixed = mixed.reshape(2, top, width)
        output_weight_gradient = mixed[:, :heads_half].reshape(width, width)
        position_gradient = mixed[:, heads_half : top - 32].reshape(places, width)
        small = mixed[0, top - 32 :]
    (
        norm_one_gain_gradient,
        norm_one_shift_gradient,
        query_bias_gradient,
        value_bias_gradient,
        output_bias_gradient,
        norm_two_gain_gradient,
        norm_two_shift_gradient,
        reduce_bias_gradient,
    ) = (small[k] for k in range(8))
    expand_bias_gradient = small[8:12].reshape(-1)
    return (
        layer_output,
        token_gradient,
        position_gradient,
        norm_one_gain_gradient,
        norm_one_shift_gradient,
        project_weight_gradient,
        query_bias_gradient,
        value_bias_gradient,
        output_weight_gradient,
        output_bias_gradient,
        norm_two_gain_gradient,
        norm_two_shift_gradient,
        expand_weight_gradient,
        expand_bias_gradient,
        reduce_weight_gradient,
        reduce_bias_gradient,
    )


def solution(mesh):
    wide, narrow = mesh.shape["wide"], mesh.shape["narrow"]
    mesh = Mesh(mesh.devices.reshape(wide // 4, 2, 2, narrow), AXES)
    placed = (
        P(AXES, None),
        P(AXES, None),
        P(AXES),
        P(),
        P(),
        P(),
        P(),
        P(),
        P(),
        P(),
        P(),
        P(),
        P(),
        P(),
        P(),
        P(),
        P(),
        P(AXES, None),
    )
    return jax.shard_map(
        body,
        mesh=mesh,
        in_specs=placed,
        out_specs=(
            P(AXES, None),
            P(AXES, None),
            P(),
            P(),
            P(),
            P(),
            P(),
            P(),
            P(),
            P(),
            P(),
            P(),
            P(),
            P(),
            P(),
            P(),
        ),
        check_vma=False,
    )
```

time: 874 us -> 471 us (0.54)
  waiting for transfers between devices: 538 us -> 130 us
  Pallas kernels: 0 us -> 177 us
  matrix products: 150 us -> 0 us
  local copies, waits for them, and re-layouts: 112 us -> 41.1 us
  starting transfers between devices: 0.16 us -> 57.9 us
  other arithmetic: 57.7 us -> 44.3 us
    psum x4 -> x0, waiting for transfers between devices: 538 us -> none  [the longest x1 157 us: body(): expand_weight_gradient = lax.psum(expand_weight_gradient, every)]
    pallas_call x0 -> x14, Pallas kernels: none -> 177 us  [the longest x4 54.6 us: body(): pl.pallas_call(back_kernel, name='back', cost_estimate=SMALL, grid=(1,),...]
    dot_general x18 -> x0, matrix products: 150 us -> none  [the longest x1 48.8 us: body(): jnp.dot(second_low, expand_weight, preferred_element_type=f32)]
    ppermute x0 -> x45, waiting for transfers between devices: none -> 129 us  [send(): return lax.ppermute(value, AXES, pairs(sizes, target))]
    ppermute x0 -> x45, starting transfers between devices: none -> 57.3 us  [send(): return lax.ppermute(value, AXES, pairs(sizes, target))]
    unnamed x146 -> x38, local copies, waits for them, and re-layouts: 60.9 us -> 7.11 us
    add x1 -> x25, other arithmetic: 0.02 us -> 28.3 us  [the longest x5 10.2 us: plane_first(): value = sum((half(part, c) for part in parts)) + came]
    reduce_sum x9 -> x0, other arithmetic: 22 us -> none  [the longest x2 9.42 us: norm_backward(): jnp.sum(upstream * normed, axis=0)]
  transfers between devices with their start and end apart: 4 -> 47, of which waited for: 4 -> 12; matrix products, arithmetic and copies ran while one was open for 19% -> 13% of each run, Pallas kernels for 0% -> 29%
where the time goes in v2:
time: 471 us; the launch traced here: 465 us
  Pallas kernels  177 us (38%)
  waiting for transfers between devices  130 us (28%)
  starting transfers between devices  57.9 us (12%)
  other arithmetic  44.3 us (9%)
  local copies, waits for them, and re-layouts  41.1 us (9%)
  between operations  14.9 us (3%)
    ppermute x45, waiting for transfers between devices, send(): return lax.ppermute(value, AXES, pairs(sizes, target))  129 us
    ppermute x45, starting transfers between devices, send(): return lax.ppermute(value, AXES, pairs(sizes, target))  57.3 us
    pallas_call x4, Pallas kernels, body(): pl.pallas_call(back_kernel, name='back', cost_estimate=SMALL, grid=(1,),...  54.6 us
    pallas_call x1, Pallas kernels, body(): pl.pallas_call(last_reduce_kernel, name='reduce_two', cost_estimate=SMALL...  21.3 us
    pallas_call x1, Pallas kernels, body(): pl.pallas_call(first_reduce_kernel, name='reduce_one', cost_estimate=SMAL...  20 us
    pallas_call x1, Pallas kernels, body(): pl.pallas_call(expand_kernel, name='expand', grid=(hidden_width // WIDE,)...  18.1 us
    pallas_call x1, Pallas kernels, body(): pl.pallas_call(front_kernel, name='front', grid=(rows // BLOCK,), in_spec...  17.9 us
    dynamic_slice x14, local copies, waits for them, and re-layouts, half(): return lax.dynamic_slice_in_dim(value, index * rows, rows, 0)  16.3 us
  transfers between devices with their start and end apart: 47, of which 12 were waited for; matrix products, arithmetic and copies ran while one was open for 13% of the time, Pallas kernels for 29%

profile of v2, /device:TPU:0, one launch (start us, length us, event | category | flops | bytes accessed | tf_op | source)
XLA Modules:
  0.0 465.1 jit_solution(5846206072121632179)
XLA Ops:
  20.3 17.9 %front.1 = (f32[1024,768]{1,0:T(8,128)}, bf16[1024,768]{1,0:T(8,128)(2,1)}, bf16[1024,2304]{1,0:T(8,128)(2,1)}, bf16[1024,768]{1,0:T(8,128)(2,1)}, f32[1024,768]{1,0:T(8,128)}, /*index=5*/bf16[1024,768]{1,0:T(8,128)(2,1)}) custom-call(bf16[1024,768]{1,0:T(8,128)(2,1)} %tokens.1, s32[1024,1]{1,0:T(8,128)} %copy.49.place_column, ...), custom_call_target="tpu_custom_call" | custom-call | tf_op jit(solution)/shard_map/front/pallas_call | solution.py:556
  38.2 18.1 %expand.1 = (bf16[1024,3072]{1,0:T(8,128)(2,1)}, bf16[1024,3072]{1,0:T(8,128)(2,1)}, f32[3072,768]{1,0:T(8,128)}) custom-call(bf16[1024,768]{1,0:T(8,128)(2,1)} %get-tuple-element.282.second, bf16[1024,768]{1,0:T(8,128)(2,1)} %cotangent.13, bf16[768,3072]{1,0:T(8,128)(2,1)} %expand_weight.5, f32[1,3072]{1,0:T(1,128)} %bitcast.12), custom_call_target="tpu_custom_call" | custom-call | tf_op jit(solution)/shard_map/expand/pallas_call | solution.py:575
  57.5 20.0 %reduce_one.1 = (f32[1024,768]{1,0:T(8,128)}, f32[1024,768]{1,0:T(8,128)}, f32[768,1536]{1,0:T(8,128)}, f32[3,1,512]{2,1,0:T(1,128)}) custom-call(bf16[1024,768]{1,0:T(8,128)(2,1)} %get-tuple-element.282.second, bf16[1024,768]{1,0:T(8,128)(2,1)} %cotangent.13, f32[1024,768]{1,0:T(8,128)} %get-tuple-element.283.mid, ...), custom_call_target="tpu_custom_call" | custom-call | flops 1 | bytes 1 | tf_op jit(solution)/shard_map/reduce_one/pallas_call | solution.py:642
  81.4 21.3 %reduce_two.1 = (bf16[1024,768]{1,0:T(8,128)(2,1)}, f32[1024,768]{1,0:T(8,128)}, f32[768,1536]{1,0:T(8,128)}, f32[3,1,512]{2,1,0:T(1,128)}) custom-call(bf16[1024,768]{1,0:T(8,128)(2,1)} %get-tuple-element.282.second, bf16[1024,768]{1,0:T(8,128)(2,1)} %cotangent.13, f32[1024,768]{1,0:T(8,128)} %get-tuple-element.286.before_total, ...), custom_call_target="tpu_custom_call" | custom-call | flops 1 | bytes 1 | tf_op jit(solution)/shard_map/reduce_two/pallas_call | solution.py:655
  112.5 13.5 %back.4 = (bf16[1024,768]{1,0:T(8,128)(2,1)}, f32[1024,768]{1,0:T(8,128)}, bf16[1024,2304]{1,0:T(8,128)(2,1)}, bf16[1024,768]{1,0:T(8,128)(2,1)}, f32[4,8,768]{2,1,0:T(8,128)}) custom-call(f32[1024,768]{1,0:T(8,128)} %get-tuple-element.353.second_gradient, f32[1024,768]{1,0:T(8,128)} %get-tuple-element.283.mid, f32[1024,768]{1,0:T(8,128)} %get-tuple-element.307.stream, ...), custom_call_target="tpu_custom_call" | custom-call | flops 1 | bytes 1 | tf_op jit(solution)/shard_map/back/pallas_call | solution.py:688
  130.3 13.7 %back.5 = (bf16[1024,768]{1,0:T(8,128)(2,1)}, f32[1024,768]{1,0:T(8,128)}, bf16[1024,2304]{1,0:T(8,128)(2,1)}, bf16[1024,768]{1,0:T(8,128)(2,1)}, f32[4,8,768]{2,1,0:T(8,128)}) custom-call(f32[1024,768]{1,0:T(8,128)} %get-tuple-element.353.second_gradient, ...), custom_call_target="tpu_custom_call", output_to_operand_aliasing={{0}: (11, {}), {1}: (12, {}), {2}: (13, {}), {3}: (14, {}),... | custom-call | flops 1 | bytes 1 | tf_op jit(solution)/shard_map/back/pallas_call | solution.py:688
  146.7 13.5 %back.6 = (bf16[1024,768]{1,0:T(8,128)(2,1)}, f32[1024,768]{1,0:T(8,128)}, bf16[1024,2304]{1,0:T(8,128)(2,1)}, bf16[1024,768]{1,0:T(8,128)(2,1)}, f32[4,8,768]{2,1,0:T(8,128)}) custom-call(f32[1024,768]{1,0:T(8,128)} %get-tuple-element.353.second_gradient, ...), custom_call_target="tpu_custom_call", output_to_operand_aliasing={{0}: (11, {}), {1}: (12, {}), {2}: (13, {}), {3}: (14, {}),... | custom-call | flops 1 | bytes 1 | tf_op jit(solution)/shard_map/back/pallas_call | solution.py:688
  165.1 13.9 %back.7 = (bf16[1024,768]{1,0:T(8,128)(2,1)}, f32[1024,768]{1,0:T(8,128)}, bf16[1024,2304]{1,0:T(8,128)(2,1)}, bf16[1024,768]{1,0:T(8,128)(2,1)}, f32[4,8,768]{2,1,0:T(8,128)}) custom-call(f32[1024,768]{1,0:T(8,128)} %get-tuple-element.353.second_gradient, ...), custom_call_target="tpu_custom_call", output_to_operand_aliasing={{0}: (11, {}), {1}: (12, {}), {2}: (13, {}), {3}: (14, {}),... | custom-call | flops 1 | bytes 1 | tf_op jit(solution)/shard_map/back/pallas_call | solution.py:688
  184.9 10.0 %project.1 = f32[768,2304]{1,0:T(8,128)} custom-call(bf16[1024,768]{1,0:T(8,128)(2,1)} %get-tuple-element.368.first, bf16[1024,2304]{1,0:T(8,128)(2,1)} %get-tuple-element.379.pieces), custom_call_target="tpu_custom_call" | custom-call | flops 1 | bytes 1 | tf_op jit(solution)/shard_map/project/pallas_call | solution.py:730
  207.5 8.4 %mixed.1 = f32[1472,768]{1,0:T(8,128)} custom-call(bf16[1024,768]{1,0:T(8,128)(2,1)} %get-tuple-element.366.heads, bf16[1024,768]{1,0:T(8,128)(2,1)} %get-tuple-element.385.branch, f32[1024,768]{1,0:T(8,128)} %get-tuple-element.386.in_gradient, s32[1,1024]{1,0:T(1,128)} %bitcast.14, f32[4,8,768]{2,1,0:T(8,128)} %get-tuple-element.387.sums, ...), custom_call_target="tpu_custom_call" | custom-call | flops 1 | bytes 1 | tf_op jit(solution)/shard_map/mixed/pallas_call | solution.py:749
  235.8 14.1 %collective-permute-done.11 = f32[96,1536]{1,0:T(8,128)} collective-permute-done((f32[96,1536]{1,0:T(8,128)S(1)}, f32[96,1536]{1,0:T(8,128)}, u32[]{:S(2)}, u32[]{:S(2)}) %collective-permute-start.11) | collective-permute-done | bytes 589856 | tf_op jit(solution)/shard_map/ppermute | solution.py:45
  259.8 23.7 %collective-permute-done.10 = f32[368,768]{1,0:T(8,128)S(1)} collective-permute-done((f32[368,768]{1,0:T(8,128)S(1)}, f32[368,768]{1,0:T(8,128)S(1)}, u32[]{:S(2)}, u32[]{:S(2)}) %collective-permute-start.10) | collective-permute-done | bytes 1130528 | tf_op jit(solution)/shard_map/ppermute | solution.py:45
  294.4 19.4 %collective-permute-done.17 = f32[96,1536]{1,0:T(8,128)S(1)} collective-permute-done((f32[96,1536]{1,0:T(8,128)S(1)}, f32[96,1536]{1,0:T(8,128)S(1)}, u32[]{:S(2)}, u32[]{:S(2)}) %collective-permute-start.17) | collective-permute-done | bytes 589856 | tf_op jit(solution)/shard_map/ppermute | solution.py:45
  314.1 15.0 %collective-permute-done.22 = f32[96,1152]{1,0:T(8,128)S(1)} collective-permute-done((f32[96,1152]{1,0:T(8,128)S(1)}, f32[96,1152]{1,0:T(8,128)S(1)}, u32[]{:S(2)}, u32[]{:S(2)}) %collective-permute-start.22) | collective-permute-done | bytes 442400 | tf_op jit(solution)/shard_map/ppermute | solution.py:45
  334.7 5.7 %collective-permute-start.21 = (f32[184,768]{1,0:T(8,128)S(1)}, f32[184,768]{1,0:T(8,128)}, u32[]{:S(2)}, u32[]{:S(2)}) collective-permute-start(f32[184,768]{1,0:T(8,128)S(1)} %dynamic-slice_add_fusion.12), channel_id=1, source_target_pairs={{0,8},{1,9},{2,10},{3,11},{4,12},{5,13},{6,14},{7,15},{24,16},{25,... | collective-permute-start | bytes 1695752 | tf_op jit(solution)/shard_map/ppermute | solution.py:45
  346.5 7.7 %copied.1 = f32[3072,768]{1,0:T(8,128)} custom-call(f32[3072,768]{1,0:T(8,128)} %all-gather.2.cloned.1.call-done.source), custom_call_target="tpu_custom_call" | custom-call | tf_op jit(solution)/shard_map/copied/pallas_call | solution.py:185
  363.3 7.4 %collective-permute-done.31 = f32[96,1152]{1,0:T(8,128)S(1)} collective-permute-done((f32[96,1152]{1,0:T(8,128)S(1)}, f32[96,1152]{1,0:T(8,128)S(1)}, u32[]{:S(2)}, u32[]{:S(2)}) %collective-permute-start.31) | collective-permute-done | bytes 442400 | tf_op jit(solution)/shard_map/ppermute | solution.py:45
  371.4 7.5 %collective-permute-done.35 = f32[96,1152]{1,0:T(8,128)S(1)} collective-permute-done((f32[96,1152]{1,0:T(8,128)S(1)}, f32[96,1152]{1,0:T(8,128)S(1)}, u32[]{:S(2)}, u32[]{:S(2)}) %collective-permute-start.35) | collective-permute-done | bytes 442400 | tf_op jit(solution)/shard_map/ppermute | solution.py:45
  381.2 6.1 %collective-permute-done.42 = f32[96,1152]{1,0:T(8,128)S(1)} collective-permute-done((f32[96,1152]{1,0:T(8,128)S(1)}, f32[96,1152]{1,0:T(8,128)S(1)}, u32[]{:S(2)}, u32[]{:S(2)}) %collective-permute-start.42) | collective-permute-done | bytes 442400 | tf_op jit(solution)/shard_map/ppermute | solution.py:45
  389.7 4.9 %collective-permute-done.33 = f32[184,768]{1,0:T(8,128)S(1)} collective-permute-done((f32[184,768]{1,0:T(8,128)S(1)}, f32[184,768]{1,0:T(8,128)S(1)}, u32[]{:S(2)}, u32[]{:S(2)}) %collective-permute-start.33) | collective-permute-done | bytes 565280 | tf_op jit(solution)/shard_map/ppermute | solution.py:45
  397.8 12.5 %collective-permute-done.37 = f32[184,768]{1,0:T(8,128)S(1)} collective-permute-done((f32[184,768]{1,0:T(8,128)S(1)}, f32[184,768]{1,0:T(8,128)S(1)}, u32[]{:S(2)}, u32[]{:S(2)}) %collective-permute-start.37) | collective-permute-done | bytes 565280 | tf_op jit(solution)/shard_map/ppermute | solution.py:45
  416.5 11.9 %collective-permute-done.38 = f32[368,768]{1,0:T(8,128)S(1)} collective-permute-done((f32[368,768]{1,0:T(8,128)S(1)}, f32[368,768]{1,0:T(8,128)S(1)}, u32[]{:S(2)}, u32[]{:S(2)}) %collective-permute-start.38) | collective-permute-done | bytes 1130528 | tf_op jit(solution)/shard_map/ppermute | solution.py:45
  435.4 8.1 %assemble.2 = f32[768,3072]{1,0:T(8,128)} custom-call(s32[1]{0:T(128)} %bitcast.5.where, f32[384,1536]{1,0:T(8,128)} %copy-done.3, f32[384,1536]{1,0:T(8,128)} %copy-done.4, f32[384,1536]{1,0:T(8,128)} %copy-done.15, f32[384,1536]{1,0:T(8,128)} %copy-done.14), custom_call_target="tpu_custom_call" | custom-call | tf_op jit(solution)/shard_map/assemble/pallas_call | solution.py:165
  443.5 6.7 %assemble.3 = f32[768,2304]{1,0:T(8,128)} custom-call(s32[1]{0:T(128)} %bitcast.5.where, f32[384,1152]{1,0:T(8,128)} %pad_maximum_fusion.3.refs_0_, f32[384,1152]{1,0:T(8,128)} %pad_maximum_fusion.4.refs_1_, f32[384,1152]{1,0:T(8,128)} %collective-permute-done.41.refs_2_, f32[384,1152]{1,0:T(8,128)} %collective-permute-done.44.refs_3_), custom_call_target="tpu_custom_call" | custom-call | tf_op jit(solution)/shard_map/assemble/pallas_call | solution.py:165
  (210 shorter events, 149.2 us)
Async XLA Ops:
  7.2 221.1 %reduce-scatter.2.cloned.1.call-start = ((), (), s32[]{:S(2)}) async-start(), calls=%async_computation.1 | async-start | bytes 9732096 | tf_op jit(solution)/shard_map/reduce_scatter | solution.py:599
  56.3 290.2 %all-gather.2.cloned.1.call-start = ((), (), s32[]{:S(2)}) async-start(), calls=%async_computation.2 | async-start | bytes 9732096 | tf_op jit(solution)/shard_map/all_gather | solution.py:609
  80.9 25.1 %collective-permute-start.1 = (f32[384,1536]{1,0:T(8,128)}, f32[384,1536]{1,0:T(8,128)S(1)}, u32[]{:S(2)}, u32[]{:S(2)}) collective-permute-start(f32[384,1536]{1,0:T(8,128)} %constant_dynamic-slice_fusion.14), channel_id=1, source_target_pairs={{0,2},{1,3},{2,0},{3,1},{4,6},{5,7},{6,4},{7,5},{8,10},{9,11},{10,... | collective-permute-start | bytes 7077896 | tf_op jit(solution)/shard_map/ppermute | solution.py:45
  109.5 34.5 %collective-permute-start.3 = (f32[192,1536]{1,0:T(8,128)S(1)}, f32[192,1536]{1,0:T(8,128)}, u32[]{:S(2)}, u32[]{:S(2)}) collective-permute-start(f32[192,1536]{1,0:T(8,128)S(1)} %constant_dynamic-slice_fusion.12), channel_id=1, source_target_pairs={{0,1},{1,0},{2,6},{3,7},{4,5},{5,4},{6,2},{7,3},{8,9},{9,8},{10,14... | collective-permute-start | bytes 3538952 | tf_op jit(solution)/shard_map/ppermute | solution.py:45
  129.9 32.1 %collective-permute-start.2 = (f32[192,1536]{1,0:T(8,128)}, f32[192,1536]{1,0:T(8,128)}, u32[]{:S(2)}, u32[]{:S(2)}) collective-permute-start(f32[192,1536]{1,0:T(8,128)} %constant_dynamic-slice_fusion.11), channel_id=1, source_target_pairs={{0,1},{1,0},{2,6},{3,7},{4,5},{5,4},{6,2},{7,3},{8,9},{9,8},{10,14... | collective-permute-start | bytes 3538952 | tf_op jit(solution)/shard_map/ppermute | solution.py:45
  201.4 23.0 %collective-permute-start.7 = (f32[384,1152]{1,0:T(8,128)}, f32[384,1152]{1,0:T(8,128)}, u32[]{:S(2)}, u32[]{:S(2)}) collective-permute-start(f32[384,1152]{1,0:T(8,128)} %get-tuple-element.395), channel_id=1, source_target_pairs={{0,2},{1,3},{2,0},{3,1},{4,6},{5,7},{6,4},{7,5},{8,10},{9,11},{10,... | collective-permute-start | bytes 5308424 | tf_op jit(solution)/shard_map/ppermute | solution.py:45
  228.4 22.6 %collective-permute-start.15 = (f32[192,1152]{1,0:T(8,128)}, f32[192,1152]{1,0:T(8,128)}, u32[]{:S(2)}, u32[]{:S(2)}) collective-permute-start(f32[192,1152]{1,0:T(8,128)} %constant_dynamic-slice_fusion.5), channel_id=1, source_target_pairs={{0,1},{1,0},{2,6},{3,7},{4,5},{5,4},{6,2},{7,3},{8,9},{9,8},{10,14... | collective-permute-start | bytes 2654216 | tf_op jit(solution)/shard_map/ppermute | solution.py:45
  251.0 32.5 %collective-permute-start.10 = (f32[368,768]{1,0:T(8,128)S(1)}, f32[368,768]{1,0:T(8,128)S(1)}, u32[]{:S(2)}, u32[]{:S(2)}) collective-permute-start(f32[368,768]{1,0:T(8,128)S(1)} %constant_dynamic-slice_fusion.3), channel_id=1, source_target_pairs={{0,1},{1,0},{2,6},{3,7},{4,5},{5,4},{6,2},{7,3},{8,9},{9,8},{10,14... | collective-permute-start | bytes 3391496 | tf_op jit(solution)/shard_map/ppermute | solution.py:45
  254.0 29.8 %collective-permute-start.20 = (f32[96,1536]{1,0:T(8,128)S(1)}, f32[96,1536]{1,0:T(8,128)S(1)}, u32[]{:S(2)}, u32[]{:S(2)}) collective-permute-start(f32[96,1536]{1,0:T(8,128)S(1)} %add.169), channel_id=1, source_target_pairs={{8,0},{9,1},{10,2},{11,3},{12,4},{13,5},{14,6},{15,7},{16,24},{17,... | collective-permute-start | bytes 1769480 | tf_op jit(solution)/shard_map/ppermute | solution.py:45
  256.3 27.7 %collective-permute-start.18 = (f32[96,1152]{1,0:T(8,128)S(1)}, f32[96,1152]{1,0:T(8,128)S(1)}, u32[]{:S(2)}, u32[]{:S(2)}) collective-permute-start(f32[96,1152]{1,0:T(8,128)S(1)} %constant_dynamic-slice_fusion.1), channel_id=1, source_target_pairs={{0,4},{1,5},{2,3},{3,2},{4,0},{5,1},{6,7},{7,6},{8,12},{9,13},{10,... | collective-permute-start | bytes 1327112 | tf_op jit(solution)/shard_map/ppermute | solution.py:45
  257.4 26.5 %collective-permute-start.19 = (f32[96,1152]{1,0:T(8,128)S(1)}, f32[96,1152]{1,0:T(8,128)S(1)}, u32[]{:S(2)}, u32[]{:S(2)}) collective-permute-start(f32[96,1152]{1,0:T(8,128)S(1)} %constant_dynamic-slice_fusion.2), channel_id=1, source_target_pairs={{0,4},{1,5},{2,3},{3,2},{4,0},{5,1},{6,7},{7,6},{8,12},{9,13},{10,... | collective-permute-start | bytes 1327112 | tf_op jit(solution)/shard_map/ppermute | solution.py:45
  258.5 55.3 %collective-permute-start.17 = (f32[96,1536]{1,0:T(8,128)S(1)}, f32[96,1536]{1,0:T(8,128)S(1)}, u32[]{:S(2)}, u32[]{:S(2)}) collective-permute-start(f32[96,1536]{1,0:T(8,128)S(1)} %add.171), channel_id=1, source_target_pairs={{8,0},{9,1},{10,2},{11,3},{12,4},{13,5},{14,6},{15,7},{16,24},{17,... | collective-permute-start | bytes 1769480 | tf_op jit(solution)/shard_map/ppermute | solution.py:45
  284.0 30.0 %collective-permute-start.16 = (f32[184,768]{1,0:T(8,128)S(1)}, f32[184,768]{1,0:T(8,128)S(1)}, u32[]{:S(2)}, u32[]{:S(2)}) collective-permute-start(f32[184,768]{1,0:T(8,128)S(1)} %constant_dynamic-slice_fusion), channel_id=1, source_target_pairs={{0,4},{1,5},{2,3},{3,2},{4,0},{5,1},{6,7},{7,6},{8,12},{9,13},{10,... | collective-permute-start | bytes 1695752 | tf_op jit(solution)/shard_map/ppermute | solution.py:45
  286.7 53.7 %collective-permute-start.25 = (f32[96,1152]{1,0:T(8,128)S(1)}, f32[96,1152]{1,0:T(8,128)}, u32[]{:S(2)}, u32[]{:S(2)}) collective-permute-start(f32[96,1152]{1,0:T(8,128)S(1)} %dynamic-slice_add_fusion.14), channel_id=1, source_target_pairs={{0,8},{1,9},{2,10},{3,11},{4,12},{5,13},{6,14},{7,15},{24,16},{25,... | collective-permute-start | bytes 1327112 | tf_op jit(solution)/shard_map/ppermute | solution.py:45
  291.0 38.1 %collective-permute-start.22 = (f32[96,1152]{1,0:T(8,128)S(1)}, f32[96,1152]{1,0:T(8,128)S(1)}, u32[]{:S(2)}, u32[]{:S(2)}) collective-permute-start(f32[96,1152]{1,0:T(8,128)S(1)} %dynamic-slice_add_fusion.13), channel_id=1, source_target_pairs={{0,8},{1,9},{2,10},{3,11},{4,12},{5,13},{6,14},{7,15},{24,16},{25,... | collective-permute-start | bytes 1327112 | tf_op jit(solution)/shard_map/ppermute | solution.py:45
  292.3 37.6 %collective-permute-start.26 = (f32[96,1536]{1,0:T(8,128)S(1)}, f32[96,1536]{1,0:T(8,128)S(1)}, u32[]{:S(2)}, u32[]{:S(2)}) collective-permute-start(f32[96,1536]{1,0:T(8,128)S(1)} %broadcast_select_fusion.15), channel_id=1, source_target_pairs={{0,4},{1,5},{2,3},{3,2},{4,0},{5,1},{6,7},{7,6},{8,12},{9,13},{10,... | collective-permute-start | bytes 1769480 | tf_op jit(solution)/shard_map/ppermute | solution.py:45
  313.9 29.8 %collective-permute-start.24 = (f32[96,1536]{1,0:T(8,128)S(1)}, f32[96,1536]{1,0:T(8,128)}, u32[]{:S(2)}, u32[]{:S(2)}) collective-permute-start(f32[96,1536]{1,0:T(8,128)S(1)} %broadcast_select_fusion.14), channel_id=1, source_target_pairs={{0,4},{1,5},{2,3},{3,2},{4,0},{5,1},{6,7},{7,6},{8,12},{9,13},{10,... | collective-permute-start | bytes 1769480 | tf_op jit(solution)/shard_map/ppermute | solution.py:45
  331.1 27.4 %collective-permute-start.28 = (f32[192,1536]{1,0:T(8,128)}, f32[192,1536]{1,0:T(8,128)}, u32[]{:S(2)}, u32[]{:S(2)}) collective-permute-start(f32[192,1536]{1,0:T(8,128)} %pad_maximum_fusion.5), channel_id=1, source_target_pairs={{0,1},{1,0},{2,6},{3,7},{4,5},{5,4},{6,2},{7,3},{8,9},{9,8},{10,14... | collective-permute-start | bytes 3538952 | tf_op jit(solution)/shard_map/ppermute | solution.py:45
  346.0 33.6 %collective-permute-start.30 = (f32[192,1536]{1,0:T(8,128)}, f32[192,1536]{1,0:T(8,128)}, u32[]{:S(2)}, u32[]{:S(2)}) collective-permute-start(f32[192,1536]{1,0:T(8,128)} %pad_maximum_fusion.6), channel_id=1, source_target_pairs={{0,1},{1,0},{2,6},{3,7},{4,5},{5,4},{6,2},{7,3},{8,9},{9,8},{10,14... | collective-permute-start | bytes 3538952 | tf_op jit(solution)/shard_map/ppermute | solution.py:45
  357.8 21.8 %collective-permute-start.27 = (f32[184,768]{1,0:T(8,128)S(1)}, f32[184,768]{1,0:T(8,128)S(1)}, u32[]{:S(2)}, u32[]{:S(2)}) collective-permute-start(f32[184,768]{1,0:T(8,128)S(1)} %add.181), channel_id=1, source_target_pairs={{8,16},{9,17},{10,18},{11,19},{12,20},{13,21},{14,22},{15,23},{16,... | collective-permute-start | bytes 1695752 | tf_op jit(solution)/shard_map/ppermute | solution.py:45
  387.6 24.8 %collective-permute-start.40 = (f32[192,1152]{1,0:T(8,128)S(1)}, f32[192,1152]{1,0:T(8,128)S(1)}, u32[]{:S(2)}, u32[]{:S(2)}) collective-permute-start(f32[192,1152]{1,0:T(8,128)S(1)} %pad_maximum_fusion.8), channel_id=1, source_target_pairs={{0,1},{1,0},{2,6},{3,7},{4,5},{5,4},{6,2},{7,3},{8,9},{9,8},{10,14... | collective-permute-start | bytes 2654216 | tf_op jit(solution)/shard_map/ppermute | solution.py:45
  387.7 28.6 %collective-permute-start.43 = (f32[192,1152]{1,0:T(8,128)S(1)}, f32[192,1152]{1,0:T(8,128)S(1)}, u32[]{:S(2)}, u32[]{:S(2)}) collective-permute-start(f32[192,1152]{1,0:T(8,128)S(1)} %pad_maximum_fusion.9), channel_id=1, source_target_pairs={{0,1},{1,0},{2,6},{3,7},{4,5},{5,4},{6,2},{7,3},{8,9},{9,8},{10,14... | collective-permute-start | bytes 2654216 | tf_op jit(solution)/shard_map/ppermute | solution.py:45
  396.4 36.9 %collective-permute-start.34 = (f32[384,1536]{1,0:T(8,128)S(1)}, f32[384,1536]{1,0:T(8,128)S(1)}, u32[]{:S(2)}, u32[]{:S(2)}) collective-permute-start(f32[384,1536]{1,0:T(8,128)S(1)} %pad_maximum_fusion.1.refs_1_), channel_id=1, source_target_pairs={{0,2},{1,3},{2,0},{3,1},{4,6},{5,7},{6,4},{7,5},{8,10},{9,11},{10,... | collective-permute-start | bytes 7077896 | tf_op jit(solution)/shard_map/ppermute | solution.py:45
  397.8 35.5 %collective-permute-start.29 = (f32[384,1536]{1,0:T(8,128)S(1)}, f32[384,1536]{1,0:T(8,128)S(1)}, u32[]{:S(2)}, u32[]{:S(2)}) collective-permute-start(f32[384,1536]{1,0:T(8,128)S(1)} %pad_maximum_fusion.refs_0_), channel_id=1, source_target_pairs={{0,2},{1,3},{2,0},{3,1},{4,6},{5,7},{6,4},{7,5},{8,10},{9,11},{10,... | collective-permute-start | bytes 7077896 | tf_op jit(solution)/shard_map/ppermute | solution.py:45
  (42 other events, 491.8 us)
Sparse Core Ops, SparseCore 0:
  56.4 147.6 reduce-scatter.1
  228.4 106.0 all-gather.1

commit v3 on v2

--- a/solution.py
+++ b/solution.py
@@ -121,6 +121,8 @@
 
     def post(self, name, step):
         value, target = step
+        if name == "m" and target is across_core and "ab" in self.results:
+            value = after(value, self.results["ab"], self.results["w"])
         self.flying[name] = send(self.order.tie(value), self.sizes, target)
 
     def wait(self, *names):
@@ -176,6 +178,18 @@
     )(jnp.reshape(index, (1,)), *(own for own, _ in pairs), *(other for _, other in pairs))
 
 
+def after(value, *others):
+    anywhere = pl.BlockSpec(memory_space=pl.ANY)
+    return pl.pallas_call(
+        lambda *refs: None,
+        name="after",
+        in_specs=[anywhere] * (1 + len(others)),
+        out_specs=anywhere,
+        out_shape=jax.ShapeDtypeStruct(value.shape, value.dtype),
+        input_output_aliases={0: 0},
+    )(value, *others)
+
+
 def copy_kernel(source, target):
     target[...] = source[...]
 
@@ -247,26 +261,39 @@
     )
 
 
-def pair_probs(queries_two, keys_pair, same):
-    scores = jnp.where(same, mm_nt(queries_two, keys_pair), big_negative)
-    exponent = jnp.exp(scores - jnp.max(scores, axis=-1, keepdims=True))
-    return exponent * (1.0 / jnp.sum(exponent, axis=-1, keepdims=True))
+def all_probs(queries, keys, same):
+    scores = [mm_nt(q, k) for q, k in zip(queries, keys)]
+    scores = [jnp.where(same, one, big_negative) for one in scores]
+    tops = [jnp.max(one, axis=-1, keepdims=True) for one in scores]
+    exponents = [jnp.exp(one - top) for one, top in zip(scores, tops)]
+    totals = [jnp.sum(one, axis=-1, keepdims=True) for one in exponents]
+    return [one * (1.0 / total) for one, total in zip(exponents, totals)]
+
+
+def row_of(codes, which):
+    return jnp.concatenate([codes[k][which : which + 1] for k in range(codes.shape[0])], axis=1)
+
+
+def chosen_places(codes, places):
+    row = row_of(codes, 0)
+    numbers = lax.broadcasted_iota(jnp.int32, (places, row.shape[1]), 0)
+    return (numbers == row).astype(bf16)
+
+
+def same_sample(codes, g):
+    numbers = lax.broadcasted_iota(jnp.int32, (16, codes.shape[2]), 0)
+    member = (numbers == codes[g][1:2]).astype(bf16)
+    same = mm_tn(member, member)
+    return jnp.concatenate([same, same], axis=0) > 0.5
 
 
 def front_kernel(
     tokens,
-    place_column,
-    sample_column,
-    sample_row,
+    codes,
     table,
-    one_gain,
-    one_shift,
+    lines,
     project_weight,
-    joined_bias,
     output_weight,
-    output_bias,
-    two_gain,
-    two_shift,
     stream_out,
     first_out,
     projected_out,
@@ -275,34 +302,34 @@
     second_out,
 ):
     rows, width = tokens.shape
-    group = sample_row.shape[2]
+    group = codes.shape[2]
     scale = (width // HEADS) ** (-0.5)
-    places = lax.broadcasted_iota(jnp.int32, (rows, table.shape[0]), 1)
-    chosen = (places == place_column[...]).astype(bf16)
-    stream = tokens[...].astype(f32) + mm(chosen, table[...])
+    chosen = chosen_places(codes, table.shape[0])
+    stream = tokens[...].astype(f32) + mm_tn(chosen, table[...])
     stream_out[...] = stream
     normed, _ = normalize(stream)
-    first = (normed * one_gain[...] + one_shift[...]).astype(bf16)
+    first = (normed * lines[0:1] + lines[1:2]).astype(bf16)
     first_out[...] = first
-    projected_out[...] = (mm(first, project_weight[...]) + joined_bias[...]).astype(bf16)
+    joined_bias = jnp.concatenate([lines[6:7], jnp.zeros((1, width), f32), lines[7:8]], axis=1)
+    projected_out[...] = (mm(first, project_weight[...]) + joined_bias).astype(bf16)
     low_lanes = lax.broadcasted_iota(jnp.int32, (group, 128), 1) < 64
     for g in range(rows // group):
         span = slice(g * group, (g + 1) * group)
-        same = sample_column[span, :] == sample_row[g]
-        same = jnp.concatenate([same, same], axis=0)
-        for j in range(width // 128):
-            queries = projected_out[span, j * 128 : (j + 1) * 128] * bf16(scale)
-            keys = projected_out[span, width + j * 128 : width + (j + 1) * 128]
-            values = projected_out[span, 2 * width + j * 128 : 2 * width + (j + 1) * 128]
-            probs = pair_probs(two_heads(queries, low_lanes), keys, same)
-            both = mm(probs.astype(bf16), values)
-            heads_out[span, j * 128 : (j + 1) * 128] = jnp.where(
-                low_lanes, both[:group], both[group:]
+        same = same_sample(codes, g)
+        here = [slice(j * 128, (j + 1) * 128) for j in range(3 * width // 128)]
+        count = width // 128
+        columns = [projected_out[span, one] for one in here]
+        queries = [two_heads(one * bf16(scale), low_lanes) for one in columns[:count]]
+        probs = all_probs(queries, columns[count : 2 * count], same)
+        both = [mm(p.astype(bf16), v) for p, v in zip(probs, columns[2 * count :])]
+        for j in range(count):
+            heads_out[span, here[j]] = jnp.where(
+                low_lanes, both[j][:group], both[j][group:]
             ).astype(bf16)
-    mid = stream + (mm(heads_out[...], output_weight[...]) + output_bias[...])
+    mid = stream + (mm(heads_out[...], output_weight[...]) + lines[4:5])
     mid_out[...] = mid
     normed, _ = normalize(mid)
-    second_out[...] = (normed * two_gain[...] + two_shift[...]).astype(bf16)
+    second_out[...] = (normed * lines[2:3] + lines[3:4]).astype(bf16)
 
 
 def expand_kernel(
@@ -326,7 +353,7 @@
     slope,
     expand_weight,
     reduce_weight,
-    reduce_bias,
+    lines,
     total,
     second_gradient,
     expand_gradient,
@@ -346,7 +373,7 @@
     def _():
         if fresh:
             second_gradient[...] = back
-            total[...] = before_total[...] + reduce_bias[...] + ahead
+            total[...] = before_total[...] + lines[5:6] + ahead
         else:
             second_gradient[...] = before_gradient[...] + back
             total[...] = before_total[...] + ahead
@@ -358,10 +385,10 @@
 
 
 def first_reduce_kernel(
-    second, cotangent, mid, hidden, slope, expand_weight, reduce_weight, reduce_bias, *outs
+    second, cotangent, mid, hidden, slope, expand_weight, reduce_weight, lines, *outs
 ):
     reduce_kernel(
-        second, cotangent, mid, None, hidden, slope, expand_weight, reduce_weight, reduce_bias,
+        second, cotangent, mid, None, hidden, slope, expand_weight, reduce_weight, lines,
         *outs, fresh=True,
     )
 
@@ -387,24 +414,22 @@
     stream,
     cotangent,
     projected,
-    sample_column,
-    sample_row,
-    one_gain,
-    two_gain,
+    codes,
+    lines,
     output_weight,
     project_weight,
     *rest,
 ):
     token_gradient, in_gradient_out, pieces, branch_out, sums = rest[-5:]
     rows, width = stream.shape
-    group = sample_row.shape[2]
+    group = codes.shape[2]
     scale = (width // HEADS) ** (-0.5)
     upstream = second_gradient[...]
     out_gradient = cotangent[...].astype(f32)
     normed, inverse = normalize(mid[...])
     two_gain_gradient = column_sum(upstream * normed)
     two_shift_gradient = column_sum(upstream)
-    mid_gradient = out_gradient + norm_backward(upstream, normed, inverse, two_gain[...])
+    mid_gradient = out_gradient + norm_backward(upstream, normed, inverse, lines[2:3])
     branch = mid_gradient.astype(bf16)
     branch_out[...] = branch
     bias_gradient = column_sum(branch.astype(f32))
@@ -412,29 +437,30 @@
     low_lanes = lax.broadcasted_iota(jnp.int32, (group, 128), 1) < 64
     for g in range(rows // group):
         span = slice(g * group, (g + 1) * group)
-        same = sample_column[span, :] == sample_row[g]
-        same = jnp.concatenate([same, same], axis=0)
-        for j in range(width // 128):
-            here = [
-                slice(k * width + j * 128, k * width + (j + 1) * 128) for k in range(3)
-            ]
-            queries = two_heads(projected[span, here[0]] * bf16(scale), low_lanes)
-            keys = projected[span, here[1]]
-            values = projected[span, here[2]]
-            upper = two_heads(heads_gradient[span, here[0]], low_lanes)
-            probs = pair_probs(queries, keys, same)
-            weight_gradient = mm_nt(upper, values)
-            inner = jnp.sum(weight_gradient * probs, axis=-1, keepdims=True)
-            score_gradient = (probs * (weight_gradient - inner)).astype(bf16)
-            both = mm(score_gradient, keys)
-            pieces[span, here[0]] = (
+        same = same_sample(codes, g)
+        here = [slice(j * 128, (j + 1) * 128) for j in range(3 * width // 128)]
+        count = width // 128
+        columns = [projected[span, one] for one in here]
+        queries = [two_heads(one * bf16(scale), low_lanes) for one in columns[:count]]
+        keys, values = columns[count : 2 * count], columns[2 * count :]
+        uppers = [two_heads(heads_gradient[span, one], low_lanes) for one in here[:count]]
+        probs = all_probs(queries, keys, same)
+        weights = [mm_nt(upper, v) for upper, v in zip(uppers, values)]
+        inner = [jnp.sum(w * p, axis=-1, keepdims=True) for w, p in zip(weights, probs)]
+        scores = [(p * (w - n)).astype(bf16) for p, w, n in zip(probs, weights, inner)]
+        for_queries = [mm(one, k) for one, k in zip(scores, keys)]
+        for_keys = [mm_tn(one, q) for one, q in zip(scores, queries)]
+        for_values = [mm_tn(p.astype(bf16), upper) for p, upper in zip(probs, uppers)]
+        for j in range(count):
+            both = for_queries[j]
+            pieces[span, here[j]] = (
                 jnp.where(low_lanes, both[:group], both[group:]) * scale
             ).astype(bf16)
-            pieces[span, here[1]] = mm_tn(score_gradient, queries).astype(bf16)
-            pieces[span, here[2]] = mm_tn(probs.astype(bf16), upper).astype(bf16)
+            pieces[span, here[count + j]] = for_keys[j].astype(bf16)
+            pieces[span, here[2 * count + j]] = for_values[j].astype(bf16)
     upstream = mm_nt(pieces[...], project_weight[...])
     normed, inverse = normalize(stream[...])
-    in_gradient = mid_gradient + norm_backward(upstream, normed, inverse, one_gain[...])
+    in_gradient = mid_gradient + norm_backward(upstream, normed, inverse, lines[0:1])
     in_gradient_out[...] = in_gradient
     token_gradient[...] = in_gradient.astype(bf16)
     sums[0] = jnp.concatenate(
@@ -452,12 +478,14 @@
     )
 
 
-def project_kernel(first, pieces, project_gradient):
+def project_kernel(first, pieces, *rest):
+    project_gradient = rest[-1]
     project_gradient[...] = mm_tn(first[...], pieces[...])
 
 
-def mixed_kernel(heads, branch, in_gradient, place_row, sums, expand_bias_gradient, mixed):
-    rows, width = heads.shape
+def mixed_kernel(heads, branch, in_gradient, codes, sums, expand_bias_gradient, *rest):
+    mixed = rest[-1]
+    width = heads.shape[1]
     top = mixed.shape[0] // 2
     heads_half = width // 2
     place_half = top - heads_half - 32
@@ -466,8 +494,7 @@
     mixed[top : top + heads_half, :] = both[heads_half:]
     high = in_gradient[...].astype(bf16)
     low = (in_gradient[...] - high.astype(f32)).astype(bf16)
-    numbers = lax.broadcasted_iota(jnp.int32, (2 * place_half, rows), 0)
-    chosen = (numbers == place_row[...]).astype(bf16)
+    chosen = chosen_places(codes, 2 * place_half)
     both = mm(chosen, high) + mm(chosen, low)
     mixed[heads_half : heads_half + place_half, :] = both[:place_half]
     mixed[top + heads_half : top + heads_half + place_half, :] = both[place_half:]
@@ -478,6 +505,13 @@
         total = total + sums[k]
     mixed[top - 32 : top - 24, :] = total
     mixed[top - 24 : top - 20, :] = expand_bias_gradient[...]
+
+
+def lines_kernel(*refs):
+    *vectors, last, lines, bias_row = refs
+    for k, vector in enumerate(vectors):
+        lines[k : k + 1, :] = vector[...].astype(f32).reshape(1, -1)
+    bias_row[...] = last[...].astype(f32).reshape(1, -1)
 
 
 def whole(array):
@@ -524,16 +558,25 @@
     fine_grid = resolution[:, None] == 1
     place = jnp.where(fine_grid, PATCH_LO + kept_patches, kept_patches % PATCH_LO)
     sample = jnp.where(fine_grid, 0, kept_patches // PATCH_LO)
-    place_column = place.reshape(rows, 1)
-    place_row = place.reshape(1, rows)
-    sample_column = sample.reshape(rows, 1)
-    sample_row = sample.reshape(groups, 1, group_rows)
-
-    def line(vector):
-        return vector.astype(f32).reshape(1, -1)
-
-    one_gain, two_gain = line(norm_one_gain), line(norm_two_gain)
-    joined_bias = line(jnp.concatenate([query_bias, jnp.zeros_like(query_bias), value_bias]))
+    codes = jnp.stack([place, sample], axis=1)
+    vectors = (
+        norm_one_gain,
+        norm_one_shift,
+        norm_two_gain,
+        norm_two_shift,
+        output_bias,
+        reduce_bias,
+        query_bias,
+        value_bias,
+        expand_bias,
+    )
+    lines, bias_row = pl.pallas_call(
+        lines_kernel,
+        name="lines",
+        in_specs=[pl.BlockSpec(memory_space=pltpu.VMEM)] * len(vectors),
+        out_specs=[pl.BlockSpec(memory_space=pltpu.VMEM)] * 2,
+        out_shape=(shape((8, width), f32), shape((1, hidden_width), f32)),
+    )(*vectors)
     front_shapes = (
         shape((rows, width), f32),
         shape((rows, width), bf16),
@@ -542,36 +585,20 @@
         shape((rows, width), f32),
         shape((rows, width), bf16),
     )
-    fixed = (
-        position_table,
-        one_gain,
-        line(norm_one_shift),
-        project_weight,
-        joined_bias,
-        output_weight,
-        line(output_bias),
-        two_gain,
-        line(norm_two_shift),
-    )
+    fixed = (position_table, lines, project_weight, output_weight)
     stream, first, projected, heads, mid, second = pl.pallas_call(
         front_kernel,
         name="front",
         grid=(rows // BLOCK,),
-        in_specs=[
-            row_block(tokens),
-            row_block(place_column),
-            row_block(sample_column),
-            lead_block(sample_row, per_step),
-        ]
+        in_specs=[row_block(tokens), lead_block(codes, per_step)]
         + [whole(array) for array in fixed],
         out_specs=[row_block(array) for array in front_shapes],
         out_shape=front_shapes,
-    )(tokens, place_column, sample_column, sample_row, *fixed)
+    )(tokens, codes, *fixed)
 
     columns = pl.BlockSpec((width, WIDE), lambda i: (0, i))
     tall = pl.BlockSpec((rows, WIDE), lambda i: (0, i))
-    lines = pl.BlockSpec((WIDE, width), lambda i: (i, 0))
-    bias_row = line(expand_bias)
+    low_lines = pl.BlockSpec((WIDE, width), lambda i: (i, 0))
     hidden, slope, reduce_weight_gradient = pl.pallas_call(
         expand_kernel,
         name="expand",
@@ -582,7 +609,7 @@
             columns,
             pl.BlockSpec((1, WIDE), lambda i: (0, i)),
         ],
-        out_specs=[tall, tall, lines],
+        out_specs=[tall, tall, low_lines],
         out_shape=(
             shape((rows, hidden_width), bf16),
             shape((rows, hidden_width), bf16),
@@ -592,7 +619,7 @@
 
     sizes = tuple(lax.axis_size(axis) for axis in AXES)
     paired = sizes == (4, 2, 2, 2)
-    order = Order(place_row)
+    order = Order(codes)
     sums = Sums(sizes, order)
     reduce_weight_gradient, second = order.tie(reduce_weight_gradient, second)
     if paired:
@@ -620,7 +647,6 @@
                             assemble(lax.axis_index("c"), pairs, 0, width // 2, width // 4)
                         )
 
-    reduce_row = line(reduce_bias)
     half_steps = hidden_width // WIDE // 2
     part = hidden_width // 2
     reduce_shapes = (
@@ -644,10 +670,10 @@
         name="reduce_one",
         cost_estimate=SMALL,
         grid=(half_steps,),
-        in_specs=[whole(second), whole(cotangent), whole(mid)] + from_step(0) + [whole(reduce_row)],
+        in_specs=[whole(second), whole(cotangent), whole(mid)] + from_step(0) + [whole(lines)],
         out_specs=reduce_outs,
         out_shape=reduce_shapes,
-    )(second, cotangent, mid, hidden, slope, expand_weight, reduce_weight, reduce_row)
+    )(second, cotangent, mid, hidden, slope, expand_weight, reduce_weight, lines)
     if paired:
         sums.begin("a", plane_first([order.tie(expand_one)], sizes))
     advance()
@@ -696,27 +722,23 @@
                 some(stream),
                 some(cotangent),
                 some(projected),
-                some(sample_column),
-                lead((per_step, 1, group_rows)),
-                whole(one_gain),
-                whole(two_gain),
+                lead((per_step,) + codes.shape[1:]),
+                whole(lines),
                 whole(output_weight),
                 whole(project_weight),
             ]
             + [pl.BlockSpec(memory_space=pl.ANY)] * len(backs),
             out_specs=[some(array) for array in back_shapes[:4]] + [lead((1, 8, width))],
             out_shape=back_shapes,
-            input_output_aliases={11 + k: k for k in range(len(backs))},
+            input_output_aliases={9 + k: k for k in range(len(backs))},
         )(
             order.tie(second_gradient),
             mid,
             stream,
             cotangent,
             projected,
-            sample_column,
-            sample_row,
-            one_gain,
-            two_gain,
+            codes,
+            lines,
             output_weight,
             project_weight,
             *backs,
@@ -744,7 +766,7 @@
     heads_half, place_half = width // 2, places // 2
     top = heads_half + place_half + 32
     bias_rows = jnp.concatenate([bias_one, bias_two]).reshape(-1, width)
-    mixed_inputs = (heads, order.tie(branch), in_gradient, place_row, block_sums, bias_rows)
+    mixed_inputs = (heads, order.tie(branch), in_gradient, codes, block_sums, bias_rows)
     mixed_shape = shape((2 * top, width), f32)
     mixed = pl.pallas_call(
         mixed_kernel,

time: 471 us -> 461 us (0.979)
  Pallas kernels: 177 us -> 167 us
  local copies, waits for them, and re-layouts: 41.1 us -> 34.2 us
  waiting for transfers between devices: 130 us -> 135 us
    pallas_call x4, Pallas kernels: 54.6 us -> 41.3 us  [body(): pl.pallas_call(back_kernel, name='back', cost_estimate=SMALL, grid=(1,),...]
    reshape x8 -> x0, local copies, waits for them, and re-layouts: 8.94 us -> none  [the longest x6 6.89 us: line(): return vector.astype(f32).reshape(1, -1)]
    ppermute x45, waiting for transfers between devices: 129 us -> 135 us  [send(): return lax.ppermute(value, AXES, pairs(sizes, target))]
    unnamed x38 -> x43, local copies, waits for them, and re-layouts: 7.11 us -> 10.3 us
  transfers between devices with their start and end apart: 47 -> 47, of which waited for: 12 -> 15; matrix products, arithmetic and copies ran while one was open for 13% -> 13% of each run, Pallas kernels for 29% -> 27%
where the time goes in v3:
time: 461 us; the launch traced here: 455 us
  Pallas kernels  167 us (36%)
  waiting for transfers between devices  135 us (29%)
  starting transfers between devices  61.2 us (13%)
  other arithmetic  41.6 us (9%)
  local copies, waits for them, and re-layouts  34.2 us (7%)
  between operations  14.8 us (3%)
    ppermute x45, waiting for transfers between devices, send(): return lax.ppermute(value, AXES, pairs(sizes, target))  135 us
    ppermute x45, starting transfers between devices, send(): return lax.ppermute(value, AXES, pairs(sizes, target))  60.6 us
    pallas_call x4, Pallas kernels, body(): pl.pallas_call(back_kernel, name='back', cost_estimate=SMALL, grid=(1,),...  41.3 us
    pallas_call x1, Pallas kernels, body(): pl.pallas_call(last_reduce_kernel, name='reduce_two', cost_estimate=SMALL...  21.3 us
    pallas_call x1, Pallas kernels, body(): pl.pallas_call(first_reduce_kernel, name='reduce_one', cost_estimate=SMAL...  20 us
    pallas_call x1, Pallas kernels, body(): pl.pallas_call(front_kernel, name='front', grid=(rows // BLOCK,), in_spec...  18.9 us
    pallas_call x1, Pallas kernels, body(): pl.pallas_call(expand_kernel, name='expand', grid=(hidden_width // WIDE,)...  18.1 us
    dynamic_slice x14, local copies, waits for them, and re-layouts, half(): return lax.dynamic_slice_in_dim(value, index * rows, rows, 0)  16.3 us
  transfers between devices with their start and end apart: 47, of which 15 were waited for; matrix products, arithmetic and copies ran while one was open for 13% of the time, Pallas kernels for 27%

profile of v3, /device:TPU:0, one launch (start us, length us, event | category | flops | bytes accessed | tf_op | source)
XLA Modules:
  0.0 454.6 jit_solution(5048818753371262232)
XLA Ops:
  10.7 18.9 %front.1 = (f32[1024,768]{1,0:T(8,128)}, bf16[1024,768]{1,0:T(8,128)(2,1)}, bf16[1024,2304]{1,0:T(8,128)(2,1)}, bf16[1024,768]{1,0:T(8,128)(2,1)}, f32[1024,768]{1,0:T(8,128)}, /*index=5*/bf16[1024,768]{1,0:T(8,128)(2,1)}) custom-call(bf16[1024,768]{1,0:T(8,128)(2,1)} %tokens.1, s32[8,2,128]{2,1,0:T(2,128)} %pad_add_fusion.codes, bf16[640,768]{1,0:T(8,128)(2,1)} %table.1, ...), custom_call_target="tpu_custom_call" | custom-call | tf_op jit(solution)/shard_map/front/pallas_call | solution.py:589
  29.6 18.1 %expand.1 = (bf16[1024,3072]{1,0:T(8,128)(2,1)}, bf16[1024,3072]{1,0:T(8,128)(2,1)}, f32[3072,768]{1,0:T(8,128)}) custom-call(bf16[1024,768]{1,0:T(8,128)(2,1)} %get-tuple-element.286.second, bf16[1024,768]{1,0:T(8,128)(2,1)} %cotangent.13, bf16[768,3072]{1,0:T(8,128)(2,1)} %expand_weight.5, f32[1,3072]{1,0:T(1,128)} %get-tuple-element.284.expand_bias), custom_call_target="tpu_custom_call" | custom-call | tf_op jit(solution)/shard_map/expand/pallas_call | solution.py:602
  48.3 20.0 %reduce_one.1 = (f32[1024,768]{1,0:T(8,128)}, f32[1024,768]{1,0:T(8,128)}, f32[768,1536]{1,0:T(8,128)}, f32[3,1,512]{2,1,0:T(1,128)}) custom-call(bf16[1024,768]{1,0:T(8,128)(2,1)} %get-tuple-element.286.second, bf16[1024,768]{1,0:T(8,128)(2,1)} %cotangent.13, f32[1024,768]{1,0:T(8,128)} %get-tuple-element.287.mid, ...), custom_call_target="tpu_custom_call" | custom-call | flops 1 | bytes 1 | tf_op jit(solution)/shard_map/reduce_one/pallas_call | solution.py:668
  72.2 21.3 %reduce_two.1 = (bf16[1024,768]{1,0:T(8,128)(2,1)}, f32[1024,768]{1,0:T(8,128)}, f32[768,1536]{1,0:T(8,128)}, f32[3,1,512]{2,1,0:T(1,128)}) custom-call(bf16[1024,768]{1,0:T(8,128)(2,1)} %get-tuple-element.286.second, bf16[1024,768]{1,0:T(8,128)(2,1)} %cotangent.13, f32[1024,768]{1,0:T(8,128)} %get-tuple-element.290.before_total, ...), custom_call_target="tpu_custom_call" | custom-call | flops 1 | bytes 1 | tf_op jit(solution)/shard_map/reduce_two/pallas_call | solution.py:681
  103.3 10.1 %back.4 = (bf16[1024,768]{1,0:T(8,128)(2,1)}, f32[1024,768]{1,0:T(8,128)}, bf16[1024,2304]{1,0:T(8,128)(2,1)}, bf16[1024,768]{1,0:T(8,128)(2,1)}, f32[4,8,768]{2,1,0:T(8,128)}) custom-call(f32[1024,768]{1,0:T(8,128)} %get-tuple-element.357.second_gradient, f32[1024,768]{1,0:T(8,128)} %get-tuple-element.287.mid, f32[1024,768]{1,0:T(8,128)} %get-tuple-element.311.stream, ...), custom_call_target="tpu_custom_call" | custom-call | flops 1 | bytes 1 | tf_op jit(solution)/shard_map/back/pallas_call | solution.py:714
  118.1 10.4 %back.5 = (bf16[1024,768]{1,0:T(8,128)(2,1)}, f32[1024,768]{1,0:T(8,128)}, bf16[1024,2304]{1,0:T(8,128)(2,1)}, bf16[1024,768]{1,0:T(8,128)(2,1)}, f32[4,8,768]{2,1,0:T(8,128)}) custom-call(f32[1024,768]{1,0:T(8,128)} %get-tuple-element.357.second_gradient, ...), custom_call_target="tpu_custom_call", output_to_operand_aliasing={{0}: (9, {}), {1}: (10, {}), {2}: (11, {}), {3}: (12, {}), ... | custom-call | flops 1 | bytes 1 | tf_op jit(solution)/shard_map/back/pallas_call | solution.py:714
  131.2 10.7 %back.6 = (bf16[1024,768]{1,0:T(8,128)(2,1)}, f32[1024,768]{1,0:T(8,128)}, bf16[1024,2304]{1,0:T(8,128)(2,1)}, bf16[1024,768]{1,0:T(8,128)(2,1)}, f32[4,8,768]{2,1,0:T(8,128)}) custom-call(f32[1024,768]{1,0:T(8,128)} %get-tuple-element.357.second_gradient, ...), custom_call_target="tpu_custom_call", output_to_operand_aliasing={{0}: (9, {}), {1}: (10, {}), {2}: (11, {}), {3}: (12, {}), ... | custom-call | flops 1 | bytes 1 | tf_op jit(solution)/shard_map/back/pallas_call | solution.py:714
  143.6 5.6 %collective-permute-done.2 = f32[192,1536]{1,0:T(8,128)} collective-permute-done((f32[192,1536]{1,0:T(8,128)}, f32[192,1536]{1,0:T(8,128)}, u32[]{:S(2)}, u32[]{:S(2)}) %collective-permute-start.2) | collective-permute-done | bytes 1179680 | tf_op jit(solution)/shard_map/ppermute | solution.py:45
  153.7 10.1 %back.7 = (bf16[1024,768]{1,0:T(8,128)(2,1)}, f32[1024,768]{1,0:T(8,128)}, bf16[1024,2304]{1,0:T(8,128)(2,1)}, bf16[1024,768]{1,0:T(8,128)(2,1)}, f32[4,8,768]{2,1,0:T(8,128)}) custom-call(f32[1024,768]{1,0:T(8,128)} %get-tuple-element.357.second_gradient, ...), custom_call_target="tpu_custom_call", output_to_operand_aliasing={{0}: (9, {}), {1}: (10, {}), {2}: (11, {}), {3}: (12, {}), ... | custom-call | flops 1 | bytes 1 | tf_op jit(solution)/shard_map/back/pallas_call | solution.py:714
  170.7 10.0 %project.1 = f32[768,2304]{1,0:T(8,128)} custom-call(bf16[1024,768]{1,0:T(8,128)(2,1)} %get-tuple-element.372.first, bf16[1024,2304]{1,0:T(8,128)(2,1)} %get-tuple-element.383.pieces), custom_call_target="tpu_custom_call" | custom-call | flops 1 | bytes 1 | tf_op jit(solution)/shard_map/project/pallas_call | solution.py:752
  193.8 8.5 %mixed.1 = f32[1472,768]{1,0:T(8,128)} custom-call(bf16[1024,768]{1,0:T(8,128)(2,1)} %get-tuple-element.370.heads, bf16[1024,768]{1,0:T(8,128)(2,1)} %get-tuple-element.389.branch, f32[1024,768]{1,0:T(8,128)} %get-tuple-element.390.in_gradient, s32[8,2,128]{2,1,0:T(2,128)} %pad_add_fusion.codes, f32[4,8,768]{2,1,0:T(8,128)} %get-tuple-element.391.sums, ...), custom_call_target="tpu_custom_call" | custom-call | flops 1 | bytes 1 | tf_op jit(solution)/shard_map/mixed/pallas_call | solution.py:771
  222.1 14.3 %collective-permute-done.11 = f32[96,1536]{1,0:T(8,128)} collective-permute-done((f32[96,1536]{1,0:T(8,128)S(1)}, f32[96,1536]{1,0:T(8,128)}, u32[]{:S(2)}, u32[]{:S(2)}) %collective-permute-start.11) | collective-permute-done | bytes 589856 | tf_op jit(solution)/shard_map/ppermute | solution.py:45
  246.4 24.4 %collective-permute-done.10 = f32[368,768]{1,0:T(8,128)S(1)} collective-permute-done((f32[368,768]{1,0:T(8,128)S(1)}, f32[368,768]{1,0:T(8,128)S(1)}, u32[]{:S(2)}, u32[]{:S(2)}) %collective-permute-start.10) | collective-permute-done | bytes 1130528 | tf_op jit(solution)/shard_map/ppermute | solution.py:45
  279.4 20.1 %collective-permute-done.17 = f32[96,1536]{1,0:T(8,128)S(1)} collective-permute-done((f32[96,1536]{1,0:T(8,128)S(1)}, f32[96,1536]{1,0:T(8,128)S(1)}, u32[]{:S(2)}, u32[]{:S(2)}) %collective-permute-start.17) | collective-permute-done | bytes 589856 | tf_op jit(solution)/shard_map/ppermute | solution.py:45
  304.6 11.3 %collective-permute-done.22 = f32[96,1152]{1,0:T(8,128)S(1)} collective-permute-done((f32[96,1152]{1,0:T(8,128)S(1)}, f32[96,1152]{1,0:T(8,128)S(1)}, u32[]{:S(2)}, u32[]{:S(2)}) %collective-permute-start.22) | collective-permute-done | bytes 442400 | tf_op jit(solution)/shard_map/ppermute | solution.py:45
  323.5 6.1 %collective-permute-start.21 = (f32[184,768]{1,0:T(8,128)}, f32[184,768]{1,0:T(8,128)}, u32[]{:S(2)}, u32[]{:S(2)}) collective-permute-start(f32[184,768]{1,0:T(8,128)} %dynamic-slice_add_fusion.12), channel_id=1, source_target_pairs={{0,8},{1,9},{2,10},{3,11},{4,12},{5,13},{6,14},{7,15},{24,16},{25,... | collective-permute-start | bytes 1695752 | tf_op jit(solution)/shard_map/ppermute | solution.py:45
  331.0 5.4 %collective-permute-done.30 = f32[192,1536]{1,0:T(8,128)S(1)} collective-permute-done((f32[192,1536]{1,0:T(8,128)}, f32[192,1536]{1,0:T(8,128)S(1)}, u32[]{:S(2)}, u32[]{:S(2)}) %collective-permute-start.30) | collective-permute-done | bytes 1179680 | tf_op jit(solution)/shard_map/ppermute | solution.py:45
  336.9 8.4 %copied.1.refs_2_ = f32[3072,768]{1,0:T(8,128)} custom-call(f32[3072,768]{1,0:T(8,128)} %all-gather.2.cloned.1.call-done.source), custom_call_target="tpu_custom_call" | custom-call | tf_op jit(solution)/shard_map/copied/pallas_call | solution.py:199
  354.7 8.0 %collective-permute-done.31 = f32[96,1152]{1,0:T(8,128)S(1)} collective-permute-done((f32[96,1152]{1,0:T(8,128)S(1)}, f32[96,1152]{1,0:T(8,128)S(1)}, u32[]{:S(2)}, u32[]{:S(2)}) %collective-permute-start.31) | collective-permute-done | bytes 442400 | tf_op jit(solution)/shard_map/ppermute | solution.py:45
  363.7 7.4 %collective-permute-done.35 = f32[96,1152]{1,0:T(8,128)S(1)} collective-permute-done((f32[96,1152]{1,0:T(8,128)S(1)}, f32[96,1152]{1,0:T(8,128)S(1)}, u32[]{:S(2)}, u32[]{:S(2)}) %collective-permute-start.35) | collective-permute-done | bytes 442400 | tf_op jit(solution)/shard_map/ppermute | solution.py:45
  375.2 8.3 %collective-permute-done.42 = f32[96,1152]{1,0:T(8,128)S(1)} collective-permute-done((f32[96,1152]{1,0:T(8,128)S(1)}, f32[96,1152]{1,0:T(8,128)S(1)}, u32[]{:S(2)}, u32[]{:S(2)}) %collective-permute-start.42) | collective-permute-done | bytes 442400 | tf_op jit(solution)/shard_map/ppermute | solution.py:45
  389.8 13.8 %collective-permute-done.37 = f32[184,768]{1,0:T(8,128)S(1)} collective-permute-done((f32[184,768]{1,0:T(8,128)S(1)}, f32[184,768]{1,0:T(8,128)S(1)}, u32[]{:S(2)}, u32[]{:S(2)}) %collective-permute-start.37) | collective-permute-done | bytes 565280 | tf_op jit(solution)/shard_map/ppermute | solution.py:45
  409.5 8.1 %assemble.2.refs_1_ = f32[768,3072]{1,0:T(8,128)} custom-call(s32[1]{0:T(128)} %bitcast.3.where, f32[384,1536]{1,0:T(8,128)} %copy-done.5, f32[384,1536]{1,0:T(8,128)} %copy-done.4, f32[384,1536]{1,0:T(8,128)} %copy-done.19, f32[384,1536]{1,0:T(8,128)} %collective-permute-done.34.refs_3_), custom_call_target="tpu_custom_call" | custom-call | tf_op jit(solution)/shard_map/assemble/pallas_call | solution.py:167
  432.9 6.7 %assemble.3 = f32[768,2304]{1,0:T(8,128)} custom-call(s32[1]{0:T(128)} %bitcast.3.where, f32[384,1152]{1,0:T(8,128)} %copy-done.11, f32[384,1152]{1,0:T(8,128)} %copy-done.10, f32[384,1152]{1,0:T(8,128)} %collective-permute-done.41.refs_2_, f32[384,1152]{1,0:T(8,128)} %copy-done.20), custom_call_target="tpu_custom_call" | custom-call | tf_op jit(solution)/shard_map/assemble/pallas_call | solution.py:167
  (204 shorter events, 153.6 us)
Async XLA Ops:
  7.2 207.5 %reduce-scatter.2.cloned.1.call-start = ((), (), s32[]{:S(2)}) async-start(), calls=%async_computation.1 | async-start | bytes 9732096 | tf_op jit(solution)/shard_map/reduce_scatter | solution.py:626
  47.8 289.1 %all-gather.2.cloned.1.call-start = ((), (), s32[]{:S(2)}) async-start(), calls=%async_computation.2 | async-start | bytes 9732096 | tf_op jit(solution)/shard_map/all_gather | solution.py:636
  71.7 25.1 %collective-permute-start.1 = (f32[384,1536]{1,0:T(8,128)}, f32[384,1536]{1,0:T(8,128)S(1)}, u32[]{:S(2)}, u32[]{:S(2)}) collective-permute-start(f32[384,1536]{1,0:T(8,128)} %constant_dynamic-slice_fusion.14), channel_id=1, source_target_pairs={{0,2},{1,3},{2,0},{3,1},{4,6},{5,7},{6,4},{7,5},{8,10},{9,11},{10,... | collective-permute-start | bytes 7077896 | tf_op jit(solution)/shard_map/ppermute | solution.py:45
  100.3 28.2 %collective-permute-start.3 = (f32[192,1536]{1,0:T(8,128)S(1)}, f32[192,1536]{1,0:T(8,128)}, u32[]{:S(2)}, u32[]{:S(2)}) collective-permute-start(f32[192,1536]{1,0:T(8,128)S(1)} %constant_dynamic-slice_fusion.12), channel_id=1, source_target_pairs={{0,1},{1,0},{2,6},{3,7},{4,5},{5,4},{6,2},{7,3},{8,9},{9,8},{10,14... | collective-permute-start | bytes 3538952 | tf_op jit(solution)/shard_map/ppermute | solution.py:45
  117.3 31.9 %collective-permute-start.2 = (f32[192,1536]{1,0:T(8,128)}, f32[192,1536]{1,0:T(8,128)}, u32[]{:S(2)}, u32[]{:S(2)}) collective-permute-start(f32[192,1536]{1,0:T(8,128)} %constant_dynamic-slice_fusion.11), channel_id=1, source_target_pairs={{0,1},{1,0},{2,6},{3,7},{4,5},{5,4},{6,2},{7,3},{8,9},{9,8},{10,14... | collective-permute-start | bytes 3538952 | tf_op jit(solution)/shard_map/ppermute | solution.py:45
  187.3 23.5 %collective-permute-start.7 = (f32[384,1152]{1,0:T(8,128)}, f32[384,1152]{1,0:T(8,128)}, u32[]{:S(2)}, u32[]{:S(2)}) collective-permute-start(f32[384,1152]{1,0:T(8,128)} %get-tuple-element.399), channel_id=1, source_target_pairs={{0,2},{1,3},{2,0},{3,1},{4,6},{5,7},{6,4},{7,5},{8,10},{9,11},{10,... | collective-permute-start | bytes 5308424 | tf_op jit(solution)/shard_map/ppermute | solution.py:45
  214.7 22.8 %collective-permute-start.15 = (f32[192,1152]{1,0:T(8,128)}, f32[192,1152]{1,0:T(8,128)}, u32[]{:S(2)}, u32[]{:S(2)}) collective-permute-start(f32[192,1152]{1,0:T(8,128)} %constant_dynamic-slice_fusion.5), channel_id=1, source_target_pairs={{0,1},{1,0},{2,6},{3,7},{4,5},{5,4},{6,2},{7,3},{8,9},{9,8},{10,14... | collective-permute-start | bytes 2654216 | tf_op jit(solution)/shard_map/ppermute | solution.py:45
  217.8 22.7 %collective-permute-start.14 = (f32[96,1536]{1,0:T(8,128)S(1)}, f32[96,1536]{1,0:T(8,128)S(1)}, u32[]{:S(2)}, u32[]{:S(2)}) collective-permute-start(f32[96,1536]{1,0:T(8,128)S(1)} %copy-done.16), channel_id=1, source_target_pairs={{8,16},{9,17},{10,18},{11,19},{12,20},{13,21},{14,22},{15,23},{16,... | collective-permute-start | bytes 1769480 | tf_op jit(solution)/shard_map/ppermute | solution.py:45
  237.5 33.4 %collective-permute-start.10 = (f32[368,768]{1,0:T(8,128)S(1)}, f32[368,768]{1,0:T(8,128)S(1)}, u32[]{:S(2)}, u32[]{:S(2)}) collective-permute-start(f32[368,768]{1,0:T(8,128)S(1)} %constant_dynamic-slice_fusion.3), channel_id=1, source_target_pairs={{0,1},{1,0},{2,6},{3,7},{4,5},{5,4},{6,2},{7,3},{8,9},{9,8},{10,14... | collective-permute-start | bytes 3391496 | tf_op jit(solution)/shard_map/ppermute | solution.py:45
  240.6 30.5 %collective-permute-start.20 = (f32[96,1536]{1,0:T(8,128)S(1)}, f32[96,1536]{1,0:T(8,128)S(1)}, u32[]{:S(2)}, u32[]{:S(2)}) collective-permute-start(f32[96,1536]{1,0:T(8,128)S(1)} %add.169), channel_id=1, source_target_pairs={{8,0},{9,1},{10,2},{11,3},{12,4},{13,5},{14,6},{15,7},{16,24},{17,... | collective-permute-start | bytes 1769480 | tf_op jit(solution)/shard_map/ppermute | solution.py:45
  242.9 28.4 %collective-permute-start.18 = (f32[96,1152]{1,0:T(8,128)S(1)}, f32[96,1152]{1,0:T(8,128)S(1)}, u32[]{:S(2)}, u32[]{:S(2)}) collective-permute-start(f32[96,1152]{1,0:T(8,128)S(1)} %constant_dynamic-slice_fusion.1), channel_id=1, source_target_pairs={{0,4},{1,5},{2,3},{3,2},{4,0},{5,1},{6,7},{7,6},{8,12},{9,13},{10,... | collective-permute-start | bytes 1327112 | tf_op jit(solution)/shard_map/ppermute | solution.py:45
  243.2 28.1 %collective-permute-start.19 = (f32[96,1152]{1,0:T(8,128)S(1)}, f32[96,1152]{1,0:T(8,128)S(1)}, u32[]{:S(2)}, u32[]{:S(2)}) collective-permute-start(f32[96,1152]{1,0:T(8,128)S(1)} %constant_dynamic-slice_fusion.2), channel_id=1, source_target_pairs={{0,4},{1,5},{2,3},{3,2},{4,0},{5,1},{6,7},{7,6},{8,12},{9,13},{10,... | collective-permute-start | bytes 1327112 | tf_op jit(solution)/shard_map/ppermute | solution.py:45
  245.1 54.4 %collective-permute-start.17 = (f32[96,1536]{1,0:T(8,128)S(1)}, f32[96,1536]{1,0:T(8,128)S(1)}, u32[]{:S(2)}, u32[]{:S(2)}) collective-permute-start(f32[96,1536]{1,0:T(8,128)S(1)} %add.171), channel_id=1, source_target_pairs={{8,0},{9,1},{10,2},{11,3},{12,4},{13,5},{14,6},{15,7},{16,24},{17,... | collective-permute-start | bytes 1769480 | tf_op jit(solution)/shard_map/ppermute | solution.py:45
  271.3 32.4 %collective-permute-start.16 = (f32[184,768]{1,0:T(8,128)S(1)}, f32[184,768]{1,0:T(8,128)S(1)}, u32[]{:S(2)}, u32[]{:S(2)}) collective-permute-start(f32[184,768]{1,0:T(8,128)S(1)} %constant_dynamic-slice_fusion), channel_id=1, source_target_pairs={{0,4},{1,5},{2,3},{3,2},{4,0},{5,1},{6,7},{7,6},{8,12},{9,13},{10,... | collective-permute-start | bytes 1695752 | tf_op jit(solution)/shard_map/ppermute | solution.py:45
  272.7 45.2 %collective-permute-start.25 = (f32[96,1152]{1,0:T(8,128)S(1)}, f32[96,1152]{1,0:T(8,128)S(1)}, u32[]{:S(2)}, u32[]{:S(2)}) collective-permute-start(f32[96,1152]{1,0:T(8,128)S(1)} %dynamic-slice_add_fusion.14), channel_id=1, source_target_pairs={{0,8},{1,9},{2,10},{3,11},{4,12},{5,13},{6,14},{7,15},{24,16},{25,... | collective-permute-start | bytes 1327112 | tf_op jit(solution)/shard_map/ppermute | solution.py:45
  277.3 38.6 %collective-permute-start.22 = (f32[96,1152]{1,0:T(8,128)S(1)}, f32[96,1152]{1,0:T(8,128)S(1)}, u32[]{:S(2)}, u32[]{:S(2)}) collective-permute-start(f32[96,1152]{1,0:T(8,128)S(1)} %dynamic-slice_add_fusion.13), channel_id=1, source_target_pairs={{0,8},{1,9},{2,10},{3,11},{4,12},{5,13},{6,14},{7,15},{24,16},{25,... | collective-permute-start | bytes 1327112 | tf_op jit(solution)/shard_map/ppermute | solution.py:45
  278.6 38.1 %collective-permute-start.26 = (f32[96,1536]{1,0:T(8,128)S(1)}, f32[96,1536]{1,0:T(8,128)S(1)}, u32[]{:S(2)}, u32[]{:S(2)}) collective-permute-start(f32[96,1536]{1,0:T(8,128)S(1)} %broadcast_select_fusion.15), channel_id=1, source_target_pairs={{0,4},{1,5},{2,3},{3,2},{4,0},{5,1},{6,7},{7,6},{8,12},{9,13},{10,... | collective-permute-start | bytes 1769480 | tf_op jit(solution)/shard_map/ppermute | solution.py:45
  321.1 28.7 %collective-permute-start.28 = (f32[192,1536]{1,0:T(8,128)}, f32[192,1536]{1,0:T(8,128)}, u32[]{:S(2)}, u32[]{:S(2)}) collective-permute-start(f32[192,1536]{1,0:T(8,128)} %pad_maximum_fusion.5), channel_id=1, source_target_pairs={{0,1},{1,0},{2,6},{3,7},{4,5},{5,4},{6,2},{7,3},{8,9},{9,8},{10,14... | collective-permute-start | bytes 3538952 | tf_op jit(solution)/shard_map/ppermute | solution.py:45
  322.0 23.3 %collective-permute-start.23 = (f32[96,1152]{1,0:T(8,128)}, f32[96,1152]{1,0:T(8,128)}, u32[]{:S(2)}, u32[]{:S(2)}) collective-permute-start(f32[96,1152]{1,0:T(8,128)} %add.178), channel_id=1, source_target_pairs={{8,16},{9,17},{10,18},{11,19},{12,20},{13,21},{14,22},{15,23},{16,... | collective-permute-start | bytes 1327112 | tf_op jit(solution)/shard_map/ppermute | solution.py:45
  323.5 23.0 %collective-permute-start.21 = (f32[184,768]{1,0:T(8,128)}, f32[184,768]{1,0:T(8,128)}, u32[]{:S(2)}, u32[]{:S(2)}) collective-permute-start(f32[184,768]{1,0:T(8,128)} %dynamic-slice_add_fusion.12), channel_id=1, source_target_pairs={{0,8},{1,9},{2,10},{3,11},{4,12},{5,13},{6,14},{7,15},{24,16},{25,... | collective-permute-start | bytes 1695752 | tf_op jit(solution)/shard_map/ppermute | solution.py:45
  336.8 53.0 %collective-permute-start.34 = (f32[384,1536]{1,0:T(8,128)S(1)}, f32[384,1536]{1,0:T(8,128)}, u32[]{:S(2)}, u32[]{:S(2)}) collective-permute-start(f32[384,1536]{1,0:T(8,128)S(1)} %pad_maximum_fusion.1.refs_1_), channel_id=1, source_target_pairs={{0,2},{1,3},{2,0},{3,1},{4,6},{5,7},{6,4},{7,5},{8,10},{9,11},{10,... | collective-permute-start | bytes 7077896 | tf_op jit(solution)/shard_map/ppermute | solution.py:45
  349.1 23.0 %collective-permute-start.27 = (f32[184,768]{1,0:T(8,128)S(1)}, f32[184,768]{1,0:T(8,128)S(1)}, u32[]{:S(2)}, u32[]{:S(2)}) collective-permute-start(f32[184,768]{1,0:T(8,128)S(1)} %add.181), channel_id=1, source_target_pairs={{8,16},{9,17},{10,18},{11,19},{12,20},{13,21},{14,22},{15,23},{16,... | collective-permute-start | bytes 1695752 | tf_op jit(solution)/shard_map/ppermute | solution.py:45
  354.6 53.5 %collective-permute-start.29 = (f32[384,1536]{1,0:T(8,128)S(1)}, f32[384,1536]{1,0:T(8,128)S(1)}, u32[]{:S(2)}, u32[]{:S(2)}) collective-permute-start(f32[384,1536]{1,0:T(8,128)S(1)} %pad_maximum_fusion.refs_0_), channel_id=1, source_target_pairs={{0,2},{1,3},{2,0},{3,1},{4,6},{5,7},{6,4},{7,5},{8,10},{9,11},{10,... | collective-permute-start | bytes 7077896 | tf_op jit(solution)/shard_map/ppermute | solution.py:45
  373.8 31.8 %collective-permute-start.40 = (f32[192,1152]{1,0:T(8,128)S(1)}, f32[192,1152]{1,0:T(8,128)S(1)}, u32[]{:S(2)}, u32[]{:S(2)}) collective-permute-start(f32[192,1152]{1,0:T(8,128)S(1)} %pad_maximum_fusion.8), channel_id=1, source_target_pairs={{0,1},{1,0},{2,6},{3,7},{4,5},{5,4},{6,2},{7,3},{8,9},{9,8},{10,14... | collective-permute-start | bytes 2654216 | tf_op jit(solution)/shard_map/ppermute | solution.py:45
  (44 other events, 443.6 us)
Sparse Core Ops, SparseCore 0:
  47.9 148.8 reduce-scatter.1
  214.8 105.4 all-gather.1

commit v4 on v3

--- a/solution.py
+++ b/solution.py
@@ -313,8 +313,8 @@
     joined_bias = jnp.concatenate([lines[6:7], jnp.zeros((1, width), f32), lines[7:8]], axis=1)
     projected_out[...] = (mm(first, project_weight[...]) + joined_bias).astype(bf16)
     low_lanes = lax.broadcasted_iota(jnp.int32, (group, 128), 1) < 64
-    for g in range(rows // group):
-        span = slice(g * group, (g + 1) * group)
+    def one_group(g, carry):
+        span = pl.ds(pl.multiple_of(g * group, group), group)
         same = same_sample(codes, g)
         here = [slice(j * 128, (j + 1) * 128) for j in range(3 * width // 128)]
         count = width // 128
@@ -326,6 +326,9 @@
             heads_out[span, here[j]] = jnp.where(
                 low_lanes, both[j][:group], both[j][group:]
             ).astype(bf16)
+        return carry
+
+    lax.fori_loop(0, rows // group, one_group, 0)
     mid = stream + (mm(heads_out[...], output_weight[...]) + lines[4:5])
     mid_out[...] = mid
     normed, _ = normalize(mid)
@@ -435,15 +438,17 @@
     bias_gradient = column_sum(branch.astype(f32))
     heads_gradient = mm_nt(branch, output_weight[...]).astype(bf16)
     low_lanes = lax.broadcasted_iota(jnp.int32, (group, 128), 1) < 64
-    for g in range(rows // group):
-        span = slice(g * group, (g + 1) * group)
+    token_gradient[...] = heads_gradient
+
+    def one_group(g, carry):
+        span = pl.ds(pl.multiple_of(g * group, group), group)
         same = same_sample(codes, g)
         here = [slice(j * 128, (j + 1) * 128) for j in range(3 * width // 128)]
         count = width // 128
         columns = [projected[span, one] for one in here]
         queries = [two_heads(one * bf16(scale), low_lanes) for one in columns[:count]]
         keys, values = columns[count : 2 * count], columns[2 * count :]
-        uppers = [two_heads(heads_gradient[span, one], low_lanes) for one in here[:count]]
+        uppers = [two_heads(token_gradient[span, one], low_lanes) for one in here[:count]]
         probs = all_probs(queries, keys, same)
         weights = [mm_nt(upper, v) for upper, v in zip(uppers, values)]
         inner = [jnp.sum(w * p, axis=-1, keepdims=True) for w, p in zip(weights, probs)]
@@ -458,6 +463,9 @@
             ).astype(bf16)
             pieces[span, here[count + j]] = for_keys[j].astype(bf16)
             pieces[span, here[2 * count + j]] = for_values[j].astype(bf16)
+        return carry
+
+    lax.fori_loop(0, rows // group, one_group, 0)
     upstream = mm_nt(pieces[...], project_weight[...])
     normed, inverse = normalize(stream[...])
     in_gradient = mid_gradient + norm_backward(upstream, normed, inverse, lines[0:1])

time: 461 us -> 463 us (level)
  no operation moved by 1% of the time
where the time goes in v4:
time: 463 us; the launch traced here: 457 us
  Pallas kernels  169 us (37%)
  waiting for transfers between devices  138 us (30%)
  starting transfers between devices  59.2 us (13%)
  other arithmetic  41.7 us (9%)
  local copies, waits for them, and re-layouts  34.1 us (7%)
  between operations  14.8 us (3%)
    ppermute x45, waiting for transfers between devices, send(): return lax.ppermute(value, AXES, pairs(sizes, target))  138 us
    ppermute x45, starting transfers between devices, send(): return lax.ppermute(value, AXES, pairs(sizes, target))  58.9 us
    pallas_call x4, Pallas kernels, body(): pl.pallas_call(back_kernel, name='back', cost_estimate=SMALL, grid=(1,),...  40.7 us
    pallas_call x1, Pallas kernels, body(): pl.pallas_call(front_kernel, name='front', grid=(rows // BLOCK,), in_spec...  21.3 us
    pallas_call x1, Pallas kernels, body(): pl.pallas_call(last_reduce_kernel, name='reduce_two', cost_estimate=SMALL...  21.2 us
    pallas_call x1, Pallas kernels, body(): pl.pallas_call(first_reduce_kernel, name='reduce_one', cost_estimate=SMAL...  20 us
    pallas_call x1, Pallas kernels, body(): pl.pallas_call(expand_kernel, name='expand', grid=(hidden_width // WIDE,)...  18.1 us
    dynamic_slice x14, local copies, waits for them, and re-layouts, half(): return lax.dynamic_slice_in_dim(value, index * rows, rows, 0)  16.3 us
  transfers between devices with their start and end apart: 47, of which 15 were waited for; matrix products, arithmetic and copies ran while one was open for 13% of the time, Pallas kernels for 27%

profile of v4, /device:TPU:0, one launch (start us, length us, event | category | flops | bytes accessed | tf_op | source)
XLA Modules:
  0.0 456.9 jit_solution(12815814900094672030)
XLA Ops:
  10.7 21.3 %front.1 = (f32[1024,768]{1,0:T(8,128)}, bf16[1024,768]{1,0:T(8,128)(2,1)}, bf16[1024,2304]{1,0:T(8,128)(2,1)}, bf16[1024,768]{1,0:T(8,128)(2,1)}, f32[1024,768]{1,0:T(8,128)}, /*index=5*/bf16[1024,768]{1,0:T(8,128)(2,1)}) custom-call(bf16[1024,768]{1,0:T(8,128)(2,1)} %tokens.1, s32[8,2,128]{2,1,0:T(2,128)} %pad_add_fusion.codes, bf16[640,768]{1,0:T(8,128)(2,1)} %table.1, ...), custom_call_target="tpu_custom_call" | custom-call | tf_op jit(solution)/shard_map/front/pallas_call | solution.py:597
  32.0 18.1 %expand.1 = (bf16[1024,3072]{1,0:T(8,128)(2,1)}, bf16[1024,3072]{1,0:T(8,128)(2,1)}, f32[3072,768]{1,0:T(8,128)}) custom-call(bf16[1024,768]{1,0:T(8,128)(2,1)} %get-tuple-element.286.second, bf16[1024,768]{1,0:T(8,128)(2,1)} %cotangent.13, bf16[768,3072]{1,0:T(8,128)(2,1)} %expand_weight.5, f32[1,3072]{1,0:T(1,128)} %get-tuple-element.284.expand_bias), custom_call_target="tpu_custom_call" | custom-call | tf_op jit(solution)/shard_map/expand/pallas_call | solution.py:610
  50.4 20.0 %reduce_one.1 = (f32[1024,768]{1,0:T(8,128)}, f32[1024,768]{1,0:T(8,128)}, f32[768,1536]{1,0:T(8,128)}, f32[3,1,512]{2,1,0:T(1,128)}) custom-call(bf16[1024,768]{1,0:T(8,128)(2,1)} %get-tuple-element.286.second, bf16[1024,768]{1,0:T(8,128)(2,1)} %cotangent.13, f32[1024,768]{1,0:T(8,128)} %get-tuple-element.287.mid, ...), custom_call_target="tpu_custom_call" | custom-call | flops 1 | bytes 1 | tf_op jit(solution)/shard_map/reduce_one/pallas_call | solution.py:676
  74.2 21.2 %reduce_two.1 = (bf16[1024,768]{1,0:T(8,128)(2,1)}, f32[1024,768]{1,0:T(8,128)}, f32[768,1536]{1,0:T(8,128)}, f32[3,1,512]{2,1,0:T(1,128)}) custom-call(bf16[1024,768]{1,0:T(8,128)(2,1)} %get-tuple-element.286.second, bf16[1024,768]{1,0:T(8,128)(2,1)} %cotangent.13, f32[1024,768]{1,0:T(8,128)} %get-tuple-element.290.before_total, ...), custom_call_target="tpu_custom_call" | custom-call | flops 1 | bytes 1 | tf_op jit(solution)/shard_map/reduce_two/pallas_call | solution.py:689
  105.2 10.1 %back.4 = (bf16[1024,768]{1,0:T(8,128)(2,1)}, f32[1024,768]{1,0:T(8,128)}, bf16[1024,2304]{1,0:T(8,128)(2,1)}, bf16[1024,768]{1,0:T(8,128)(2,1)}, f32[4,8,768]{2,1,0:T(8,128)}) custom-call(f32[1024,768]{1,0:T(8,128)} %get-tuple-element.357.second_gradient, f32[1024,768]{1,0:T(8,128)} %get-tuple-element.287.mid, f32[1024,768]{1,0:T(8,128)} %get-tuple-element.311.stream, ...), custom_call_target="tpu_custom_call" | custom-call | flops 1 | bytes 1 | tf_op jit(solution)/shard_map/back/pallas_call | solution.py:722
  120.1 10.1 %back.5 = (bf16[1024,768]{1,0:T(8,128)(2,1)}, f32[1024,768]{1,0:T(8,128)}, bf16[1024,2304]{1,0:T(8,128)(2,1)}, bf16[1024,768]{1,0:T(8,128)(2,1)}, f32[4,8,768]{2,1,0:T(8,128)}) custom-call(f32[1024,768]{1,0:T(8,128)} %get-tuple-element.357.second_gradient, ...), custom_call_target="tpu_custom_call", output_to_operand_aliasing={{0}: (9, {}), {1}: (10, {}), {2}: (11, {}), {3}: (12, {}), ... | custom-call | flops 1 | bytes 1 | tf_op jit(solution)/shard_map/back/pallas_call | solution.py:722
  132.9 10.2 %back.6 = (bf16[1024,768]{1,0:T(8,128)(2,1)}, f32[1024,768]{1,0:T(8,128)}, bf16[1024,2304]{1,0:T(8,128)(2,1)}, bf16[1024,768]{1,0:T(8,128)(2,1)}, f32[4,8,768]{2,1,0:T(8,128)}) custom-call(f32[1024,768]{1,0:T(8,128)} %get-tuple-element.357.second_gradient, ...), custom_call_target="tpu_custom_call", output_to_operand_aliasing={{0}: (9, {}), {1}: (10, {}), {2}: (11, {}), {3}: (12, {}), ... | custom-call | flops 1 | bytes 1 | tf_op jit(solution)/shard_map/back/pallas_call | solution.py:722
  145.1 7.4 %collective-permute-done.2 = f32[192,1536]{1,0:T(8,128)} collective-permute-done((f32[192,1536]{1,0:T(8,128)}, f32[192,1536]{1,0:T(8,128)}, u32[]{:S(2)}, u32[]{:S(2)}) %collective-permute-start.2) | collective-permute-done | bytes 1179680 | tf_op jit(solution)/shard_map/ppermute | solution.py:45
  157.1 10.3 %back.7 = (bf16[1024,768]{1,0:T(8,128)(2,1)}, f32[1024,768]{1,0:T(8,128)}, bf16[1024,2304]{1,0:T(8,128)(2,1)}, bf16[1024,768]{1,0:T(8,128)(2,1)}, f32[4,8,768]{2,1,0:T(8,128)}) custom-call(f32[1024,768]{1,0:T(8,128)} %get-tuple-element.357.second_gradient, ...), custom_call_target="tpu_custom_call", output_to_operand_aliasing={{0}: (9, {}), {1}: (10, {}), {2}: (11, {}), {3}: (12, {}), ... | custom-call | flops 1 | bytes 1 | tf_op jit(solution)/shard_map/back/pallas_call | solution.py:722
  173.1 10.0 %project.1 = f32[768,2304]{1,0:T(8,128)} custom-call(bf16[1024,768]{1,0:T(8,128)(2,1)} %get-tuple-element.372.first, bf16[1024,2304]{1,0:T(8,128)(2,1)} %get-tuple-element.383.pieces), custom_call_target="tpu_custom_call" | custom-call | flops 1 | bytes 1 | tf_op jit(solution)/shard_map/project/pallas_call | solution.py:760
  195.8 8.5 %mixed.1 = f32[1472,768]{1,0:T(8,128)} custom-call(bf16[1024,768]{1,0:T(8,128)(2,1)} %get-tuple-element.370.heads, bf16[1024,768]{1,0:T(8,128)(2,1)} %get-tuple-element.389.branch, f32[1024,768]{1,0:T(8,128)} %get-tuple-element.390.in_gradient, s32[8,2,128]{2,1,0:T(2,128)} %pad_add_fusion.codes, f32[4,8,768]{2,1,0:T(8,128)} %get-tuple-element.391.sums, ...), custom_call_target="tpu_custom_call" | custom-call | flops 1 | bytes 1 | tf_op jit(solution)/shard_map/mixed/pallas_call | solution.py:779
  224.5 14.3 %collective-permute-done.11 = f32[96,1536]{1,0:T(8,128)} collective-permute-done((f32[96,1536]{1,0:T(8,128)S(1)}, f32[96,1536]{1,0:T(8,128)}, u32[]{:S(2)}, u32[]{:S(2)}) %collective-permute-start.11) | collective-permute-done | bytes 589856 | tf_op jit(solution)/shard_map/ppermute | solution.py:45
  248.8 24.7 %collective-permute-done.10 = f32[368,768]{1,0:T(8,128)S(1)} collective-permute-done((f32[368,768]{1,0:T(8,128)S(1)}, f32[368,768]{1,0:T(8,128)S(1)}, u32[]{:S(2)}, u32[]{:S(2)}) %collective-permute-start.10) | collective-permute-done | bytes 1130528 | tf_op jit(solution)/shard_map/ppermute | solution.py:45
  281.7 19.4 %collective-permute-done.17 = f32[96,1536]{1,0:T(8,128)S(1)} collective-permute-done((f32[96,1536]{1,0:T(8,128)S(1)}, f32[96,1536]{1,0:T(8,128)S(1)}, u32[]{:S(2)}, u32[]{:S(2)}) %collective-permute-start.17) | collective-permute-done | bytes 589856 | tf_op jit(solution)/shard_map/ppermute | solution.py:45
  304.3 14.0 %collective-permute-done.22 = f32[96,1152]{1,0:T(8,128)S(1)} collective-permute-done((f32[96,1152]{1,0:T(8,128)S(1)}, f32[96,1152]{1,0:T(8,128)S(1)}, u32[]{:S(2)}, u32[]{:S(2)}) %collective-permute-start.22) | collective-permute-done | bytes 442400 | tf_op jit(solution)/shard_map/ppermute | solution.py:45
  325.9 6.3 %collective-permute-start.21 = (f32[184,768]{1,0:T(8,128)}, f32[184,768]{1,0:T(8,128)}, u32[]{:S(2)}, u32[]{:S(2)}) collective-permute-start(f32[184,768]{1,0:T(8,128)} %dynamic-slice_add_fusion.12), channel_id=1, source_target_pairs={{0,8},{1,9},{2,10},{3,11},{4,12},{5,13},{6,14},{7,15},{24,16},{25,... | collective-permute-start | bytes 1695752 | tf_op jit(solution)/shard_map/ppermute | solution.py:45
  333.6 5.2 %collective-permute-done.30 = f32[192,1536]{1,0:T(8,128)S(1)} collective-permute-done((f32[192,1536]{1,0:T(8,128)}, f32[192,1536]{1,0:T(8,128)S(1)}, u32[]{:S(2)}, u32[]{:S(2)}) %collective-permute-start.30) | collective-permute-done | bytes 1179680 | tf_op jit(solution)/shard_map/ppermute | solution.py:45
  339.3 8.4 %copied.1.refs_2_ = f32[3072,768]{1,0:T(8,128)} custom-call(f32[3072,768]{1,0:T(8,128)} %all-gather.2.cloned.1.call-done.source), custom_call_target="tpu_custom_call" | custom-call | tf_op jit(solution)/shard_map/copied/pallas_call | solution.py:199
  357.3 7.9 %collective-permute-done.31 = f32[96,1152]{1,0:T(8,128)S(1)} collective-permute-done((f32[96,1152]{1,0:T(8,128)S(1)}, f32[96,1152]{1,0:T(8,128)S(1)}, u32[]{:S(2)}, u32[]{:S(2)}) %collective-permute-start.31) | collective-permute-done | bytes 442400 | tf_op jit(solution)/shard_map/ppermute | solution.py:45
  366.1 7.4 %collective-permute-done.35 = f32[96,1152]{1,0:T(8,128)S(1)} collective-permute-done((f32[96,1152]{1,0:T(8,128)S(1)}, f32[96,1152]{1,0:T(8,128)S(1)}, u32[]{:S(2)}, u32[]{:S(2)}) %collective-permute-start.35) | collective-permute-done | bytes 442400 | tf_op jit(solution)/shard_map/ppermute | solution.py:45
  377.3 8.9 %collective-permute-done.42 = f32[96,1152]{1,0:T(8,128)S(1)} collective-permute-done((f32[96,1152]{1,0:T(8,128)S(1)}, f32[96,1152]{1,0:T(8,128)S(1)}, u32[]{:S(2)}, u32[]{:S(2)}) %collective-permute-start.42) | collective-permute-done | bytes 442400 | tf_op jit(solution)/shard_map/ppermute | solution.py:45
  392.2 13.8 %collective-permute-done.37 = f32[184,768]{1,0:T(8,128)S(1)} collective-permute-done((f32[184,768]{1,0:T(8,128)S(1)}, f32[184,768]{1,0:T(8,128)S(1)}, u32[]{:S(2)}, u32[]{:S(2)}) %collective-permute-start.37) | collective-permute-done | bytes 565280 | tf_op jit(solution)/shard_map/ppermute | solution.py:45
  411.9 8.1 %assemble.2.refs_1_ = f32[768,3072]{1,0:T(8,128)} custom-call(s32[1]{0:T(128)} %bitcast.3.where, f32[384,1536]{1,0:T(8,128)} %copy-done.5, f32[384,1536]{1,0:T(8,128)} %copy-done.4, f32[384,1536]{1,0:T(8,128)} %copy-done.19, f32[384,1536]{1,0:T(8,128)} %collective-permute-done.34.refs_3_), custom_call_target="tpu_custom_call" | custom-call | tf_op jit(solution)/shard_map/assemble/pallas_call | solution.py:167
  435.2 6.7 %assemble.3 = f32[768,2304]{1,0:T(8,128)} custom-call(s32[1]{0:T(128)} %bitcast.3.where, f32[384,1152]{1,0:T(8,128)} %copy-done.11, f32[384,1152]{1,0:T(8,128)} %copy-done.10, f32[384,1152]{1,0:T(8,128)} %collective-permute-done.41.refs_2_, f32[384,1152]{1,0:T(8,128)} %copy-done.20), custom_call_target="tpu_custom_call" | custom-call | tf_op jit(solution)/shard_map/assemble/pallas_call | solution.py:167
  (204 shorter events, 149.9 us)
Async XLA Ops:
  7.2 209.4 %reduce-scatter.2.cloned.1.call-start = ((), (), s32[]{:S(2)}) async-start(), calls=%async_computation.1 | async-start | bytes 9732096 | tf_op jit(solution)/shard_map/reduce_scatter | solution.py:634
  50.2 289.1 %all-gather.2.cloned.1.call-start = ((), (), s32[]{:S(2)}) async-start(), calls=%async_computation.2 | async-start | bytes 9732096 | tf_op jit(solution)/shard_map/all_gather | solution.py:644
  73.8 25.0 %collective-permute-start.1 = (f32[384,1536]{1,0:T(8,128)}, f32[384,1536]{1,0:T(8,128)S(1)}, u32[]{:S(2)}, u32[]{:S(2)}) collective-permute-start(f32[384,1536]{1,0:T(8,128)} %constant_dynamic-slice_fusion.14), channel_id=1, source_target_pairs={{0,2},{1,3},{2,0},{3,1},{4,6},{5,7},{6,4},{7,5},{8,10},{9,11},{10,... | collective-permute-start | bytes 7077896 | tf_op jit(solution)/shard_map/ppermute | solution.py:45
  102.3 27.9 %collective-permute-start.3 = (f32[192,1536]{1,0:T(8,128)S(1)}, f32[192,1536]{1,0:T(8,128)}, u32[]{:S(2)}, u32[]{:S(2)}) collective-permute-start(f32[192,1536]{1,0:T(8,128)S(1)} %constant_dynamic-slice_fusion.12), channel_id=1, source_target_pairs={{0,1},{1,0},{2,6},{3,7},{4,5},{5,4},{6,2},{7,3},{8,9},{9,8},{10,14... | collective-permute-start | bytes 3538952 | tf_op jit(solution)/shard_map/ppermute | solution.py:45
  119.3 33.2 %collective-permute-start.2 = (f32[192,1536]{1,0:T(8,128)}, f32[192,1536]{1,0:T(8,128)}, u32[]{:S(2)}, u32[]{:S(2)}) collective-permute-start(f32[192,1536]{1,0:T(8,128)} %constant_dynamic-slice_fusion.11), channel_id=1, source_target_pairs={{0,1},{1,0},{2,6},{3,7},{4,5},{5,4},{6,2},{7,3},{8,9},{9,8},{10,14... | collective-permute-start | bytes 3538952 | tf_op jit(solution)/shard_map/ppermute | solution.py:45
  143.1 24.2 %collective-permute-start.5 = (f32[96,1536]{1,0:T(8,128)}, f32[96,1536]{1,0:T(8,128)}, u32[]{:S(2)}, u32[]{:S(2)}) collective-permute-start(f32[96,1536]{1,0:T(8,128)} %constant_dynamic-slice_fusion.10), channel_id=1, source_target_pairs={{0,4},{1,5},{2,3},{3,2},{4,0},{5,1},{6,7},{7,6},{8,12},{9,13},{10,... | collective-permute-start | bytes 1769480 | tf_op jit(solution)/shard_map/ppermute | solution.py:45
  189.7 23.0 %collective-permute-start.7 = (f32[384,1152]{1,0:T(8,128)}, f32[384,1152]{1,0:T(8,128)}, u32[]{:S(2)}, u32[]{:S(2)}) collective-permute-start(f32[384,1152]{1,0:T(8,128)} %get-tuple-element.399), channel_id=1, source_target_pairs={{0,2},{1,3},{2,0},{3,1},{4,6},{5,7},{6,4},{7,5},{8,10},{9,11},{10,... | collective-permute-start | bytes 5308424 | tf_op jit(solution)/shard_map/ppermute | solution.py:45
  216.7 23.2 %collective-permute-start.15 = (f32[192,1152]{1,0:T(8,128)}, f32[192,1152]{1,0:T(8,128)}, u32[]{:S(2)}, u32[]{:S(2)}) collective-permute-start(f32[192,1152]{1,0:T(8,128)} %constant_dynamic-slice_fusion.5), channel_id=1, source_target_pairs={{0,1},{1,0},{2,6},{3,7},{4,5},{5,4},{6,2},{7,3},{8,9},{9,8},{10,14... | collective-permute-start | bytes 2654216 | tf_op jit(solution)/shard_map/ppermute | solution.py:45
  239.9 33.6 %collective-permute-start.10 = (f32[368,768]{1,0:T(8,128)S(1)}, f32[368,768]{1,0:T(8,128)S(1)}, u32[]{:S(2)}, u32[]{:S(2)}) collective-permute-start(f32[368,768]{1,0:T(8,128)S(1)} %constant_dynamic-slice_fusion.3), channel_id=1, source_target_pairs={{0,1},{1,0},{2,6},{3,7},{4,5},{5,4},{6,2},{7,3},{8,9},{9,8},{10,14... | collective-permute-start | bytes 3391496 | tf_op jit(solution)/shard_map/ppermute | solution.py:45
  243.0 30.8 %collective-permute-start.20 = (f32[96,1536]{1,0:T(8,128)S(1)}, f32[96,1536]{1,0:T(8,128)S(1)}, u32[]{:S(2)}, u32[]{:S(2)}) collective-permute-start(f32[96,1536]{1,0:T(8,128)S(1)} %add.169), channel_id=1, source_target_pairs={{8,0},{9,1},{10,2},{11,3},{12,4},{13,5},{14,6},{15,7},{16,24},{17,... | collective-permute-start | bytes 1769480 | tf_op jit(solution)/shard_map/ppermute | solution.py:45
  245.3 28.7 %collective-permute-start.18 = (f32[96,1152]{1,0:T(8,128)S(1)}, f32[96,1152]{1,0:T(8,128)S(1)}, u32[]{:S(2)}, u32[]{:S(2)}) collective-permute-start(f32[96,1152]{1,0:T(8,128)S(1)} %constant_dynamic-slice_fusion.1), channel_id=1, source_target_pairs={{0,4},{1,5},{2,3},{3,2},{4,0},{5,1},{6,7},{7,6},{8,12},{9,13},{10,... | collective-permute-start | bytes 1327112 | tf_op jit(solution)/shard_map/ppermute | solution.py:45
  246.0 27.9 %collective-permute-start.19 = (f32[96,1152]{1,0:T(8,128)S(1)}, f32[96,1152]{1,0:T(8,128)S(1)}, u32[]{:S(2)}, u32[]{:S(2)}) collective-permute-start(f32[96,1152]{1,0:T(8,128)S(1)} %constant_dynamic-slice_fusion.2), channel_id=1, source_target_pairs={{0,4},{1,5},{2,3},{3,2},{4,0},{5,1},{6,7},{7,6},{8,12},{9,13},{10,... | collective-permute-start | bytes 1327112 | tf_op jit(solution)/shard_map/ppermute | solution.py:45
  247.5 53.6 %collective-permute-start.17 = (f32[96,1536]{1,0:T(8,128)S(1)}, f32[96,1536]{1,0:T(8,128)S(1)}, u32[]{:S(2)}, u32[]{:S(2)}) collective-permute-start(f32[96,1536]{1,0:T(8,128)S(1)} %add.171), channel_id=1, source_target_pairs={{8,0},{9,1},{10,2},{11,3},{12,4},{13,5},{14,6},{15,7},{16,24},{17,... | collective-permute-start | bytes 1769480 | tf_op jit(solution)/shard_map/ppermute | solution.py:45
  274.0 29.4 %collective-permute-start.16 = (f32[184,768]{1,0:T(8,128)S(1)}, f32[184,768]{1,0:T(8,128)S(1)}, u32[]{:S(2)}, u32[]{:S(2)}) collective-permute-start(f32[184,768]{1,0:T(8,128)S(1)} %constant_dynamic-slice_fusion), channel_id=1, source_target_pairs={{0,4},{1,5},{2,3},{3,2},{4,0},{5,1},{6,7},{7,6},{8,12},{9,13},{10,... | collective-permute-start | bytes 1695752 | tf_op jit(solution)/shard_map/ppermute | solution.py:45
  275.2 45.2 %collective-permute-start.25 = (f32[96,1152]{1,0:T(8,128)S(1)}, f32[96,1152]{1,0:T(8,128)S(1)}, u32[]{:S(2)}, u32[]{:S(2)}) collective-permute-start(f32[96,1152]{1,0:T(8,128)S(1)} %dynamic-slice_add_fusion.14), channel_id=1, source_target_pairs={{0,8},{1,9},{2,10},{3,11},{4,12},{5,13},{6,14},{7,15},{24,16},{25,... | collective-permute-start | bytes 1327112 | tf_op jit(solution)/shard_map/ppermute | solution.py:45
  279.8 38.5 %collective-permute-start.22 = (f32[96,1152]{1,0:T(8,128)S(1)}, f32[96,1152]{1,0:T(8,128)S(1)}, u32[]{:S(2)}, u32[]{:S(2)}) collective-permute-start(f32[96,1152]{1,0:T(8,128)S(1)} %dynamic-slice_add_fusion.13), channel_id=1, source_target_pairs={{0,8},{1,9},{2,10},{3,11},{4,12},{5,13},{6,14},{7,15},{24,16},{25,... | collective-permute-start | bytes 1327112 | tf_op jit(solution)/shard_map/ppermute | solution.py:45
  281.1 38.0 %collective-permute-start.26 = (f32[96,1536]{1,0:T(8,128)S(1)}, f32[96,1536]{1,0:T(8,128)S(1)}, u32[]{:S(2)}, u32[]{:S(2)}) collective-permute-start(f32[96,1536]{1,0:T(8,128)S(1)} %broadcast_select_fusion.15), channel_id=1, source_target_pairs={{0,4},{1,5},{2,3},{3,2},{4,0},{5,1},{6,7},{7,6},{8,12},{9,13},{10,... | collective-permute-start | bytes 1769480 | tf_op jit(solution)/shard_map/ppermute | solution.py:45
  323.5 28.9 %collective-permute-start.28 = (f32[192,1536]{1,0:T(8,128)}, f32[192,1536]{1,0:T(8,128)}, u32[]{:S(2)}, u32[]{:S(2)}) collective-permute-start(f32[192,1536]{1,0:T(8,128)} %pad_maximum_fusion.5), channel_id=1, source_target_pairs={{0,1},{1,0},{2,6},{3,7},{4,5},{5,4},{6,2},{7,3},{8,9},{9,8},{10,14... | collective-permute-start | bytes 3538952 | tf_op jit(solution)/shard_map/ppermute | solution.py:45
  324.4 23.3 %collective-permute-start.23 = (f32[96,1152]{1,0:T(8,128)}, f32[96,1152]{1,0:T(8,128)}, u32[]{:S(2)}, u32[]{:S(2)}) collective-permute-start(f32[96,1152]{1,0:T(8,128)} %add.178), channel_id=1, source_target_pairs={{8,16},{9,17},{10,18},{11,19},{12,20},{13,21},{14,22},{15,23},{16,... | collective-permute-start | bytes 1327112 | tf_op jit(solution)/shard_map/ppermute | solution.py:45
  325.9 23.0 %collective-permute-start.21 = (f32[184,768]{1,0:T(8,128)}, f32[184,768]{1,0:T(8,128)}, u32[]{:S(2)}, u32[]{:S(2)}) collective-permute-start(f32[184,768]{1,0:T(8,128)} %dynamic-slice_add_fusion.12), channel_id=1, source_target_pairs={{0,8},{1,9},{2,10},{3,11},{4,12},{5,13},{6,14},{7,15},{24,16},{25,... | collective-permute-start | bytes 1695752 | tf_op jit(solution)/shard_map/ppermute | solution.py:45
  339.2 53.0 %collective-permute-start.34 = (f32[384,1536]{1,0:T(8,128)S(1)}, f32[384,1536]{1,0:T(8,128)}, u32[]{:S(2)}, u32[]{:S(2)}) collective-permute-start(f32[384,1536]{1,0:T(8,128)S(1)} %pad_maximum_fusion.1.refs_1_), channel_id=1, source_target_pairs={{0,2},{1,3},{2,0},{3,1},{4,6},{5,7},{6,4},{7,5},{8,10},{9,11},{10,... | collective-permute-start | bytes 7077896 | tf_op jit(solution)/shard_map/ppermute | solution.py:45
  351.5 22.9 %collective-permute-start.27 = (f32[184,768]{1,0:T(8,128)S(1)}, f32[184,768]{1,0:T(8,128)S(1)}, u32[]{:S(2)}, u32[]{:S(2)}) collective-permute-start(f32[184,768]{1,0:T(8,128)S(1)} %add.181), channel_id=1, source_target_pairs={{8,16},{9,17},{10,18},{11,19},{12,20},{13,21},{14,22},{15,23},{16,... | collective-permute-start | bytes 1695752 | tf_op jit(solution)/shard_map/ppermute | solution.py:45
  357.2 53.3 %collective-permute-start.29 = (f32[384,1536]{1,0:T(8,128)S(1)}, f32[384,1536]{1,0:T(8,128)S(1)}, u32[]{:S(2)}, u32[]{:S(2)}) collective-permute-start(f32[384,1536]{1,0:T(8,128)S(1)} %pad_maximum_fusion.refs_0_), channel_id=1, source_target_pairs={{0,2},{1,3},{2,0},{3,1},{4,6},{5,7},{6,4},{7,5},{8,10},{9,11},{10,... | collective-permute-start | bytes 7077896 | tf_op jit(solution)/shard_map/ppermute | solution.py:45
  376.0 32.0 %collective-permute-start.40 = (f32[192,1152]{1,0:T(8,128)S(1)}, f32[192,1152]{1,0:T(8,128)S(1)}, u32[]{:S(2)}, u32[]{:S(2)}) collective-permute-start(f32[192,1152]{1,0:T(8,128)S(1)} %pad_maximum_fusion.8), channel_id=1, source_target_pairs={{0,1},{1,0},{2,6},{3,7},{4,5},{5,4},{6,2},{7,3},{8,9},{9,8},{10,14... | collective-permute-start | bytes 2654216 | tf_op jit(solution)/shard_map/ppermute | solution.py:45
  (44 other events, 443.2 us)
Sparse Core Ops, SparseCore 0:
  50.3 148.8 reduce-scatter.1
  216.8 105.7 all-gather.1

commit v5 on v3

--- a/solution.py
+++ b/solution.py
@@ -10,6 +10,7 @@
 HEADS = 12
 PATCH_LO = 128
 BLOCK = 256
+FRONT = 512
 WIDE = 512
 PLAN = "|a|b|a|b|ab||paq+mbpaqbmapqbmpaqb*pmaqpbampqbmpqmpqqmm"
 
@@ -519,7 +520,7 @@
 
 
 def row_block(array):
-    return pl.BlockSpec((BLOCK, array.shape[1]), lambda i: (i, 0))
+    return pl.BlockSpec((FRONT, array.shape[1]), lambda i: (i, 0))
 
 
 def lead_block(array, count=1):
@@ -589,8 +590,8 @@
     stream, first, projected, heads, mid, second = pl.pallas_call(
         front_kernel,
         name="front",
-        grid=(rows // BLOCK,),
-        in_specs=[row_block(tokens), lead_block(codes, per_step)]
+        grid=(rows // FRONT,),
+        in_specs=[row_block(tokens), lead_block(codes, FRONT // group_rows)]
         + [whole(array) for array in fixed],
         out_specs=[row_block(array) for array in front_shapes],
         out_shape=front_shapes,

time: 461 us -> 462 us (level)
  no operation moved by 1% of the time
where the time goes in v5:
time: 462 us; the launch traced here: 454 us
  Pallas kernels  167 us (36%)
  waiting for transfers between devices  135 us (29%)
  starting transfers between devices  61.3 us (13%)
  other arithmetic  41.6 us (9%)
  local copies, waits for them, and re-layouts  34.2 us (7%)
  between operations  14.8 us (3%)
    ppermute x45, waiting for transfers between devices, send(): return lax.ppermute(value, AXES, pairs(sizes, target))  135 us
    ppermute x45, starting transfers between devices, send(): return lax.ppermute(value, AXES, pairs(sizes, target))  60.7 us
    pallas_call x4, Pallas kernels, body(): pl.pallas_call(back_kernel, name='back', cost_estimate=SMALL, grid=(1,),...  41.3 us
    pallas_call x1, Pallas kernels, body(): pl.pallas_call(last_reduce_kernel, name='reduce_two', cost_estimate=SMALL...  21.3 us
    pallas_call x1, Pallas kernels, body(): pl.pallas_call(first_reduce_kernel, name='reduce_one', cost_estimate=SMAL...  20 us
    pallas_call x1, Pallas kernels, body(): pl.pallas_call(front_kernel, name='front', grid=(rows // FRONT,), in_spec...  18.4 us
    pallas_call x1, Pallas kernels, body(): pl.pallas_call(expand_kernel, name='expand', grid=(hidden_width // WIDE,)...  18.1 us
    dynamic_slice x14, local copies, waits for them, and re-layouts, half(): return lax.dynamic_slice_in_dim(value, index * rows, rows, 0)  16.3 us
  transfers between devices with their start and end apart: 47, of which 15 were waited for; matrix products, arithmetic and copies ran while one was open for 13% of the time, Pallas kernels for 27%

profile of v5, /device:TPU:0, one launch (start us, length us, event | category | flops | bytes accessed | tf_op | source)
XLA Modules:
  0.0 454.1 jit_solution(1101209129139889729)
XLA Ops:
  10.7 18.4 %front.1 = (f32[1024,768]{1,0:T(8,128)}, bf16[1024,768]{1,0:T(8,128)(2,1)}, bf16[1024,2304]{1,0:T(8,128)(2,1)}, bf16[1024,768]{1,0:T(8,128)(2,1)}, f32[1024,768]{1,0:T(8,128)}, /*index=5*/bf16[1024,768]{1,0:T(8,128)(2,1)}) custom-call(bf16[1024,768]{1,0:T(8,128)(2,1)} %tokens.1, s32[8,2,128]{2,1,0:T(2,128)} %pad_add_fusion.codes, bf16[640,768]{1,0:T(8,128)(2,1)} %table.1, ...), custom_call_target="tpu_custom_call" | custom-call | tf_op jit(solution)/shard_map/front/pallas_call | solution.py:590
  29.1 18.1 %expand.1 = (bf16[1024,3072]{1,0:T(8,128)(2,1)}, bf16[1024,3072]{1,0:T(8,128)(2,1)}, f32[3072,768]{1,0:T(8,128)}) custom-call(bf16[1024,768]{1,0:T(8,128)(2,1)} %get-tuple-element.286.second, bf16[1024,768]{1,0:T(8,128)(2,1)} %cotangent.13, bf16[768,3072]{1,0:T(8,128)(2,1)} %expand_weight.5, f32[1,3072]{1,0:T(1,128)} %get-tuple-element.284.expand_bias), custom_call_target="tpu_custom_call" | custom-call | tf_op jit(solution)/shard_map/expand/pallas_call | solution.py:603
  47.8 20.0 %reduce_one.1 = (f32[1024,768]{1,0:T(8,128)}, f32[1024,768]{1,0:T(8,128)}, f32[768,1536]{1,0:T(8,128)}, f32[3,1,512]{2,1,0:T(1,128)}) custom-call(bf16[1024,768]{1,0:T(8,128)(2,1)} %get-tuple-element.286.second, bf16[1024,768]{1,0:T(8,128)(2,1)} %cotangent.13, f32[1024,768]{1,0:T(8,128)} %get-tuple-element.287.mid, ...), custom_call_target="tpu_custom_call" | custom-call | flops 1 | bytes 1 | tf_op jit(solution)/shard_map/reduce_one/pallas_call | solution.py:669
  71.7 21.3 %reduce_two.1 = (bf16[1024,768]{1,0:T(8,128)(2,1)}, f32[1024,768]{1,0:T(8,128)}, f32[768,1536]{1,0:T(8,128)}, f32[3,1,512]{2,1,0:T(1,128)}) custom-call(bf16[1024,768]{1,0:T(8,128)(2,1)} %get-tuple-element.286.second, bf16[1024,768]{1,0:T(8,128)(2,1)} %cotangent.13, f32[1024,768]{1,0:T(8,128)} %get-tuple-element.290.before_total, ...), custom_call_target="tpu_custom_call" | custom-call | flops 1 | bytes 1 | tf_op jit(solution)/shard_map/reduce_two/pallas_call | solution.py:682
  102.8 10.1 %back.4 = (bf16[1024,768]{1,0:T(8,128)(2,1)}, f32[1024,768]{1,0:T(8,128)}, bf16[1024,2304]{1,0:T(8,128)(2,1)}, bf16[1024,768]{1,0:T(8,128)(2,1)}, f32[4,8,768]{2,1,0:T(8,128)}) custom-call(f32[1024,768]{1,0:T(8,128)} %get-tuple-element.357.second_gradient, f32[1024,768]{1,0:T(8,128)} %get-tuple-element.287.mid, f32[1024,768]{1,0:T(8,128)} %get-tuple-element.311.stream, ...), custom_call_target="tpu_custom_call" | custom-call | flops 1 | bytes 1 | tf_op jit(solution)/shard_map/back/pallas_call | solution.py:715
  117.7 10.4 %back.5 = (bf16[1024,768]{1,0:T(8,128)(2,1)}, f32[1024,768]{1,0:T(8,128)}, bf16[1024,2304]{1,0:T(8,128)(2,1)}, bf16[1024,768]{1,0:T(8,128)(2,1)}, f32[4,8,768]{2,1,0:T(8,128)}) custom-call(f32[1024,768]{1,0:T(8,128)} %get-tuple-element.357.second_gradient, ...), custom_call_target="tpu_custom_call", output_to_operand_aliasing={{0}: (9, {}), {1}: (10, {}), {2}: (11, {}), {3}: (12, {}), ... | custom-call | flops 1 | bytes 1 | tf_op jit(solution)/shard_map/back/pallas_call | solution.py:715
  130.7 10.7 %back.6 = (bf16[1024,768]{1,0:T(8,128)(2,1)}, f32[1024,768]{1,0:T(8,128)}, bf16[1024,2304]{1,0:T(8,128)(2,1)}, bf16[1024,768]{1,0:T(8,128)(2,1)}, f32[4,8,768]{2,1,0:T(8,128)}) custom-call(f32[1024,768]{1,0:T(8,128)} %get-tuple-element.357.second_gradient, ...), custom_call_target="tpu_custom_call", output_to_operand_aliasing={{0}: (9, {}), {1}: (10, {}), {2}: (11, {}), {3}: (12, {}), ... | custom-call | flops 1 | bytes 1 | tf_op jit(solution)/shard_map/back/pallas_call | solution.py:715
  143.1 5.6 %collective-permute-done.2 = f32[192,1536]{1,0:T(8,128)} collective-permute-done((f32[192,1536]{1,0:T(8,128)}, f32[192,1536]{1,0:T(8,128)}, u32[]{:S(2)}, u32[]{:S(2)}) %collective-permute-start.2) | collective-permute-done | bytes 1179680 | tf_op jit(solution)/shard_map/ppermute | solution.py:46
  153.1 10.1 %back.7 = (bf16[1024,768]{1,0:T(8,128)(2,1)}, f32[1024,768]{1,0:T(8,128)}, bf16[1024,2304]{1,0:T(8,128)(2,1)}, bf16[1024,768]{1,0:T(8,128)(2,1)}, f32[4,8,768]{2,1,0:T(8,128)}) custom-call(f32[1024,768]{1,0:T(8,128)} %get-tuple-element.357.second_gradient, ...), custom_call_target="tpu_custom_call", output_to_operand_aliasing={{0}: (9, {}), {1}: (10, {}), {2}: (11, {}), {3}: (12, {}), ... | custom-call | flops 1 | bytes 1 | tf_op jit(solution)/shard_map/back/pallas_call | solution.py:715
  170.2 10.0 %project.1 = f32[768,2304]{1,0:T(8,128)} custom-call(bf16[1024,768]{1,0:T(8,128)(2,1)} %get-tuple-element.372.first, bf16[1024,2304]{1,0:T(8,128)(2,1)} %get-tuple-element.383.pieces), custom_call_target="tpu_custom_call" | custom-call | flops 1 | bytes 1 | tf_op jit(solution)/shard_map/project/pallas_call | solution.py:753
  193.3 8.5 %mixed.1 = f32[1472,768]{1,0:T(8,128)} custom-call(bf16[1024,768]{1,0:T(8,128)(2,1)} %get-tuple-element.370.heads, bf16[1024,768]{1,0:T(8,128)(2,1)} %get-tuple-element.389.branch, f32[1024,768]{1,0:T(8,128)} %get-tuple-element.390.in_gradient, s32[8,2,128]{2,1,0:T(2,128)} %pad_add_fusion.codes, f32[4,8,768]{2,1,0:T(8,128)} %get-tuple-element.391.sums, ...), custom_call_target="tpu_custom_call" | custom-call | flops 1 | bytes 1 | tf_op jit(solution)/shard_map/mixed/pallas_call | solution.py:772
  221.6 14.3 %collective-permute-done.11 = f32[96,1536]{1,0:T(8,128)} collective-permute-done((f32[96,1536]{1,0:T(8,128)S(1)}, f32[96,1536]{1,0:T(8,128)}, u32[]{:S(2)}, u32[]{:S(2)}) %collective-permute-start.11) | collective-permute-done | bytes 589856 | tf_op jit(solution)/shard_map/ppermute | solution.py:46
  245.9 24.4 %collective-permute-done.10 = f32[368,768]{1,0:T(8,128)S(1)} collective-permute-done((f32[368,768]{1,0:T(8,128)S(1)}, f32[368,768]{1,0:T(8,128)S(1)}, u32[]{:S(2)}, u32[]{:S(2)}) %collective-permute-start.10) | collective-permute-done | bytes 1130528 | tf_op jit(solution)/shard_map/ppermute | solution.py:46
  278.8 20.2 %collective-permute-done.17 = f32[96,1536]{1,0:T(8,128)S(1)} collective-permute-done((f32[96,1536]{1,0:T(8,128)S(1)}, f32[96,1536]{1,0:T(8,128)S(1)}, u32[]{:S(2)}, u32[]{:S(2)}) %collective-permute-start.17) | collective-permute-done | bytes 589856 | tf_op jit(solution)/shard_map/ppermute | solution.py:46
  304.3 11.1 %collective-permute-done.22 = f32[96,1152]{1,0:T(8,128)S(1)} collective-permute-done((f32[96,1152]{1,0:T(8,128)S(1)}, f32[96,1152]{1,0:T(8,128)S(1)}, u32[]{:S(2)}, u32[]{:S(2)}) %collective-permute-start.22) | collective-permute-done | bytes 442400 | tf_op jit(solution)/shard_map/ppermute | solution.py:46
  323.0 6.2 %collective-permute-start.21 = (f32[184,768]{1,0:T(8,128)}, f32[184,768]{1,0:T(8,128)}, u32[]{:S(2)}, u32[]{:S(2)}) collective-permute-start(f32[184,768]{1,0:T(8,128)} %dynamic-slice_add_fusion.12), channel_id=1, source_target_pairs={{0,8},{1,9},{2,10},{3,11},{4,12},{5,13},{6,14},{7,15},{24,16},{25,... | collective-permute-start | bytes 1695752 | tf_op jit(solution)/shard_map/ppermute | solution.py:46
  330.6 5.3 %collective-permute-done.30 = f32[192,1536]{1,0:T(8,128)S(1)} collective-permute-done((f32[192,1536]{1,0:T(8,128)}, f32[192,1536]{1,0:T(8,128)S(1)}, u32[]{:S(2)}, u32[]{:S(2)}) %collective-permute-start.30) | collective-permute-done | bytes 1179680 | tf_op jit(solution)/shard_map/ppermute | solution.py:46
  336.4 8.4 %copied.1.refs_2_ = f32[3072,768]{1,0:T(8,128)} custom-call(f32[3072,768]{1,0:T(8,128)} %all-gather.2.cloned.1.call-done.source), custom_call_target="tpu_custom_call" | custom-call | tf_op jit(solution)/shard_map/copied/pallas_call | solution.py:200
  354.2 8.0 %collective-permute-done.31 = f32[96,1152]{1,0:T(8,128)S(1)} collective-permute-done((f32[96,1152]{1,0:T(8,128)S(1)}, f32[96,1152]{1,0:T(8,128)S(1)}, u32[]{:S(2)}, u32[]{:S(2)}) %collective-permute-start.31) | collective-permute-done | bytes 442400 | tf_op jit(solution)/shard_map/ppermute | solution.py:46
  363.2 7.4 %collective-permute-done.35 = f32[96,1152]{1,0:T(8,128)S(1)} collective-permute-done((f32[96,1152]{1,0:T(8,128)S(1)}, f32[96,1152]{1,0:T(8,128)S(1)}, u32[]{:S(2)}, u32[]{:S(2)}) %collective-permute-start.35) | collective-permute-done | bytes 442400 | tf_op jit(solution)/shard_map/ppermute | solution.py:46
  374.7 8.3 %collective-permute-done.42 = f32[96,1152]{1,0:T(8,128)S(1)} collective-permute-done((f32[96,1152]{1,0:T(8,128)S(1)}, f32[96,1152]{1,0:T(8,128)S(1)}, u32[]{:S(2)}, u32[]{:S(2)}) %collective-permute-start.42) | collective-permute-done | bytes 442400 | tf_op jit(solution)/shard_map/ppermute | solution.py:46
  389.2 13.9 %collective-permute-done.37 = f32[184,768]{1,0:T(8,128)S(1)} collective-permute-done((f32[184,768]{1,0:T(8,128)S(1)}, f32[184,768]{1,0:T(8,128)S(1)}, u32[]{:S(2)}, u32[]{:S(2)}) %collective-permute-start.37) | collective-permute-done | bytes 565280 | tf_op jit(solution)/shard_map/ppermute | solution.py:46
  409.0 8.1 %assemble.2.refs_1_ = f32[768,3072]{1,0:T(8,128)} custom-call(s32[1]{0:T(128)} %bitcast.3.where, f32[384,1536]{1,0:T(8,128)} %copy-done.5, f32[384,1536]{1,0:T(8,128)} %copy-done.4, f32[384,1536]{1,0:T(8,128)} %copy-done.19, f32[384,1536]{1,0:T(8,128)} %collective-permute-done.34.refs_3_), custom_call_target="tpu_custom_call" | custom-call | tf_op jit(solution)/shard_map/assemble/pallas_call | solution.py:168
  432.4 6.7 %assemble.3 = f32[768,2304]{1,0:T(8,128)} custom-call(s32[1]{0:T(128)} %bitcast.3.where, f32[384,1152]{1,0:T(8,128)} %copy-done.11, f32[384,1152]{1,0:T(8,128)} %copy-done.10, f32[384,1152]{1,0:T(8,128)} %collective-permute-done.41.refs_2_, f32[384,1152]{1,0:T(8,128)} %copy-done.20), custom_call_target="tpu_custom_call" | custom-call | tf_op jit(solution)/shard_map/assemble/pallas_call | solution.py:168
  (204 shorter events, 153.6 us)
Async XLA Ops:
  7.2 207.0 %reduce-scatter.2.cloned.1.call-start = ((), (), s32[]{:S(2)}) async-start(), calls=%async_computation.1 | async-start | bytes 9732096 | tf_op jit(solution)/shard_map/reduce_scatter | solution.py:627
  47.3 289.1 %all-gather.2.cloned.1.call-start = ((), (), s32[]{:S(2)}) async-start(), calls=%async_computation.2 | async-start | bytes 9732096 | tf_op jit(solution)/shard_map/all_gather | solution.py:637
  71.2 25.1 %collective-permute-start.1 = (f32[384,1536]{1,0:T(8,128)}, f32[384,1536]{1,0:T(8,128)S(1)}, u32[]{:S(2)}, u32[]{:S(2)}) collective-permute-start(f32[384,1536]{1,0:T(8,128)} %constant_dynamic-slice_fusion.14), channel_id=1, source_target_pairs={{0,2},{1,3},{2,0},{3,1},{4,6},{5,7},{6,4},{7,5},{8,10},{9,11},{10,... | collective-permute-start | bytes 7077896 | tf_op jit(solution)/shard_map/ppermute | solution.py:46
  99.8 28.3 %collective-permute-start.3 = (f32[192,1536]{1,0:T(8,128)S(1)}, f32[192,1536]{1,0:T(8,128)}, u32[]{:S(2)}, u32[]{:S(2)}) collective-permute-start(f32[192,1536]{1,0:T(8,128)S(1)} %constant_dynamic-slice_fusion.12), channel_id=1, source_target_pairs={{0,1},{1,0},{2,6},{3,7},{4,5},{5,4},{6,2},{7,3},{8,9},{9,8},{10,14... | collective-permute-start | bytes 3538952 | tf_op jit(solution)/shard_map/ppermute | solution.py:46
  116.8 31.8 %collective-permute-start.2 = (f32[192,1536]{1,0:T(8,128)}, f32[192,1536]{1,0:T(8,128)}, u32[]{:S(2)}, u32[]{:S(2)}) collective-permute-start(f32[192,1536]{1,0:T(8,128)} %constant_dynamic-slice_fusion.11), channel_id=1, source_target_pairs={{0,1},{1,0},{2,6},{3,7},{4,5},{5,4},{6,2},{7,3},{8,9},{9,8},{10,14... | collective-permute-start | bytes 3538952 | tf_op jit(solution)/shard_map/ppermute | solution.py:46
  186.9 23.4 %collective-permute-start.7 = (f32[384,1152]{1,0:T(8,128)}, f32[384,1152]{1,0:T(8,128)}, u32[]{:S(2)}, u32[]{:S(2)}) collective-permute-start(f32[384,1152]{1,0:T(8,128)} %get-tuple-element.399), channel_id=1, source_target_pairs={{0,2},{1,3},{2,0},{3,1},{4,6},{5,7},{6,4},{7,5},{8,10},{9,11},{10,... | collective-permute-start | bytes 5308424 | tf_op jit(solution)/shard_map/ppermute | solution.py:46
  214.3 22.8 %collective-permute-start.15 = (f32[192,1152]{1,0:T(8,128)}, f32[192,1152]{1,0:T(8,128)}, u32[]{:S(2)}, u32[]{:S(2)}) collective-permute-start(f32[192,1152]{1,0:T(8,128)} %constant_dynamic-slice_fusion.5), channel_id=1, source_target_pairs={{0,1},{1,0},{2,6},{3,7},{4,5},{5,4},{6,2},{7,3},{8,9},{9,8},{10,14... | collective-permute-start | bytes 2654216 | tf_op jit(solution)/shard_map/ppermute | solution.py:46
  217.3 22.7 %collective-permute-start.14 = (f32[96,1536]{1,0:T(8,128)S(1)}, f32[96,1536]{1,0:T(8,128)S(1)}, u32[]{:S(2)}, u32[]{:S(2)}) collective-permute-start(f32[96,1536]{1,0:T(8,128)S(1)} %copy-done.16), channel_id=1, source_target_pairs={{8,16},{9,17},{10,18},{11,19},{12,20},{13,21},{14,22},{15,23},{16,... | collective-permute-start | bytes 1769480 | tf_op jit(solution)/shard_map/ppermute | solution.py:46
  237.0 33.4 %collective-permute-start.10 = (f32[368,768]{1,0:T(8,128)S(1)}, f32[368,768]{1,0:T(8,128)S(1)}, u32[]{:S(2)}, u32[]{:S(2)}) collective-permute-start(f32[368,768]{1,0:T(8,128)S(1)} %constant_dynamic-slice_fusion.3), channel_id=1, source_target_pairs={{0,1},{1,0},{2,6},{3,7},{4,5},{5,4},{6,2},{7,3},{8,9},{9,8},{10,14... | collective-permute-start | bytes 3391496 | tf_op jit(solution)/shard_map/ppermute | solution.py:46
  240.1 30.5 %collective-permute-start.20 = (f32[96,1536]{1,0:T(8,128)S(1)}, f32[96,1536]{1,0:T(8,128)S(1)}, u32[]{:S(2)}, u32[]{:S(2)}) collective-permute-start(f32[96,1536]{1,0:T(8,128)S(1)} %add.169), channel_id=1, source_target_pairs={{8,0},{9,1},{10,2},{11,3},{12,4},{13,5},{14,6},{15,7},{16,24},{17,... | collective-permute-start | bytes 1769480 | tf_op jit(solution)/shard_map/ppermute | solution.py:46
  242.5 28.4 %collective-permute-start.18 = (f32[96,1152]{1,0:T(8,128)S(1)}, f32[96,1152]{1,0:T(8,128)S(1)}, u32[]{:S(2)}, u32[]{:S(2)}) collective-permute-start(f32[96,1152]{1,0:T(8,128)S(1)} %constant_dynamic-slice_fusion.1), channel_id=1, source_target_pairs={{0,4},{1,5},{2,3},{3,2},{4,0},{5,1},{6,7},{7,6},{8,12},{9,13},{10,... | collective-permute-start | bytes 1327112 | tf_op jit(solution)/shard_map/ppermute | solution.py:46
  242.7 28.1 %collective-permute-start.19 = (f32[96,1152]{1,0:T(8,128)S(1)}, f32[96,1152]{1,0:T(8,128)S(1)}, u32[]{:S(2)}, u32[]{:S(2)}) collective-permute-start(f32[96,1152]{1,0:T(8,128)S(1)} %constant_dynamic-slice_fusion.2), channel_id=1, source_target_pairs={{0,4},{1,5},{2,3},{3,2},{4,0},{5,1},{6,7},{7,6},{8,12},{9,13},{10,... | collective-permute-start | bytes 1327112 | tf_op jit(solution)/shard_map/ppermute | solution.py:46
  244.6 54.4 %collective-permute-start.17 = (f32[96,1536]{1,0:T(8,128)S(1)}, f32[96,1536]{1,0:T(8,128)S(1)}, u32[]{:S(2)}, u32[]{:S(2)}) collective-permute-start(f32[96,1536]{1,0:T(8,128)S(1)} %add.171), channel_id=1, source_target_pairs={{8,0},{9,1},{10,2},{11,3},{12,4},{13,5},{14,6},{15,7},{16,24},{17,... | collective-permute-start | bytes 1769480 | tf_op jit(solution)/shard_map/ppermute | solution.py:46
  270.9 32.6 %collective-permute-start.16 = (f32[184,768]{1,0:T(8,128)S(1)}, f32[184,768]{1,0:T(8,128)S(1)}, u32[]{:S(2)}, u32[]{:S(2)}) collective-permute-start(f32[184,768]{1,0:T(8,128)S(1)} %constant_dynamic-slice_fusion), channel_id=1, source_target_pairs={{0,4},{1,5},{2,3},{3,2},{4,0},{5,1},{6,7},{7,6},{8,12},{9,13},{10,... | collective-permute-start | bytes 1695752 | tf_op jit(solution)/shard_map/ppermute | solution.py:46
  272.3 45.2 %collective-permute-start.25 = (f32[96,1152]{1,0:T(8,128)S(1)}, f32[96,1152]{1,0:T(8,128)S(1)}, u32[]{:S(2)}, u32[]{:S(2)}) collective-permute-start(f32[96,1152]{1,0:T(8,128)S(1)} %dynamic-slice_add_fusion.14), channel_id=1, source_target_pairs={{0,8},{1,9},{2,10},{3,11},{4,12},{5,13},{6,14},{7,15},{24,16},{25,... | collective-permute-start | bytes 1327112 | tf_op jit(solution)/shard_map/ppermute | solution.py:46
  276.7 38.7 %collective-permute-start.22 = (f32[96,1152]{1,0:T(8,128)S(1)}, f32[96,1152]{1,0:T(8,128)S(1)}, u32[]{:S(2)}, u32[]{:S(2)}) collective-permute-start(f32[96,1152]{1,0:T(8,128)S(1)} %dynamic-slice_add_fusion.13), channel_id=1, source_target_pairs={{0,8},{1,9},{2,10},{3,11},{4,12},{5,13},{6,14},{7,15},{24,16},{25,... | collective-permute-start | bytes 1327112 | tf_op jit(solution)/shard_map/ppermute | solution.py:46
  278.1 38.2 %collective-permute-start.26 = (f32[96,1536]{1,0:T(8,128)S(1)}, f32[96,1536]{1,0:T(8,128)S(1)}, u32[]{:S(2)}, u32[]{:S(2)}) collective-permute-start(f32[96,1536]{1,0:T(8,128)S(1)} %broadcast_select_fusion.15), channel_id=1, source_target_pairs={{0,4},{1,5},{2,3},{3,2},{4,0},{5,1},{6,7},{7,6},{8,12},{9,13},{10,... | collective-permute-start | bytes 1769480 | tf_op jit(solution)/shard_map/ppermute | solution.py:46
  320.7 28.6 %collective-permute-start.28 = (f32[192,1536]{1,0:T(8,128)}, f32[192,1536]{1,0:T(8,128)}, u32[]{:S(2)}, u32[]{:S(2)}) collective-permute-start(f32[192,1536]{1,0:T(8,128)} %pad_maximum_fusion.5), channel_id=1, source_target_pairs={{0,1},{1,0},{2,6},{3,7},{4,5},{5,4},{6,2},{7,3},{8,9},{9,8},{10,14... | collective-permute-start | bytes 3538952 | tf_op jit(solution)/shard_map/ppermute | solution.py:46
  321.5 23.3 %collective-permute-start.23 = (f32[96,1152]{1,0:T(8,128)}, f32[96,1152]{1,0:T(8,128)}, u32[]{:S(2)}, u32[]{:S(2)}) collective-permute-start(f32[96,1152]{1,0:T(8,128)} %add.178), channel_id=1, source_target_pairs={{8,16},{9,17},{10,18},{11,19},{12,20},{13,21},{14,22},{15,23},{16,... | collective-permute-start | bytes 1327112 | tf_op jit(solution)/shard_map/ppermute | solution.py:46
  323.0 23.0 %collective-permute-start.21 = (f32[184,768]{1,0:T(8,128)}, f32[184,768]{1,0:T(8,128)}, u32[]{:S(2)}, u32[]{:S(2)}) collective-permute-start(f32[184,768]{1,0:T(8,128)} %dynamic-slice_add_fusion.12), channel_id=1, source_target_pairs={{0,8},{1,9},{2,10},{3,11},{4,12},{5,13},{6,14},{7,15},{24,16},{25,... | collective-permute-start | bytes 1695752 | tf_op jit(solution)/shard_map/ppermute | solution.py:46
  336.3 53.0 %collective-permute-start.34 = (f32[384,1536]{1,0:T(8,128)S(1)}, f32[384,1536]{1,0:T(8,128)}, u32[]{:S(2)}, u32[]{:S(2)}) collective-permute-start(f32[384,1536]{1,0:T(8,128)S(1)} %pad_maximum_fusion.1.refs_1_), channel_id=1, source_target_pairs={{0,2},{1,3},{2,0},{3,1},{4,6},{5,7},{6,4},{7,5},{8,10},{9,11},{10,... | collective-permute-start | bytes 7077896 | tf_op jit(solution)/shard_map/ppermute | solution.py:46
  348.6 22.9 %collective-permute-start.27 = (f32[184,768]{1,0:T(8,128)S(1)}, f32[184,768]{1,0:T(8,128)S(1)}, u32[]{:S(2)}, u32[]{:S(2)}) collective-permute-start(f32[184,768]{1,0:T(8,128)S(1)} %add.181), channel_id=1, source_target_pairs={{8,16},{9,17},{10,18},{11,19},{12,20},{13,21},{14,22},{15,23},{16,... | collective-permute-start | bytes 1695752 | tf_op jit(solution)/shard_map/ppermute | solution.py:46
  354.1 53.5 %collective-permute-start.29 = (f32[384,1536]{1,0:T(8,128)S(1)}, f32[384,1536]{1,0:T(8,128)S(1)}, u32[]{:S(2)}, u32[]{:S(2)}) collective-permute-start(f32[384,1536]{1,0:T(8,128)S(1)} %pad_maximum_fusion.refs_0_), channel_id=1, source_target_pairs={{0,2},{1,3},{2,0},{3,1},{4,6},{5,7},{6,4},{7,5},{8,10},{9,11},{10,... | collective-permute-start | bytes 7077896 | tf_op jit(solution)/shard_map/ppermute | solution.py:46
  373.3 31.8 %collective-permute-start.40 = (f32[192,1152]{1,0:T(8,128)S(1)}, f32[192,1152]{1,0:T(8,128)S(1)}, u32[]{:S(2)}, u32[]{:S(2)}) collective-permute-start(f32[192,1152]{1,0:T(8,128)S(1)} %pad_maximum_fusion.8), channel_id=1, source_target_pairs={{0,1},{1,0},{2,6},{3,7},{4,5},{5,4},{6,2},{7,3},{8,9},{9,8},{10,14... | collective-permute-start | bytes 2654216 | tf_op jit(solution)/shard_map/ppermute | solution.py:46
  (44 other events, 443.5 us)
Sparse Core Ops, SparseCore 0:
  47.4 148.8 reduce-scatter.1
  214.3 105.2 all-gather.1
